TPU v7x, 32 devices: a whole 2x2x4 slice. The times are simulated.
32 devices in a mesh: rep: 2 (over y), shard: 16 (over z, x, core).
Axes of the slice: x: 2, y: 2, z: 4, core: 2. Of those that a mesh axis runs over, the one named last changes fastest.
Arguments:
- tokens: bfloat16 [16384, 1024], P(('rep', 'shard')), may hold values from -6 to 6
- cotangent: bfloat16 [16384, 1024], P(('rep', 'shard')), may hold values from -6 to 6
- send_slot: int32 [16384], P(('rep', 'shard')), may hold values from 0 to 1023, as said below
- recv_slot: int32 [16384], P(('rep', 'shard')), may hold values from 0 to 1023, as said below
- lengths: int32 [32, 4], P(('rep', 'shard')), may hold values from 1 to 384, 512 in all within a row
- variate: int32 [16384], P(('rep', 'shard')), may hold values from 0 to 3
- valid_mask: int32 [16384], P(('rep', 'shard')), may hold values from 0 to 1, as said below
- norm_attn: bfloat16 [1024], P('shard'), may hold values from 0.5 to 1.5
- w_query: bfloat16 [1024, 1024], P('shard'), may hold values from -0.1875 to 0.1875
- w_key: bfloat16 [1024, 1024], P('shard'), may hold values from -0.1875 to 0.1875
- w_value: bfloat16 [1024, 1024], P('shard'), may hold values from -0.1875 to 0.1875
- w_out: bfloat16 [1024, 1024], P('shard'), may hold values from -0.75 to 0.75
- variate_bias: float32 [2, 16], replicated, may hold values from -3 to 3
- norm_mlp: bfloat16 [1024], P('shard'), may hold values from 0.5 to 1.5
- w_gate: bfloat16 [1024, 4096], P('shard'), may hold values from -0.1875 to 0.1875
- w_up: bfloat16 [1024, 4096], P('shard'), may hold values from -0.1875 to 0.1875
- w_down: bfloat16 [4096, 1024], P('shard'), may hold values from -0.1875 to 0.1875
Outputs:
- output: bfloat16 [16384, 1024], P(('rep', 'shard'))
- input_grad: bfloat16 [16384, 1024], P(('rep', 'shard'))
- grad_norm_attn: float32 [1024], P('shard')
- grad_query: float32 [1024, 1024], P('shard')
- grad_key: float32 [1024, 1024], P('shard')
- grad_value: float32 [1024, 1024], P('shard')
- grad_out: float32 [1024, 1024], P('shard')
- grad_bias: float32 [2, 16], replicated
- grad_norm_mlp: float32 [1024], P('shard')
- grad_gate: float32 [1024, 4096], P('shard')
- grad_up: float32 [1024, 4096], P('shard')
- grad_down: float32 [4096, 1024], P('shard')
- root_means: float32 [5], replicated
Inputs may be any that keep to these rules, and one draw needn't show every extreme that they name: send_slot[i] = (index in the rep group of the device that gets token i) * 64 + the token's rank among its device's tokens going there. The values on one device are distinct; a device sends to each device of its group a multiple of 16 tokens and at most 64, and some device sends exactly 64 to the last device of its group. recv_slot[t] = (index in the group of the sending device) * 64 + the token's rank there; the values on one device are distinct. With send_slot it describes one permutation of the tokens of each rep group, every device receives exactly 512 tokens, and the last device of some group sends exactly 64 to some device. `valid_mask`: the first row of every device's block is 1.
All inputs are finite; a program needn't handle non-finite values.
Results may differ from a plain program's by a relative error of at most 0.017.
Values may be sent and summed in bfloat16 or wider, within the bound.
A program may use at most 256 MiB of HBM per device.

v0:
```python
import math

import jax
import jax.numpy as jnp
from jax import lax
from jax.sharding import PartitionSpec as P

epsilon = 1e-06
masked_score = -1e30


def rms_parts(stream):
    factor = lax.rsqrt(jnp.mean(stream * stream, axis=-1, keepdims=True) + epsilon)
    return (stream * factor, factor)


def rms_back(grad_normed, normed, factor, gain):
    scaled = grad_normed * gain
    return factor * (scaled - normed * jnp.mean(scaled * normed, axis=-1, keepdims=True))


def angle_tables(position, head_dim):
    half_dim = head_dim // 2
    inverse_freq = 1.0 / 10000.0 ** (jnp.arange(half_dim, dtype=jnp.float32) / half_dim)
    theta_angle = position.astype(jnp.float32)[:, None] * inverse_freq[None, :]
    return (jnp.cos(theta_angle), jnp.sin(theta_angle))


def rotate(values, cosine_table, sine_table, head_count, direction):
    row_count = values.shape[0]
    half_dim = cosine_table.shape[1]
    halves = values.reshape(row_count, head_count, 2, half_dim)
    former = halves[:, :, 0]
    latter = halves[:, :, 1]
    cosine_wide = cosine_table[:, None, :]
    sine_wide = direction * sine_table[:, None, :]
    turned = jnp.stack(
        [former * cosine_wide - latter * sine_wide, latter * cosine_wide + former * sine_wide],
        axis=2,
    )
    return turned.reshape(row_count, head_count * 2 * half_dim)


def layout(lengths_row, tok_rows):
    slot_ids = jnp.arange(tok_rows, dtype=jnp.int32)
    seq_ends = jnp.cumsum(lengths_row)
    segment = jnp.sum((slot_ids[:, None] >= seq_ends[None, :]).astype(jnp.int32), axis=1)
    starts = seq_ends - lengths_row
    chosen = segment[:, None] == jnp.arange(lengths_row.shape[0], dtype=jnp.int32)[None, :]
    begins = jnp.sum(jnp.where(chosen, starts[None, :], 0), axis=1)
    return (segment, slot_ids - begins)


def group_scores(query_part, key_part, same_variate, visible, bias_same, bias_other):
    scores = jnp.einsum("qhd,khd->hqk", query_part, key_part, preferred_element_type=jnp.float32)
    scores = scores + jnp.where(
        same_variate[None], bias_same[:, None, None], bias_other[:, None, None]
    )
    return jnp.where(visible[None], scores, masked_score)


def attention_forward(
    queries, key_rows, value_rows, same_variate, visible, variate_bias, group_size
):
    head_count = variate_bias.shape[1]
    row_count = queries.shape[0]
    head_dim = queries.shape[1] // head_count
    query_heads = queries.reshape(row_count, head_count, head_dim)
    key_heads = key_rows.reshape(row_count, head_count, head_dim)
    value_heads = value_rows.reshape(row_count, head_count, head_dim)
    outputs = []
    log_sums = []
    for head_start in range(0, head_count, group_size):
        picked = slice(head_start, head_start + group_size)
        scores = group_scores(
            query_heads[:, picked],
            key_heads[:, picked],
            same_variate,
            visible,
            variate_bias[0, picked],
            variate_bias[1, picked],
        )
        top_score = jnp.max(scores, axis=-1, keepdims=True)
        exponent_rows = jnp.exp(scores - top_score)
        row_total = jnp.sum(exponent_rows, axis=-1, keepdims=True)
        softmax_rows = (exponent_rows / row_total).astype(jnp.bfloat16)
        outputs.append(
            jnp.einsum(
                "hqk,khd->qhd",
                softmax_rows,
                value_heads[:, picked],
                preferred_element_type=jnp.float32,
            )
        )
        log_sums.append(top_score + jnp.log(row_total))
    return (jnp.concatenate(outputs, axis=1).reshape(row_count, head_count * head_dim), log_sums)


def attention_backward(
    queries,
    key_rows,
    value_rows,
    grad_attended,
    log_sums,
    same_variate,
    visible,
    variate_bias,
    group_size,
):
    head_count = variate_bias.shape[1]
    row_count = queries.shape[0]
    head_dim = queries.shape[1] // head_count
    query_heads = queries.reshape(row_count, head_count, head_dim)
    key_heads = key_rows.reshape(row_count, head_count, head_dim)
    value_heads = value_rows.reshape(row_count, head_count, head_dim)
    grad_heads = grad_attended.reshape(row_count, head_count, head_dim)
    query_grads = []
    key_grads = []
    value_grads = []
    same_grads = []
    other_grads = []
    for group_index, head_start in enumerate(range(0, head_count, group_size)):
        picked = slice(head_start, head_start + group_size)
        query_part = query_heads[:, picked]
        key_part = key_heads[:, picked]
        grad_part = grad_heads[:, picked]
        scores = group_scores(
            query_part,
            key_part,
            same_variate,
            visible,
            variate_bias[0, picked],
            variate_bias[1, picked],
        )
        softmax_rows = jnp.exp(scores - log_sums[group_index])
        grad_soft = jnp.einsum(
            "qhd,khd->hqk", grad_part, value_heads[:, picked], preferred_element_type=jnp.float32
        )
        inner_sum = jnp.sum(softmax_rows * grad_soft, axis=-1, keepdims=True)
        grad_scores = (softmax_rows * (grad_soft - inner_sum)).astype(jnp.bfloat16)
        grad_wide = grad_scores.astype(jnp.float32)
        same_grads.append(jnp.sum(jnp.where(same_variate[None], grad_wide, 0.0), axis=(1, 2)))
        other_grads.append(jnp.sum(jnp.where(same_variate[None], 0.0, grad_wide), axis=(1, 2)))
        query_grads.append(
            jnp.einsum("hqk,khd->qhd", grad_scores, key_part, preferred_element_type=jnp.float32)
        )
        key_grads.append(
            jnp.einsum("hqk,qhd->khd", grad_scores, query_part, preferred_element_type=jnp.float32)
        )
        value_grads.append(
            jnp.einsum(
                "hqk,qhd->khd",
                softmax_rows.astype(jnp.bfloat16),
                grad_part,
                preferred_element_type=jnp.float32,
            )
        )
    width_total = head_count * head_dim
    bias_grad = jnp.stack([jnp.concatenate(same_grads), jnp.concatenate(other_grads)])
    return (
        jnp.concatenate(query_grads, axis=1).reshape(row_count, width_total),
        jnp.concatenate(key_grads, axis=1).reshape(row_count, width_total),
        jnp.concatenate(value_grads, axis=1).reshape(row_count, width_total),
        bias_grad,
    )


def deal_buffer(rows_in, slot_ids, slot_total):
    return jnp.zeros((slot_total, rows_in.shape[1]), rows_in.dtype).at[slot_ids].set(rows_in)


def contract_rows(left, right):
    return lax.dot_general(
        left, right, (((0,), (0,)), ((), ())), preferred_element_type=jnp.float32
    )


def contract_cols(left, right):
    return lax.dot_general(
        left, right, (((1,), (1,)), ((), ())), preferred_element_type=jnp.float32
    )


def on_device(
    tokens,
    cotangent,
    send_slot,
    recv_slot,
    lengths,
    variate,
    valid_mask,
    norm_attn,
    w_query,
    w_key,
    w_value,
    w_out,
    variate_bias,
    norm_mlp,
    w_gate,
    w_up,
    w_down,
):
    shards = lax.axis_size("shard")
    tok_rows, model_width = tokens.shape
    capacity = 2 * tok_rows // shards
    slot_total = shards * capacity
    head_count = variate_bias.shape[1]
    head_dim = model_width // head_count
    hidden_width = w_gate.shape[1]
    group_size = 4
    score_scale = 1.0 / math.sqrt(head_dim)
    outgoing = (
        deal_buffer(tokens, send_slot, slot_total).reshape(shards, capacity, model_width),
        deal_buffer(cotangent, send_slot, slot_total).reshape(shards, capacity, model_width),
    )
    arrived_tokens, arrived_grads = (
        lax.all_to_all(outgoing[0], "shard", split_axis=0, concat_axis=0, tiled=True),
        lax.all_to_all(outgoing[1], "shard", split_axis=0, concat_axis=0, tiled=True),
    )
    stream_rows = jnp.take(arrived_tokens.reshape(slot_total, model_width), recv_slot, axis=0)
    grad_out_rows = jnp.take(arrived_grads.reshape(slot_total, model_width), recv_slot, axis=0)
    segment, position = layout(lengths[0], tok_rows)
    same_variate = variate[:, None] == variate[None, :]
    itself = jnp.arange(tok_rows)[:, None] == jnp.arange(tok_rows)[None, :]
    visible = (segment[:, None] == segment[None, :]) & ((valid_mask[None, :] > 0) | itself)
    cosine_table, sine_table = angle_tables(position, head_dim)
    gathered = (
        lax.all_gather(w_query, "shard", axis=0, tiled=True),
        lax.all_gather(w_key, "shard", axis=0, tiled=True),
        lax.all_gather(w_value, "shard", axis=0, tiled=True),
        lax.all_gather(w_out, "shard", axis=0, tiled=True),
        lax.all_gather(norm_attn, "shard", axis=0, tiled=True),
        lax.all_gather(norm_mlp, "shard", axis=0, tiled=True),
    )
    full_query, full_key, full_value, full_out, gain_bf_attn, gain_bf_mlp = gathered
    gain_attn = gain_bf_attn.astype(jnp.float32)
    gain_mlp = gain_bf_mlp.astype(jnp.float32)
    stream = stream_rows.astype(jnp.float32)
    normed_attn, factor_attn = rms_parts(stream)
    input_attn = (normed_attn * gain_attn).astype(jnp.bfloat16)
    query_proj = jnp.dot(input_attn, full_query, preferred_element_type=jnp.float32)
    key_proj = jnp.dot(input_attn, full_key, preferred_element_type=jnp.float32)
    value_proj = jnp.dot(input_attn, full_value, preferred_element_type=jnp.float32)
    queries = (rotate(query_proj, cosine_table, sine_table, head_count, 1.0) * score_scale).astype(
        jnp.bfloat16
    )
    key_rows = rotate(key_proj, cosine_table, sine_table, head_count, 1.0).astype(jnp.bfloat16)
    value_rows = value_proj.astype(jnp.bfloat16)
    attended, log_sums = attention_forward(
        queries, key_rows, value_rows, same_variate, visible, variate_bias, group_size
    )
    attended_bf = attended.astype(jnp.bfloat16)
    attn_out = jnp.dot(attended_bf, full_out, preferred_element_type=jnp.float32)
    middle = stream + attn_out
    normed_mlp, factor_mlp = rms_parts(middle)
    input_mlp = (normed_mlp * gain_mlp).astype(jnp.bfloat16)
    pieces = (
        lax.all_gather(w_gate, "shard", axis=0, tiled=True),
        lax.all_gather(w_up, "shard", axis=0, tiled=True),
    )
    columns = input_mlp
    gate_proj = jnp.dot(columns, pieces[0], preferred_element_type=jnp.float32)
    up_proj = jnp.dot(columns, pieces[1], preferred_element_type=jnp.float32)
    sigmoid_gate = jax.nn.sigmoid(gate_proj)
    hidden = (gate_proj * sigmoid_gate * up_proj).astype(jnp.bfloat16)
    columns = hidden
    mlp_out = jnp.dot(
        columns,
        lax.all_gather(w_down, "shard", axis=0, tiled=True),
        preferred_element_type=jnp.float32,
    )
    result = middle + mlp_out
    result_bf = result.astype(jnp.bfloat16)
    grad_result = grad_out_rows.astype(jnp.float32)
    grad_hidden = contract_cols(grad_out_rows, lax.all_gather(w_down, "shard", axis=0, tiled=True))
    grad_gate = (
        grad_hidden * up_proj * sigmoid_gate * (1.0 + gate_proj * (1.0 - sigmoid_gate))
    ).astype(jnp.bfloat16)
    grad_up = (grad_hidden * gate_proj * sigmoid_gate).astype(jnp.bfloat16)
    pieces = (
        lax.all_gather(w_gate, "shard", axis=0, tiled=True),
        lax.all_gather(w_up, "shard", axis=0, tiled=True),
    )
    block_cols = contract_cols(grad_gate, pieces[0]) + contract_cols(grad_up, pieces[1])
    grad_gain_mlp = jnp.sum(block_cols * normed_mlp, axis=0)
    grad_middle = grad_result + rms_back(block_cols, normed_mlp, factor_mlp, gain_mlp)
    grad_branch = grad_middle.astype(jnp.bfloat16)
    grad_attended = contract_cols(grad_branch, full_out).astype(jnp.bfloat16)
    grad_queries, grad_keys, grad_values, grad_bias_local = attention_backward(
        queries,
        key_rows,
        value_rows,
        grad_attended,
        log_sums,
        same_variate,
        visible,
        variate_bias,
        group_size,
    )
    grad_query_proj = (
        rotate(grad_queries, cosine_table, sine_table, head_count, -1.0) * score_scale
    ).astype(jnp.bfloat16)
    grad_key_proj = rotate(grad_keys, cosine_table, sine_table, head_count, -1.0).astype(
        jnp.bfloat16
    )
    grad_value_proj = grad_values.astype(jnp.bfloat16)
    grad_input_attn = (
        contract_cols(grad_query_proj, full_query)
        + contract_cols(grad_key_proj, full_key)
        + contract_cols(grad_value_proj, full_value)
    )
    grad_gain_attn = jnp.sum(grad_input_attn * normed_attn, axis=0)
    grad_stream = grad_middle + rms_back(grad_input_attn, normed_attn, factor_attn, gain_attn)
    grad_stream_bf = grad_stream.astype(jnp.bfloat16)
    projection_grads = jnp.concatenate([grad_query_proj, grad_key_proj, grad_value_proj], axis=1)
    mlp_grads = jnp.concatenate([grad_gate, grad_up], axis=1)
    width_share = lax.psum_scatter(
        jnp.concatenate(
            [
                contract_rows(input_attn, projection_grads),
                contract_rows(attended_bf, grad_branch),
                contract_rows(input_mlp, mlp_grads),
            ],
            axis=1,
        ),
        "shard",
        scatter_dimension=0,
        tiled=True,
    )
    hidden_share = lax.psum_scatter(
        contract_rows(hidden, grad_out_rows), "shard", scatter_dimension=0, tiled=True
    )
    width_share, hidden_share = (
        lax.psum(width_share.astype(jnp.bfloat16), "rep").astype(jnp.float32),
        lax.psum(hidden_share.astype(jnp.bfloat16), "rep").astype(jnp.float32),
    )
    weight_rows = (valid_mask > 0).astype(jnp.float32)[:, None]
    square_sums = jnp.stack(
        [
            jnp.sum(weight_rows * stream * stream),
            jnp.sum(weight_rows * attn_out * attn_out),
            jnp.sum(weight_rows * middle * middle),
            jnp.sum(weight_rows * mlp_out * mlp_out),
            jnp.sum(weight_rows * result * result),
            jnp.sum(weight_rows),
        ]
    )
    gain_grads = jnp.stack([grad_gain_attn, grad_gain_mlp])
    total_sums, bias_grads, gain_totals = lax.psum(
        (square_sums, grad_bias_local, gain_grads), ("rep", "shard")
    )
    root_means = jnp.sqrt(total_sums[:5] / (total_sums[5] * model_width))
    share_rows = model_width // shards
    share_start = lax.axis_index("shard") * share_rows
    grad_norm_attn = lax.dynamic_slice_in_dim(gain_totals[0], share_start, share_rows)
    grad_norm_mlp = lax.dynamic_slice_in_dim(gain_totals[1], share_start, share_rows)
    homeward = (
        deal_buffer(result_bf, recv_slot, slot_total).reshape(shards, capacity, model_width),
        deal_buffer(grad_stream_bf, recv_slot, slot_total).reshape(shards, capacity, model_width),
    )
    home_out, home_grad = (
        lax.all_to_all(homeward[0], "shard", split_axis=0, concat_axis=0, tiled=True),
        lax.all_to_all(homeward[1], "shard", split_axis=0, concat_axis=0, tiled=True),
    )
    output = jnp.take(home_out.reshape(slot_total, model_width), send_slot, axis=0)
    input_grad = jnp.take(home_grad.reshape(slot_total, model_width), send_slot, axis=0)
    grad_query = width_share[:, 0:model_width]
    grad_key = width_share[:, model_width : 2 * model_width]
    grad_value = width_share[:, 2 * model_width : 3 * model_width]
    grad_out = width_share[:, 3 * model_width : 4 * model_width]
    grad_gate_w = width_share[:, 4 * model_width : 4 * model_width + hidden_width]
    grad_up_w = width_share[:, 4 * model_width + hidden_width :]
    return (
        output,
        input_grad,
        grad_norm_attn,
        grad_query,
        grad_key,
        grad_value,
        grad_out,
        bias_grads,
        grad_norm_mlp,
        grad_gate_w,
        grad_up_w,
        hidden_share,
        root_means,
    )


def solution(mesh):
    in_specs = (
        P(("rep", "shard"), None),
        P(("rep", "shard"), None),
        P(("rep", "shard")),
        P(("rep", "shard")),
        P(("rep", "shard"), None),
        P(("rep", "shard")),
        P(("rep", "shard")),
        P("shard"),
        P("shard", None),
        P("shard", None),
        P("shard", None),
        P("shard", None),
        P(),
        P("shard"),
        P("shard", None),
        P("shard", None),
        P("shard", None),
    )
    out_specs = (
        P(("rep", "shard"), None),
        P(("rep", "shard"), None),
        P("shard"),
        P("shard", None),
        P("shard", None),
        P("shard", None),
        P("shard", None),
        P(),
        P("shard"),
        P("shard", None),
        P("shard", None),
        P("shard", None),
        P(),
    )
    return jax.shard_map(
        on_device, mesh=mesh, in_specs=in_specs, out_specs=out_specs, check_vma=False
    )
```

profile of v0, /device:TPU:8, one launch (start us, length us, event | category | flops | bytes accessed | tf_op | source)
XLA Modules:
  0.0 1228.1 jit_solution(9492257428788047338)
XLA Ops:
  28.6 51.2 %all-to-all-done.2 = bf16[16,64,1024]{2,1,0:T(8,128)(2,1)S(1)} async-done(((bf16[16,64,1024]{2,1,0:T(8,128)(2,1)}), bf16[16,64,1024]{2,1,0:T(8,128)(2,1)S(1)}, u32[]{:S(2)}, u32[]{:S(2)}) %all-to-all-start.2) | async-done | bytes 2097184 | tf_op jit(solution)/shard_map/all_to_all | solution.py:218
  79.8 6.7 all-to-all-start
  88.3 72.9 %all-reduce.3 = (bf16[1024]{0:T(1024)(128)(2,1)S(1)}, bf16[1024]{0:T(1024)(128)(2,1)S(1)}) all-reduce(bf16[1024]{0:T(1024)(128)(2,1)S(1)} %dynamic-update-slice, bf16[1024]{0:T(1024)(128)(2,1)S(1)} %dynamic-update-slice.1), channel_id=1, replica_groups=mesh['rep'=2,'shard'=16] {'shard'}, use_global_device_ids=true, to_apply=%add | all-reduce | flops 2048 | bytes 8192
  200.0 24.5 %all-gather.14.cloned.1.call-done = bf16[1024,1024]{1,0:T(8,128)(2,1)} async-done(((bf16[64,1024]{1,0:T(8,128)(2,1)}), bf16[1024,1024]{1,0:T(8,128)(2,1)}) %all-gather.14.cloned.1.call-update) | async-done | bytes 2097168 | tf_op jit(solution)/shard_map/all_gather | solution.py:231
  230.5 70.0 %all-gather.18.cloned.1.call-done = bf16[1024,4096]{1,0:T(8,128)(2,1)} async-done(((bf16[64,4096]{1,0:T(8,128)(2,1)}), bf16[1024,4096]{1,0:T(8,128)(2,1)}) %all-gather.18.cloned.1.call-update) | async-done | bytes 8388624 | tf_op jit(solution)/shard_map/all_gather | solution.py:259
  300.5 11.4 fusion.143
  311.9 63.8 %all-gather.16.cloned.1.call-done = bf16[1024,4096]{1,0:T(8,128)(2,1)} async-done(((bf16[64,4096]{1,0:T(8,128)(2,1)}), bf16[1024,4096]{1,0:T(8,128)(2,1)}) %all-gather.16.cloned.1.call-update) | async-done | bytes 8388624 | tf_op jit(solution)/shard_map/all_gather | solution.py:258
  375.7 11.4 fusion.142
  387.2 63.9 %all-gather.20.cloned.1.call-done = bf16[4096,1024]{1,0:T(8,128)(2,1)} async-done(((bf16[256,1024]{1,0:T(8,128)(2,1)}), bf16[4096,1024]{1,0:T(8,128)(2,1)}) %all-gather.20.cloned.1.call-update) | async-done | bytes 8388624 | tf_op jit(solution)/shard_map/all_gather | solution.py:269
  451.1 16.5 %multiply_convert_fusion = (bf16[512,4096]{1,0:T(8,128)(2,1)}, bf16[512,4096]{1,0:T(8,128)(2,1)}, bf16[512,4096]{1,0:T(8,128)(2,1)}) fusion(f32[512,4096]{1,0:T(8,128)} %fusion.142, f32[512,4096]{1,0:T(8,128)} %fusion.143, bf16[4096,1024]{1,0:T(8,128)(2,1)} %all-gather.20.cloned.1.call-done, bf16[512,1024]{1,0:T(8,128)(2,1)} %gather_fusion.2, ...), kind=kOutput, calls=%fused_computation.13 | convolution fusion | flops 4329046016 | bytes 38797824 | tf_op jit(solution)/shard_map/dot_general | solution.py:179
  467.5 12.9 %fusion.127 = f32[4096,1024]{1,0:T(8,128)} fusion(bf16[512,4096]{1,0:T(8,128)(2,1)} %get-tuple-element.56, bf16[512,1024]{1,0:T(8,128)(2,1)} %gather_fusion.2, pred[512]{0:T(512)(128)(4,1)S(1)} %compare_and_fusion.1), kind=kOutput, calls=%fused_computation.240 | convolution fusion | flops 4295491584 | bytes 22020608 | tf_op jit(solution)/shard_map/dot_general | solution.py:173
  481.2 8.6 fusion.144
  489.8 7.9 convolution_add_fusion
  497.8 10.5 fusion.33
  529.5 14.5 %fusion.4 = (f32[4]{0:T(128)S(1)}, f32[4]{0:T(128)S(1)}, f32[4]{0:T(128)S(1)}, f32[4]{0:T(128)S(1)}, f32[4]{0:T(128)S(1)}, /*index=5*/f32[4]{0:T(128)S(1)}, f32[...) fusion(pred[512,512]{0,1:T(8,128)(4,1)S(1)} %get-tuple-element., ...), kind=kLoop, calls=%fused_computation.25 | loop fusion | flops 37748704 | bytes 42270848 | tf_op jit(solution)/shard_map/reduce_sum | solution.py:142
  564.7 9.7 fusion.24
  574.4 19.3 %fusion = f32[1024,8192]{1,0:T(8,128)} fusion(bf16[512,1024]{1,0:T(8,128)(2,1)S(1)} %copy-done.20, bf16[512,4096]{1,0:T(8,128)(2,1)} %get-tuple-element.54, bf16[512,4096]{1,0:T(8,128)(2,1)} %get-tuple-element.55), kind=kOutput, calls=%fused_computation.9 | convolution fusion | flops 8606711808 | bytes 42991616 | tf_op jit(solution)/shard_map/dot_general | solution.py:173
  593.6 34.0 %pad_maximum_fusion = f32[1024,12288]{1,0:T(8,128)} fusion(f32[1024,8192]{1,0:T(8,128)} %fusion, f32[1024,1024]{1,0:T(8,128)} %fusion.109, f32[1024,3072]{1,0:T(8,128)} %fusion.24), kind=kLoop, calls=%fused_computation.8 | loop fusion | flops 25165824 | bytes 100663296 | tf_op jit(solution)/shard_map/concatenate | solution.py:318
  649.3 6.3 scatter_custom_fusion.3
  655.7 43.1 %all-to-all-done.1 = bf16[16,64,1024]{2,1,0:T(8,128)(2,1)S(1)} async-done(((bf16[16,64,1024]{2,1,0:T(8,128)(2,1)}), bf16[16,64,1024]{2,1,0:T(8,128)(2,1)S(1)}, u32[]{:S(2)}, u32[]{:S(2)}) %all-to-all-start.1) | async-done | bytes 2097184 | tf_op jit(solution)/shard_map/all_to_all | solution.py:362
  698.8 6.9 all-to-all-start.3
  708.0 439.3 %reduce-scatter.3.cloned.1.call-done = f32[64,12288]{1,0:T(8,128)} async-done(((f32[1024,12288]{1,0:T(8,128)}), f32[64,12288]{1,0:T(8,128)}) %reduce-scatter.3.cloned.1.call-update) | async-done | bytes 3145744 | tf_op jit(solution)/shard_map/reduce_scatter | solution.py:317
  1154.7 41.4 %all-reduce.2 = (f32[2,1024]{1,0:T(2,128)S(1)}, f32[2,16]{1,0:T(2,128)}, f32[6]{0:T(128)S(1)}) all-reduce(f32[2,1024]{1,0:T(2,128)S(1)} %pad_maximum_fusion.7, f32[2,16]{1,0:T(2,128)S(1)} %pad_maximum_fusion.8, f32[6]{0:T(128)S(1)} %stack.77), channel_id=1, replica_groups=mesh['rep'=2,'shard'=16] {'rep','shard'}, use_global_device_ids=true, to_apply=%region_25.27 | all-reduce | flops 2086 | bytes 16688 | tf_op jit(solution)/shard_map/psum | solution.py:349
  1207.3 8.7 all-reduce.7.cloned.1.call-done
  (280 shorter events, 156.0 us)
Async XLA Ops:
  7.2 166.2 %all-gather.8.cloned.1.call-start = ((), (), s32[]{:S(2)}) async-start(), calls=%async_computation.6 | async-start | bytes 2228224 | tf_op jit(solution)/shard_map/all_gather | solution.py:230
  7.9 169.0 %all-gather.12.cloned.1.call-start = ((), (), s32[]{:S(2)}) async-start(), calls=%async_computation.8 | async-start | bytes 2228224 | tf_op jit(solution)/shard_map/all_gather | solution.py:229
  8.7 173.6 %all-gather.10.cloned.1.call-start = ((), (), s32[]{:S(2)}) async-start(), calls=%async_computation.7 | async-start | bytes 2228224 | tf_op jit(solution)/shard_map/all_gather | solution.py:228
  9.4 215.0 %all-gather.14.cloned.1.call-start = ((), (), s32[]{:S(2)}) async-start(), calls=%async_computation.9 | async-start | bytes 2228224 | tf_op jit(solution)/shard_map/all_gather | solution.py:231
  10.0 290.5 %all-gather.18.cloned.1.call-start = ((), (), s32[]{:S(2)}) async-start(), calls=%async_computation.11 | async-start | bytes 8912896 | tf_op jit(solution)/shard_map/all_gather | solution.py:259
  10.6 365.2 %all-gather.16.cloned.1.call-start = ((), (), s32[]{:S(2)}) async-start(), calls=%async_computation.10 | async-start | bytes 8912896 | tf_op jit(solution)/shard_map/all_gather | solution.py:258
  16.7 63.2 %all-to-all-start.2 = ((bf16[16,64,1024]{2,1,0:T(8,128)(2,1)}), bf16[16,64,1024]{2,1,0:T(8,128)(2,1)S(1)}, u32[]{:S(2)}, u32[]{:S(2)}) async-start(bf16[16,64,1024]{2,1,0:T(8,128)(2,1)} %bitcast.171), calls=%async_computation.2 | async-start | bytes 4194304 | tf_op jit(solution)/shard_map/all_to_all | solution.py:218
  22.9 428.1 %all-gather.20.cloned.1.call-start = ((), (), s32[]{:S(2)}) async-start(), calls=%async_computation.12 | async-start | bytes 8912896 | tf_op jit(solution)/shard_map/all_gather | solution.py:269
  23.7 64.1 %copy-start.65 = (bf16[64]{0:T(256)(128)(2,1)S(1)}, bf16[64]{0:T(256)(128)(2,1)}, u32[]{:S(2)}) copy-start(bf16[64]{0:T(256)(128)(2,1)} %param.26) | copy-start | bytes 388
  23.7 64.4 %copy-start.66 = (bf16[64]{0:T(256)(128)(2,1)S(1)}, bf16[64]{0:T(256)(128)(2,1)}, u32[]{:S(2)}) copy-start(bf16[64]{0:T(256)(128)(2,1)} %param.32) | copy-start | bytes 388
  23.7 137.5 %copy-start.67 = (s32[1,4]{1,0:T(1,128)S(1)}, s32[1,4]{1,0:T(1,128)}, u32[]{:S(2)}) copy-start(s32[1,4]{1,0:T(1,128)} %param.23) | copy-start | bytes 52
  23.7 137.7 %copy-start.49 = (s32[512]{0:T(512)S(1)}, s32[512]{0:T(512)}, u32[]{:S(2)}) copy-start(s32[512]{0:T(512)} %param.22) | copy-start | bytes 6148
  23.8 138.4 %copy-start.53 = (s32[512]{0:T(512)S(1)}, s32[512]{0:T(512)}, u32[]{:S(2)}) copy-start(s32[512]{0:T(512)} %param.25) | copy-start | bytes 6148
  23.8 139.1 %copy-start.42 = (f32[2,16]{1,0:T(2,128)S(1)}, f32[2,16]{1,0:T(2,128)}, u32[]{:S(2)}) copy-start(f32[2,16]{1,0:T(2,128)} %param.31) | copy-start | bytes 388
  23.8 140.7 %copy-start.43 = (s32[512]{0:T(512)S(1)}, s32[512]{0:T(512)}, u32[]{:S(2)}) copy-start(s32[512]{0:T(512)} %param.24) | copy-start | bytes 6148
  79.8 88.4 %all-to-all-start = ((bf16[16,64,1024]{2,1,0:T(8,128)(2,1)}), bf16[16,64,1024]{2,1,0:T(8,128)(2,1)}, u32[]{:S(2)}, u32[]{:S(2)}) async-start(bf16[16,64,1024]{2,1,0:T(8,128)(2,1)} %bitcast.170), calls=%async_computation | async-start | bytes 4194304 | tf_op jit(solution)/shard_map/all_to_all | solution.py:217
  86.5 619.2 %reduce-scatter.5.cloned.1.call-start = ((), (), s32[]{:S(2)}) async-start(), calls=%async_computation.14 | async-start | bytes 17825792 | tf_op jit(solution)/shard_map/reduce_scatter | solution.py:330
  229.1 279.2 %copy-start.12 = (f32[512,1024]{1,0:T(8,128)}, f32[512,1024]{1,0:T(8,128)S(1)}, u32[]{:S(2)}) copy-start(f32[512,1024]{1,0:T(8,128)S(1)} %get-tuple-element.53) | copy-start | bytes 6291460
  480.5 666.8 %reduce-scatter.3.cloned.1.call-start = ((), (), s32[]{:S(2)}) async-start(), calls=%async_computation.13 | async-start | bytes 53477376 | tf_op jit(solution)/shard_map/reduce_scatter | solution.py:317
  634.4 64.4 %all-to-all-start.1 = ((bf16[16,64,1024]{2,1,0:T(8,128)(2,1)}), bf16[16,64,1024]{2,1,0:T(8,128)(2,1)S(1)}, u32[]{:S(2)}, u32[]{:S(2)}) async-start(bf16[16,64,1024]{2,1,0:T(8,128)(2,1)} %bitcast.167), calls=%async_computation.1 | async-start | bytes 4194304 | tf_op jit(solution)/shard_map/all_to_all | solution.py:362
  698.8 502.3 %all-to-all-start.3 = ((bf16[16,64,1024]{2,1,0:T(8,128)(2,1)}), bf16[16,64,1024]{2,1,0:T(8,128)(2,1)}, u32[]{:S(2)}, u32[]{:S(2)}) async-start(bf16[16,64,1024]{2,1,0:T(8,128)(2,1)} %bitcast.166), calls=%async_computation.3 | async-start | bytes 4194304 | tf_op jit(solution)/shard_map/all_to_all | solution.py:363
  705.7 510.3 %all-reduce.7.cloned.1.call-start = ((), (), s32[]{:S(2)}) async-start(), calls=%async_computation.15 | async-start | bytes 4194304 | tf_op jit(solution)/shard_map/psum | solution.py:334
  708.0 442.5 %copy-start.47 = (s32[512]{0:T(512)S(1)}, s32[512]{0:T(512)}, u32[]{:S(2)}) copy-start(s32[512]{0:T(512)} %copy-done.46) | copy-start | bytes 6148
  708.0 442.6 %copy-start.50 = (s32[512]{0:T(512)S(1)}, s32[512]{0:T(512)}, u32[]{:S(2)}) copy-start(s32[512]{0:T(512)} %param.21) | copy-start | bytes 6148
  (62 other events, 355.6 us)
Sparse Core Ops, SparseCore 0:
  10.2 66.1 all-gather.7
  78.5 62.0 all-gather.11
  142.8 39.4 all-gather.9
  184.2 40.1 all-gather.13
  226.4 74.0 all-gather.17
  302.5 73.1 all-gather.15
  377.9 73.1 all-gather.19
  480.6 192.5 reduce-scatter.4
  677.4 469.8 reduce-scatter.2
  1150.6 65.2 all-reduce.6
where the time goes:
time: 1240 us; the launch traced here: 1230 us
  waiting for transfers between devices  769 us (62%)
  matrix products  172 us (14%)
  blocking collectives  114 us (9%)
  other arithmetic  81.7 us (7%)
  local copies, waits for them, and re-layouts  48.4 us (4%)
  starting transfers between devices  25.7 us (2%)
  between operations  16.9 us (1%)
    reduce_scatter x1, waiting for transfers between devices, on_device(): lax.psum_scatter(jnp.concatenate([contract_rows(input_attn, projection_gr...  439 us
    unnamed x1, blocking collectives  72.9 us
    all_gather x1, waiting for transfers between devices, on_device(): lax.all_gather(w_up, 'shard', axis=0, tiled=True)  70 us
    all_gather x1, waiting for transfers between devices, on_device(): lax.all_gather(w_down, 'shard', axis=0, tiled=True)  63.9 us
    all_gather x1, waiting for transfers between devices, on_device(): lax.all_gather(w_gate, 'shard', axis=0, tiled=True)  63.8 us
    all_to_all x1, waiting for transfers between devices, on_device(): lax.all_to_all(outgoing[1], 'shard', split_axis=0, concat_axis=0, tiled=T...  51.2 us
    dot_general x4, matrix products, contract_rows(): lax.dot_general(left, right, (((0,), (0,)), ((), ())), preferred_element_...  45.2 us
    dot_general x7, matrix products, contract_cols(): lax.dot_general(left, right, (((1,), (1,)), ((), ())), preferred_element_...  44 us
  transfers between devices with their start and end apart: 14, of which 9 were waited for; matrix products, arithmetic and copies ran while one was open for 21% of the time, Pallas kernels for 0%

commit v1 on v0

--- a/solution.py
+++ b/solution.py
@@ -1,9 +1,15 @@
+import functools
 import math
 
 import jax
 import jax.numpy as jnp
 from jax import lax
+from jax.experimental import pallas as pl
+from jax.experimental.pallas import tpu as pltpu
 from jax.sharding import PartitionSpec as P
+
+MESH = pl.DeviceIdType.MESH
+DMA = pltpu.SemaphoreType.DMA
 
 epsilon = 1e-06
 masked_score = -1e30
@@ -181,6 +187,626 @@
     )
 
 
+def ring_place(chip, chips):
+    return jnp.where(chip % 2 == 0, chip // 2, chips - 1 - chip // 2)
+
+
+def ring_chip(place, chips):
+    wrapped = lax.rem(place + 2 * chips, chips)
+    return jnp.where(wrapped < chips // 2, 2 * wrapped, 2 * (chips - 1 - wrapped) + 1)
+
+
+class Spot:
+    def __init__(self, shards):
+        self.shards = shards
+        self.chips = shards // 2
+        self.hops = self.chips - 1
+        self.rep = lax.axis_index("rep")
+        self.shard = lax.axis_index("shard")
+        self.core = lax.rem(self.shard, 2)
+        self.place = ring_place(self.shard // 2, self.chips)
+        self.sibling = self.shard + 1 - 2 * self.core
+
+    def block(self, place, core=None):
+        return 2 * ring_chip(place, self.chips) + (self.core if core is None else core)
+
+    def along(self, way, distance):
+        return self.place - distance if way == 0 else self.place + distance
+
+    def ahead(self, way):
+        return (self.rep, self.block(self.along(way, -1)))
+
+
+def greet(spot, everyone=False):
+    barrier = pltpu.get_barrier_semaphore()
+    shards = spot.shards
+
+    def peer(k, carry):
+        target = lax.rem(spot.shard + k, shards)
+        pl.semaphore_signal(barrier, inc=1, device_id=(spot.rep, target), device_id_type=MESH)
+        return carry
+
+    lax.fori_loop(1, shards, peer, 0)
+    if not everyone:
+        pl.semaphore_signal(
+            barrier, inc=1, device_id=(1 - spot.rep, spot.shard), device_id_type=MESH
+        )
+        pl.semaphore_wait(barrier, shards)
+        return
+
+    def other(k, carry):
+        pl.semaphore_signal(barrier, inc=1, device_id=(1 - spot.rep, k), device_id_type=MESH)
+        return carry
+
+    lax.fori_loop(0, shards, other, 0)
+    pl.semaphore_wait(barrier, 2 * shards - 1)
+
+
+def remote(src, dst, sems, at, target):
+    return pltpu.make_async_remote_copy(
+        src_ref=src,
+        dst_ref=dst,
+        send_sem=sems[0].at[at],
+        recv_sem=sems[1].at[at],
+        device_id=target,
+        device_id_type=MESH,
+    )
+
+
+class Swap:
+    def __init__(self, spot, source, arrived, sems, own_sem):
+        self.spot, self.sems = spot, sems
+        self.source, self.arrived = source, arrived
+        self.capacity = source.shape[0] // spot.shards
+        mine = pl.ds(spot.shard * self.capacity, self.capacity)
+        self.own = pltpu.make_async_copy(source.at[mine], arrived.at[mine], own_sem)
+
+    def copy(self, k):
+        spot = self.spot
+        target = lax.rem(spot.shard + k, spot.shards)
+        return remote(
+            self.source.at[pl.ds(target * self.capacity, self.capacity)],
+            self.arrived.at[pl.ds(spot.shard * self.capacity, self.capacity)],
+            self.sems,
+            (k,),
+            (spot.rep, target),
+        )
+
+    def start(self):
+        def one(k, carry):
+            self.copy(k).start()
+            return carry
+
+        lax.fori_loop(1, self.spot.shards, one, 0)
+        self.own.start()
+
+    def finish(self):
+        def one(k, carry):
+            self.copy(k).wait()
+            return carry
+
+        lax.fori_loop(1, self.spot.shards, one, 0)
+        self.own.wait()
+
+
+class Gather:
+    def __init__(self, spot, shard_ref, full_ref, sems):
+        self.spot, self.shard_ref, self.full_ref = spot, shard_ref, full_ref
+        self.rows = shard_ref.shape[0]
+        self.unit = shard_ref.shape[1] // 8
+        self.ring_sems, self.near_sems, self.far_sems, self.far_near_sems = (
+            sems[0:2],
+            sems[2:4],
+            sems[4:6],
+            sems[6:8],
+        )
+        self.whole_sems, self.own_sem = sems[8:10], sems[10]
+
+    def cut(self, block, first, count):
+        columns = pl.ds(pl.multiple_of(first * self.unit, 128), count * self.unit)
+        return self.full_ref.at[pl.ds(block * self.rows, self.rows), columns]
+
+    def ring(self, way, hop, source=None):
+        spot = self.spot
+        region = self.cut(spot.block(spot.along(way, hop)), 2 * spot.rep + 3 * way, 3)
+        return remote(
+            region if source is None else source,
+            region,
+            self.ring_sems,
+            (way, hop),
+            spot.ahead(way),
+        )
+
+    def near(self, way, hop):
+        spot = self.spot
+        region = self.cut(spot.block(spot.along(way, hop + 1)), 2 * spot.rep + 3 * way, 3)
+        return remote(region, region, self.near_sems, (way, hop), (spot.rep, spot.sibling))
+
+    def far(self, hop):
+        spot = self.spot
+        turn = (1 - 2 * spot.rep) * (hop + 1)
+        region = self.cut(spot.block(spot.place - turn), 6 * spot.rep, 2)
+        return remote(region, region, self.far_sems, (hop,), (1 - spot.rep, spot.shard))
+
+    def far_near(self, hop):
+        spot = self.spot
+        turn = (1 - 2 * spot.rep) * (hop + 1)
+        region = self.cut(spot.block(spot.place + turn), 6 * (1 - spot.rep), 2)
+        return remote(region, region, self.far_near_sems, (hop,), (spot.rep, spot.sibling))
+
+    def own(self):
+        spot = self.spot
+        mine = self.full_ref.at[pl.ds(spot.shard * self.rows, self.rows)]
+        whole = remote(self.shard_ref, mine, self.whole_sems, (0,), (spot.rep, spot.sibling))
+        return whole, pltpu.make_async_copy(self.shard_ref, mine, self.own_sem)
+
+    def start(self):
+        for way in (0, 1):
+            first = 2 * self.spot.rep + 3 * way
+            columns = pl.ds(pl.multiple_of(first * self.unit, 128), 3 * self.unit)
+            self.ring(way, 0, self.shard_ref.at[:, columns]).start()
+        for copy in self.own():
+            copy.start()
+
+    def step(self, hop, last=False):
+        for way in (0, 1):
+            self.ring(way, hop).wait_recv()
+            if not last:
+                self.ring(way, hop + 1).start()
+            self.near(way, hop).start()
+        self.far(hop).start()
+
+    def relay(self, hop):
+        self.far(hop).wait_recv()
+        self.far_near(hop).start()
+
+    def finish(self):
+        for copy in self.own():
+            copy.wait()
+
+        def one(hop, carry):
+            for way in (0, 1):
+                self.ring(way, hop).wait_send()
+                self.near(way, hop).wait()
+            self.far(hop).wait_send()
+            self.far_near(hop).wait()
+            return carry
+
+        lax.fori_loop(0, self.spot.hops, one, 0)
+
+    @staticmethod
+    def scratch(hops):
+        pairs = [DMA((2, hops))] * 4 + [DMA((hops,))] * 4 + [DMA((1,))] * 2
+        return pairs + [DMA]
+
+
+def run_gathers(gathers, hops):
+    for gather in gathers:
+        gather.start()
+
+    def one(hop, carry):
+        for gather in gathers:
+            gather.step(hop)
+
+            @pl.when(hop > 0)
+            def _():
+                gather.relay(hop - 1)
+
+        return carry
+
+    lax.fori_loop(0, hops - 1, one, 0)
+    for gather in gathers:
+        gather.step(hops - 1, last=True)
+        gather.relay(hops - 2)
+    for gather in gathers:
+        gather.relay(hops - 1)
+        gather.finish()
+
+
+def gather_kernel(shards, group_count, swap_count, *refs):
+    spot = Spot(shards)
+    inputs, rest = refs[: group_count + swap_count], refs[group_count + swap_count :]
+    outputs, scratch = rest[: group_count + swap_count], rest[group_count + swap_count :]
+    greet(spot)
+    gathers = [
+        Gather(spot, inputs[g], outputs[g], scratch[11 * g : 11 * g + 11])
+        for g in range(group_count)
+    ]
+    scratch = scratch[11 * group_count :]
+    swaps = [
+        Swap(
+            spot,
+            inputs[group_count + i],
+            outputs[group_count + i],
+            scratch[3 * i : 3 * i + 2],
+            scratch[3 * i + 2],
+        )
+        for i in range(swap_count)
+    ]
+    for swap in swaps:
+        swap.start()
+    run_gathers(gathers, spot.hops)
+    for swap in swaps:
+        swap.finish()
+
+
+def gather_call(shards, pieces, sent, collective_id):
+    hops = shards // 2 - 1
+    scratch = Gather.scratch(hops) * len(pieces)
+    scratch += [DMA((shards,)), DMA((shards,)), DMA] * len(sent)
+    anywhere = pl.BlockSpec(memory_space=pl.ANY)
+    results = pl.pallas_call(
+        functools.partial(gather_kernel, shards, len(pieces), len(sent)),
+        out_shape=[
+            jax.ShapeDtypeStruct((shards * piece.shape[0], piece.shape[1]), piece.dtype)
+            for piece in pieces
+        ]
+        + [jax.ShapeDtypeStruct(rows.shape, rows.dtype) for rows in sent],
+        in_specs=[anywhere] * (len(pieces) + len(sent)),
+        out_specs=[anywhere] * (len(pieces) + len(sent)),
+        scratch_shapes=scratch,
+        compiler_params=pltpu.CompilerParams(
+            collective_id=collective_id, has_side_effects=True
+        ),
+    )(*pieces, *sent)
+    return results[: len(pieces)], results[len(pieces) :]
+
+
+class Reduce:
+    def __init__(self, spot, partial_ref, out_ref, refs):
+        self.spot, self.partial, self.out = spot, partial_ref, out_ref
+        self.rows, self.columns = out_ref.shape
+        self.unit = self.columns // 8
+        (
+            self.own_ring,
+            self.sib_ring,
+            self.got_ring,
+            self.own_far,
+            self.sib_far,
+            self.got_far,
+            self.got_last,
+        ) = refs[:7]
+        sems = refs[7:]
+        self.load_ring_sem, self.load_far_sem = sems[0], sems[1]
+        self.sib_ring_sems, self.sib_far_sems = sems[2:4], sems[4:6]
+        self.ring_sems, self.far_sems, self.last_sems = sems[6:8], sems[8:10], sems[10:12]
+
+    @staticmethod
+    def scratch(shards, rows, columns):
+        chips = shards // 2
+        unit = columns // 8
+        half = jnp.bfloat16
+        buffers = [
+            pltpu.VMEM((2, chips, rows, 3 * unit), half),
+            pltpu.VMEM((2, chips, rows, 3 * unit), half),
+            pltpu.VMEM((2, chips - 1, rows, 3 * unit), half),
+            pltpu.VMEM((chips, rows, 2 * unit), half),
+            pltpu.VMEM((chips, rows, 2 * unit), half),
+            pltpu.VMEM((chips, rows, 2 * unit), half),
+            pltpu.VMEM((2, rows, 3 * unit), half),
+        ]
+        sems = [DMA((2, chips)), DMA((chips,))]
+        sems += [DMA((2, chips))] * 2 + [DMA((chips,))] * 2
+        sems += [DMA((2, chips))] * 2 + [DMA((chips,))] * 2 + [DMA((2,))] * 2
+        return buffers + sems
+
+    def cut(self, block, first, count):
+        columns = pl.ds(pl.multiple_of(first * self.unit, 128), count * self.unit)
+        return self.partial.at[pl.ds(block * self.rows, self.rows), columns]
+
+    def ring_cut(self, way, step, core):
+        spot = self.spot
+        return self.cut(
+            spot.block(spot.along(way, step + 1), core), 2 * spot.rep + 3 * way, 3
+        )
+
+    def far_cut(self, step, core):
+        spot = self.spot
+        place = spot.place + (1 - 2 * spot.rep) * (step + 1)
+        return self.cut(spot.block(place, core), 6 * (1 - spot.rep), 2)
+
+    def load_ring(self, way, step):
+        return pltpu.make_async_copy(
+            self.ring_cut(way, step, self.spot.core),
+            self.own_ring.at[way, step],
+            self.load_ring_sem.at[way, step],
+        )
+
+    def load_far(self, step):
+        return pltpu.make_async_copy(
+            self.far_cut(step, self.spot.core), self.own_far.at[step], self.load_far_sem.at[step]
+        )
+
+    def give_ring(self, way, step):
+        spot = self.spot
+        return remote(
+            self.ring_cut(way, step, 1 - spot.core),
+            self.sib_ring.at[way, step],
+            self.sib_ring_sems,
+            (way, step),
+            (spot.rep, spot.sibling),
+        )
+
+    def give_far(self, step):
+        spot = self.spot
+        return remote(
+            self.far_cut(step, 1 - spot.core),
+            self.sib_far.at[step],
+            self.sib_far_sems,
+            (step,),
+            (spot.rep, spot.sibling),
+        )
+
+    def ring(self, way, step):
+        return remote(
+            self.own_ring.at[way, step],
+            self.got_ring.at[way, step],
+            self.ring_sems,
+            (way, step),
+            self.spot.ahead(way),
+        )
+
+    def far(self, step):
+        spot = self.spot
+        return remote(
+            self.own_far.at[step],
+            self.got_far.at[step],
+            self.far_sems,
+            (step,),
+            (1 - spot.rep, spot.shard),
+        )
+
+    def last(self, way):
+        spot = self.spot
+        return remote(
+            self.own_ring.at[way, spot.hops],
+            self.got_last.at[way],
+            self.last_sems,
+            (way,),
+            (1 - spot.rep, spot.shard),
+        )
+
+    def start(self):
+        def one(step, carry):
+            self.load_far(step).start()
+            self.give_far(step).start()
+            for way in (0, 1):
+                self.load_ring(way, step).start()
+                self.give_ring(way, step).start()
+            return carry
+
+        lax.fori_loop(0, self.spot.chips, one, 0)
+
+    def tiles(self, body):
+        def one(tile, carry):
+            body(pl.ds(pl.multiple_of(tile * 16, 16), 16))
+            return carry
+
+        lax.fori_loop(0, self.rows // 16, one, 0)
+
+    def far_step(self, step):
+        self.load_far(step).wait()
+        self.give_far(step).wait_recv()
+
+        def add(rows):
+            total = self.own_far[step, rows].astype(jnp.float32)
+            total += self.sib_far[step, rows].astype(jnp.float32)
+            self.own_far[step, rows] = total.astype(jnp.bfloat16)
+
+        self.tiles(add)
+        self.far(step).start()
+
+    def ring_step(self, way, step, first=False, last=False):
+        unit = self.unit
+        self.load_ring(way, step).wait()
+        self.give_ring(way, step).wait_recv()
+        if not first:
+            self.ring(way, step - 1).wait_recv()
+
+        @pl.when(self.spot.rep == way)
+        def _():
+            self.far(step).wait_recv()
+
+            def add_far(rows):
+                part = pl.ds(way * unit, 2 * unit)
+                total = self.sib_ring[way, step, rows, part].astype(jnp.float32)
+                total += self.got_far[step, rows].astype(jnp.float32)
+                self.sib_ring[way, step, rows, part] = total.astype(jnp.bfloat16)
+
+            self.tiles(add_far)
+
+        def add(rows):
+            total = self.own_ring[way, step, rows].astype(jnp.float32)
+            total += self.sib_ring[way, step, rows].astype(jnp.float32)
+            if not first:
+                total += self.got_ring[way, step - 1, rows].astype(jnp.float32)
+            self.own_ring[way, step, rows] = total.astype(jnp.bfloat16)
+
+        self.tiles(add)
+        if last:
+            self.last(way).start()
+        else:
+            self.ring(way, step).start()
+
+    def finish(self):
+        spot, unit = self.spot, self.unit
+        for way in (0, 1):
+            self.last(way).wait()
+        mine = [self.own_ring.at[way, spot.hops] for way in (0, 1)]
+        theirs = [self.got_last.at[way] for way in (0, 1)]
+
+        def write(lower, upper):
+            def body(rows):
+                def read(ref, first, count):
+                    return ref[rows, pl.ds(first * unit, count * unit)].astype(jnp.float32)
+
+                def put(first, count, value):
+                    self.out[rows, pl.ds(first * unit, count * unit)] = value
+
+                put(0, 2, read(lower[0], 0, 2))
+                put(2, 1, read(lower[0], 2, 1) + read(upper[0], 0, 1))
+                put(3, 2, read(lower[1], 0, 2) + read(upper[0], 1, 2))
+                put(5, 1, read(lower[1], 2, 1) + read(upper[1], 0, 1))
+                put(6, 2, read(upper[1], 1, 2))
+
+            self.tiles(body)
+
+        @pl.when(spot.rep == 0)
+        def _():
+            write(mine, theirs)
+
+        @pl.when(spot.rep == 1)
+        def _():
+            write(theirs, mine)
+
+        def one(step, carry):
+            self.give_far(step).wait_send()
+            self.far(step).wait_send()
+            for way in (0, 1):
+                self.give_ring(way, step).wait_send()
+
+            @pl.when(step < spot.hops)
+            def _():
+                for way in (0, 1):
+                    self.ring(way, step).wait_send()
+
+            return carry
+
+        lax.fori_loop(0, spot.chips, one, 0)
+
+
+def run_reduces(reduces, hops):
+    for reduce in reduces:
+        reduce.start()
+    for reduce in reduces:
+        reduce.far_step(0)
+    for reduce in reduces:
+        for way in (0, 1):
+            reduce.ring_step(way, 0, first=True)
+        reduce.far_step(1)
+
+    def one(step, carry):
+        for reduce in reduces:
+            for way in (0, 1):
+                reduce.ring_step(way, step)
+            reduce.far_step(step + 1)
+        return carry
+
+    lax.fori_loop(1, hops, one, 0)
+    for reduce in reduces:
+        for way in (0, 1):
+            reduce.ring_step(way, hops, last=True)
+    for reduce in reduces:
+        reduce.finish()
+
+
+class Tally:
+    def __init__(self, spot, mine, out, got, sems, own_sem):
+        self.spot, self.mine, self.out, self.got = spot, mine, out, got
+        self.sems = sems
+        self.whole = 2 * spot.shards
+        self.rank = spot.rep * spot.shards + spot.shard
+        self.own = pltpu.make_async_copy(mine, got.at[self.rank], own_sem)
+
+    def copy(self, k):
+        target = lax.rem(self.rank + k, self.whole)
+        shards = self.spot.shards
+        return remote(
+            self.mine,
+            self.got.at[self.rank],
+            self.sems,
+            (k,),
+            (target // shards, lax.rem(target, shards)),
+        )
+
+    def start(self):
+        def one(k, carry):
+            self.copy(k).start()
+            return carry
+
+        lax.fori_loop(1, self.whole, one, 0)
+        self.own.start()
+
+    def finish(self):
+        def one(k, carry):
+            self.copy(k).wait()
+            return carry
+
+        lax.fori_loop(1, self.whole, one, 0)
+        self.own.wait()
+
+        def add(k, total):
+            return total + self.got[k]
+
+        self.out[...] = lax.fori_loop(0, self.whole, add, jnp.zeros_like(self.out))
+
+
+def reduce_kernel(shards, group_count, swap_count, tally_count, *refs):
+    spot = Spot(shards)
+    total = group_count + swap_count + tally_count
+    inputs, outputs, scratch = refs[:total], refs[total : 2 * total], refs[2 * total :]
+    greet(spot, everyone=tally_count > 0)
+    reduces = [
+        Reduce(spot, inputs[g], outputs[g], scratch[19 * g : 19 * g + 19])
+        for g in range(group_count)
+    ]
+    scratch = scratch[19 * group_count :]
+    swaps = [
+        Swap(
+            spot,
+            inputs[group_count + i],
+            outputs[group_count + i],
+            scratch[3 * i : 3 * i + 2],
+            scratch[3 * i + 2],
+        )
+        for i in range(swap_count)
+    ]
+    scratch = scratch[3 * swap_count :]
+    tallies = [
+        Tally(spot, inputs[-1], outputs[-1], scratch[0], scratch[1:3], scratch[3])
+        for _ in range(tally_count)
+    ]
+    for each in tallies + swaps:
+        each.start()
+    run_reduces(reduces, spot.hops)
+    for each in tallies + swaps:
+        each.finish()
+
+
+def reduce_call(shards, partials, sent, tallied, collective_id):
+    scratch = []
+    out_shape, out_specs = [], []
+    anywhere = pl.BlockSpec(memory_space=pl.ANY)
+    inside = pl.BlockSpec(memory_space=pltpu.VMEM)
+    for part in partials:
+        rows, columns = part.shape[0] // shards, part.shape[1]
+        scratch += Reduce.scratch(shards, rows, columns)
+        out_shape.append(jax.ShapeDtypeStruct((rows, columns), jnp.float32))
+        out_specs.append(inside)
+    for rows in sent:
+        scratch += [DMA((shards,)), DMA((shards,)), DMA]
+        out_shape.append(jax.ShapeDtypeStruct(rows.shape, rows.dtype))
+        out_specs.append(anywhere)
+    for each in tallied:
+        scratch += [pltpu.VMEM((2 * shards, *each.shape), each.dtype)]
+        scratch += [DMA((2 * shards,)), DMA((2 * shards,)), DMA]
+        out_shape.append(jax.ShapeDtypeStruct(each.shape, each.dtype))
+        out_specs.append(inside)
+    in_specs = [anywhere] * (len(partials) + len(sent)) + [inside] * len(tallied)
+    results = pl.pallas_call(
+        functools.partial(reduce_kernel, shards, len(partials), len(sent), len(tallied)),
+        out_shape=out_shape,
+        in_specs=in_specs,
+        out_specs=out_specs,
+        scratch_shapes=scratch,
+        compiler_params=pltpu.CompilerParams(
+            collective_id=collective_id, has_side_effects=True, vmem_limit_bytes=56 << 20
+        ),
+    )(*partials, *sent, *tallied)
+    first, second = len(partials), len(partials) + len(sent)
+    return results[:first], results[first:second], results[second:]
+
+
 def on_device(
     tokens,
     cotangent,
@@ -210,29 +836,29 @@
     group_size = 4
     score_scale = 1.0 / math.sqrt(head_dim)
     outgoing = (
-        deal_buffer(tokens, send_slot, slot_total).reshape(shards, capacity, model_width),
-        deal_buffer(cotangent, send_slot, slot_total).reshape(shards, capacity, model_width),
-    )
-    arrived_tokens, arrived_grads = (
-        lax.all_to_all(outgoing[0], "shard", split_axis=0, concat_axis=0, tiled=True),
-        lax.all_to_all(outgoing[1], "shard", split_axis=0, concat_axis=0, tiled=True),
-    )
-    stream_rows = jnp.take(arrived_tokens.reshape(slot_total, model_width), recv_slot, axis=0)
-    grad_out_rows = jnp.take(arrived_grads.reshape(slot_total, model_width), recv_slot, axis=0)
+        deal_buffer(tokens, send_slot, slot_total),
+        deal_buffer(cotangent, send_slot, slot_total),
+    )
+    (full_in, full_out), (arrived_tokens,) = gather_call(
+        shards, [jnp.concatenate([w_query, w_key, w_value], axis=1), w_out], [outgoing[0]], 1
+    )
+    full_query, full_key, full_value = (
+        full_in[:, i * model_width : (i + 1) * model_width] for i in range(3)
+    )
+    (full_gate, full_up, full_down), (arrived_grads,) = gather_call(
+        shards, [w_gate, w_up, w_down], [outgoing[1]], 2
+    )
+    stream_rows = jnp.take(arrived_tokens, recv_slot, axis=0)
+    grad_out_rows = jnp.take(arrived_grads, recv_slot, axis=0)
     segment, position = layout(lengths[0], tok_rows)
     same_variate = variate[:, None] == variate[None, :]
     itself = jnp.arange(tok_rows)[:, None] == jnp.arange(tok_rows)[None, :]
     visible = (segment[:, None] == segment[None, :]) & ((valid_mask[None, :] > 0) | itself)
     cosine_table, sine_table = angle_tables(position, head_dim)
-    gathered = (
-        lax.all_gather(w_query, "shard", axis=0, tiled=True),
-        lax.all_gather(w_key, "shard", axis=0, tiled=True),
-        lax.all_gather(w_value, "shard", axis=0, tiled=True),
-        lax.all_gather(w_out, "shard", axis=0, tiled=True),
+    gain_bf_attn, gain_bf_mlp = (
         lax.all_gather(norm_attn, "shard", axis=0, tiled=True),
         lax.all_gather(norm_mlp, "shard", axis=0, tiled=True),
     )
-    full_query, full_key, full_value, full_out, gain_bf_attn, gain_bf_mlp = gathered
     gain_attn = gain_bf_attn.astype(jnp.float32)
     gain_mlp = gain_bf_mlp.astype(jnp.float32)
     stream = stream_rows.astype(jnp.float32)
@@ -254,10 +880,7 @@
     middle = stream + attn_out
     normed_mlp, factor_mlp = rms_parts(middle)
     input_mlp = (normed_mlp * gain_mlp).astype(jnp.bfloat16)
-    pieces = (
-        lax.all_gather(w_gate, "shard", axis=0, tiled=True),
-        lax.all_gather(w_up, "shard", axis=0, tiled=True),
-    )
+    pieces = (full_gate, full_up)
     columns = input_mlp
     gate_proj = jnp.dot(columns, pieces[0], preferred_element_type=jnp.float32)
     up_proj = jnp.dot(columns, pieces[1], preferred_element_type=jnp.float32)
@@ -266,21 +889,18 @@
     columns = hidden
     mlp_out = jnp.dot(
         columns,
-        lax.all_gather(w_down, "shard", axis=0, tiled=True),
+        full_down,
         preferred_element_type=jnp.float32,
     )
     result = middle + mlp_out
     result_bf = result.astype(jnp.bfloat16)
     grad_result = grad_out_rows.astype(jnp.float32)
-    grad_hidden = contract_cols(grad_out_rows, lax.all_gather(w_down, "shard", axis=0, tiled=True))
+    grad_hidden = contract_cols(grad_out_rows, full_down)
     grad_gate = (
         grad_hidden * up_proj * sigmoid_gate * (1.0 + gate_proj * (1.0 - sigmoid_gate))
     ).astype(jnp.bfloat16)
     grad_up = (grad_hidden * gate_proj * sigmoid_gate).astype(jnp.bfloat16)
-    pieces = (
-        lax.all_gather(w_gate, "shard", axis=0, tiled=True),
-        lax.all_gather(w_up, "shard", axis=0, tiled=True),
-    )
+    pieces = (full_gate, full_up)
     block_cols = contract_cols(grad_gate, pieces[0]) + contract_cols(grad_up, pieces[1])
     grad_gain_mlp = jnp.sum(block_cols * normed_mlp, axis=0)
     grad_middle = grad_result + rms_back(block_cols, normed_mlp, factor_mlp, gain_mlp)
@@ -313,26 +933,20 @@
     grad_stream = grad_middle + rms_back(grad_input_attn, normed_attn, factor_attn, gain_attn)
     grad_stream_bf = grad_stream.astype(jnp.bfloat16)
     projection_grads = jnp.concatenate([grad_query_proj, grad_key_proj, grad_value_proj], axis=1)
-    mlp_grads = jnp.concatenate([grad_gate, grad_up], axis=1)
-    width_share = lax.psum_scatter(
-        jnp.concatenate(
-            [
-                contract_rows(input_attn, projection_grads),
-                contract_rows(attended_bf, grad_branch),
-                contract_rows(input_mlp, mlp_grads),
-            ],
-            axis=1,
-        ),
-        "shard",
-        scatter_dimension=0,
-        tiled=True,
-    )
-    hidden_share = lax.psum_scatter(
-        contract_rows(hidden, grad_out_rows), "shard", scatter_dimension=0, tiled=True
-    )
-    width_share, hidden_share = (
-        lax.psum(width_share.astype(jnp.bfloat16), "rep").astype(jnp.float32),
-        lax.psum(hidden_share.astype(jnp.bfloat16), "rep").astype(jnp.float32),
+    homeward = (
+        deal_buffer(result_bf, recv_slot, slot_total),
+        deal_buffer(grad_stream_bf, recv_slot, slot_total),
+    )
+    (grad_gate_w, grad_up_w, hidden_share), (home_out,), _ = reduce_call(
+        shards,
+        [
+            contract_rows(input_mlp, grad_gate).astype(jnp.bfloat16),
+            contract_rows(input_mlp, grad_up).astype(jnp.bfloat16),
+            contract_rows(hidden, grad_out_rows).astype(jnp.bfloat16),
+        ],
+        [homeward[0]],
+        [],
+        3,
     )
     weight_rows = (valid_mask > 0).astype(jnp.float32)[:, None]
     square_sums = jnp.stack(
@@ -346,30 +960,34 @@
         ]
     )
     gain_grads = jnp.stack([grad_gain_attn, grad_gain_mlp])
-    total_sums, bias_grads, gain_totals = lax.psum(
-        (square_sums, grad_bias_local, gain_grads), ("rep", "shard")
-    )
+    small = [gain_grads.reshape(-1), grad_bias_local.reshape(-1), square_sums]
+    small_size = sum(each.shape[0] for each in small)
+    padded = -(-small_size // 1024) * 1024
+    small = jnp.concatenate([*small, jnp.zeros((padded - small_size,), jnp.float32)])
+    (grad_in, grad_out), (home_grad,), (small,) = reduce_call(
+        shards,
+        [
+            contract_rows(input_attn, projection_grads).astype(jnp.bfloat16),
+            contract_rows(attended_bf, grad_branch).astype(jnp.bfloat16),
+        ],
+        [homeward[1]],
+        [small.reshape(-1, 128)],
+        4,
+    )
+    small = small.reshape(-1)
+    gain_totals = small[: 2 * model_width].reshape(2, model_width)
+    bias_grads = small[2 * model_width : 2 * model_width + 2 * head_count].reshape(2, head_count)
+    total_sums = small[2 * model_width + 2 * head_count :][:6]
     root_means = jnp.sqrt(total_sums[:5] / (total_sums[5] * model_width))
     share_rows = model_width // shards
     share_start = lax.axis_index("shard") * share_rows
     grad_norm_attn = lax.dynamic_slice_in_dim(gain_totals[0], share_start, share_rows)
     grad_norm_mlp = lax.dynamic_slice_in_dim(gain_totals[1], share_start, share_rows)
-    homeward = (
-        deal_buffer(result_bf, recv_slot, slot_total).reshape(shards, capacity, model_width),
-        deal_buffer(grad_stream_bf, recv_slot, slot_total).reshape(shards, capacity, model_width),
-    )
-    home_out, home_grad = (
-        lax.all_to_all(homeward[0], "shard", split_axis=0, concat_axis=0, tiled=True),
-        lax.all_to_all(homeward[1], "shard", split_axis=0, concat_axis=0, tiled=True),
-    )
-    output = jnp.take(home_out.reshape(slot_total, model_width), send_slot, axis=0)
-    input_grad = jnp.take(home_grad.reshape(slot_total, model_width), send_slot, axis=0)
-    grad_query = width_share[:, 0:model_width]
-    grad_key = width_share[:, model_width : 2 * model_width]
-    grad_value = width_share[:, 2 * model_width : 3 * model_width]
-    grad_out = width_share[:, 3 * model_width : 4 * model_width]
-    grad_gate_w = width_share[:, 4 * model_width : 4 * model_width + hidden_width]
-    grad_up_w = width_share[:, 4 * model_width + hidden_width :]
+    output = jnp.take(home_out, send_slot, axis=0)
+    input_grad = jnp.take(home_grad, send_slot, axis=0)
+    grad_query, grad_key, grad_value = (
+        grad_in[:, i * model_width : (i + 1) * model_width] for i in range(3)
+    )
     return (
         output,
         input_grad,

time: 1240 us -> 819 us (0.66)
  waiting for transfers between devices: 769 us -> 0 us
  Pallas kernels: 0 us -> 513 us
  blocking collectives: 114 us -> 25.5 us
  other arithmetic: 81.7 us -> 50.9 us
  starting transfers between devices: 25.7 us -> 0 us
  matrix products: 172 us -> 158 us
  between operations: 16.9 us -> 3.15 us
    pallas_call x0 -> x4, Pallas kernels: none -> 513 us  [the longest x2 266 us: reduce_call(): pl.pallas_call(functools.partial(reduce_kernel, shards, len(partials), le...]
    reduce_scatter x2 -> x0, waiting for transfers between devices: 439 us -> none  [the longest x1 439 us: on_device(): lax.psum_scatter(jnp.concatenate([contract_rows(input_attn, projection_gr...]
    all_gather x7 -> x0, waiting for transfers between devices: 223 us -> none  [the longest x1 70 us: on_device(): lax.all_gather(w_up, 'shard', axis=0, tiled=True)]
    all_to_all x4 -> x0, waiting for transfers between devices: 94.3 us -> none  [the longest x1 51.2 us: on_device(): lax.all_to_all(outgoing[1], 'shard', split_axis=0, concat_axis=0, tiled=T...]
    unnamed x1, blocking collectives: 72.9 us -> 25.5 us
    psum x1 -> x0, blocking collectives: 41.4 us -> none  [on_device(): lax.psum((square_sums, grad_bias_local, gain_grads), ('rep', 'shard'))]
    concatenate x1, other arithmetic: 34 us -> 1.82 us  [on_device(): jnp.concatenate([w_query, w_key, w_value], axis=1)]
    all_to_all x4 -> x0, starting transfers between devices: 25.3 us -> none  [the longest x1 6.88 us: on_device(): lax.all_to_all(homeward[1], 'shard', split_axis=0, concat_axis=0, tiled=T...]
  transfers between devices with their start and end apart: 14 -> 0, of which waited for: 9 -> 0; matrix products, arithmetic and copies ran while one was open for 21% -> 0% of each run, Pallas kernels for 0% -> 0%
where the time goes in v1:
time: 819 us; the launch traced here: 810 us
  Pallas kernels  513 us (63%)
  matrix products  158 us (19%)
  local copies, waits for them, and re-layouts  58.9 us (7%)
  other arithmetic  50.9 us (6%)
  blocking collectives  25.5 us (3%)
    pallas_call x2, Pallas kernels, reduce_call(): pl.pallas_call(functools.partial(reduce_kernel, shards, len(partials), le...  266 us
    pallas_call x2, Pallas kernels, gather_call(): pl.pallas_call(functools.partial(gather_kernel, shards, len(pieces), len(...  247 us
    dot_general x7, matrix products, contract_cols(): lax.dot_general(left, right, (((1,), (1,)), ((), ())), preferred_element_...  40.9 us
    dot_general x5, matrix products, contract_rows(): lax.dot_general(left, right, (((0,), (0,)), ((), ())), preferred_element_...  36 us
    unnamed x1, blocking collectives  25.5 us
    unnamed x134, local copies, waits for them, and re-layouts  17.2 us

profile of v1, /device:TPU:8, one launch (start us, length us, event | category | flops | bytes accessed | tf_op | source)
XLA Modules:
  0.0 809.6 jit_solution(18424953593039411266)
XLA Ops:
  11.2 25.5 %all-reduce.2 = (bf16[1024]{0:T(1024)(128)(2,1)S(1)}, bf16[1024]{0:T(1024)(128)(2,1)S(1)}) all-reduce(bf16[1024]{0:T(1024)(128)(2,1)S(1)} %dynamic-update-slice, bf16[1024]{0:T(1024)(128)(2,1)S(1)} %dynamic-update-slice.1), channel_id=1, replica_groups=mesh['rep'=2,'shard'=16] {'shard'}, use_global_device_ids=true, to_apply=%add | all-reduce | flops 2048 | bytes 8192
  43.5 4.8 scatter_custom_fusion.1.refs_3_
  48.3 4.8 scatter_custom_fusion.refs_2_
  53.1 98.4 %shard_map.264 = (bf16[1024,3072]{1,0:T(8,128)(2,1)}, bf16[1024,1024]{1,0:T(8,128)(2,1)}, bf16[1024,1024]{1,0:T(8,128)(2,1)}) custom-call(bf16[64,3072]{1,0:T(8,128)(2,1)} %pad_maximum_fusion.6.refs_0_, bf16[64,1024]{1,0:T(8,128)(2,1)} %refs_1_.2, bf16[1024,1024]{1,0:T(8,128)(2,1)} %scatter_custom_fusion.refs_2_), custom_call_target="tpu_custom_call" | custom-call | tf_op jit(solution)/shard_map/pallas_call | solution.py:438
  151.5 4.6 gather_fusion
  187.6 148.5 %shard_map.265 = (bf16[1024,4096]{1,0:T(8,128)(2,1)}, bf16[1024,4096]{1,0:T(8,128)(2,1)}, bf16[4096,1024]{1,0:T(8,128)(2,1)}, bf16[1024,1024]{1,0:T(8,128)(2,1)}) custom-call(bf16[64,4096]{1,0:T(8,128)(2,1)} %refs_0_.1, bf16[64,4096]{1,0:T(8,128)(2,1)} %refs_1_.3, bf16[256,1024]{1,0:T(8,128)(2,1)} %refs_2_.1, bf16[1024,1024]{1,0:T(8,128)(2,1)} %scatter_custom_fusion.1.refs_3_), custom_call_target="tpu_custom_call" | custom-call | tf_op jit(solution)/shard_map/pallas_call | solution.py:438
  336.1 5.3 gather_fusion.1
  341.5 11.5 %fusion.138 = f32[512,4096]{1,0:T(8,128)} fusion(bf16[4096,1024]{1,0:T(8,128)(2,1)} %get-tuple-element.33, bf16[512,1024]{1,0:T(8,128)(2,1)} %gather_fusion.1, pred[512]{0:T(512)(128)(4,1)S(1)} %compare_and_fusion.1), kind=kOutput, calls=%fused_computation.252 | convolution fusion | flops 4295491584 | bytes 17826304 | tf_op jit(solution)/shard_map/dot_general | solution.py:185
  353.0 10.2 %fusion.148 = f32[512,4096]{1,0:T(8,128)} fusion(bf16[512,1024]{1,0:T(8,128)(2,1)S(1)} %copy-done.20, bf16[1024,4096]{1,0:T(8,128)(2,1)} %get-tuple-element.35), kind=kOutput, calls=%fused_computation.258 | convolution fusion | flops 4294967296 | bytes 17825792 | tf_op jit(solution)/shard_map/dot_general | solution.py:885
  363.2 13.6 %multiply_convert_fusion = (bf16[512,4096]{1,0:T(8,128)(2,1)}, bf16[512,4096]{1,0:T(8,128)(2,1)}, bf16[512,4096]{1,0:T(8,128)(2,1)}) fusion(f32[512,4096]{1,0:T(8,128)} %fusion.148, f32[512,4096]{1,0:T(8,128)} %fusion.138, bf16[512,1024]{1,0:T(8,128)(2,1)S(1)} %copy-done.20, bf16[1024,4096]{1,0:T(8,128)(2,1)S(1)} %copy-done.55), kind=kOutput, calls=%fused_computation.8 | convolution fusion | flops 4328521728 | bytes 38797312 | tf_op jit(solution)/shard_map/dot_general | solution.py:886
  376.8 10.7 %fusion.149 = f32[512,1024]{1,0:T(8,128)} fusion(bf16[512,4096]{1,0:T(8,128)(2,1)} %get-tuple-element.80, bf16[1024,4096]{1,0:T(8,128)(2,1)} %get-tuple-element.35), kind=kOutput, calls=%fused_computation.259 | convolution fusion | flops 4294967296 | bytes 14680064 | tf_op jit(solution)/shard_map/dot_general | solution.py:185
  387.5 7.5 convolution_add_fusion
  395.1 10.3 %fusion.28 = (f32[]{:T(128)}, f32[]{:T(128)}, f32[]{:T(128)}, f32[512]{0:T(512)S(1)}, f32[1024]{0:T(1024)S(1)}, /*index=5*/f32[]{:T(128)}, f32[512,1024]{1,0:T(8,128)}) fusion(f32[512]{0:T(512)S(1)} %copy-done.46, f32[512,1024]{1,0:T(8,128)S(1)} %get-tuple-element.78, f32[512]{0:T(512)S(1)} %add_rsqrt_fusion, f32[512,1024]{1,0:T(8,128)S(1)} %convolution_add_fusion, ...), kind=kOutput, calls=%fused_computation.85 | convolution fusion | flops 4304927232 | bytes 20985872 | tf_op jit(solution)/shard_map/dot_general | solution.py:890
  407.4 5.2 scatter_custom_fusion.2.refs_3_
  431.3 9.3 %convolution_convert_fusion.refs_2_ = bf16[4096,1024]{1,0:T(8,128)(2,1)} fusion(bf16[512,4096]{1,0:T(8,128)(2,1)} %get-tuple-element.79, bf16[512,1024]{1,0:T(8,128)(2,1)S(1)} %copy-done.13, pred[512]{0:T(512)(128)(4,1)S(1)} %compare_and_fusion.1), kind=kOutput, calls=%fused_computation.12 | convolution fusion | flops 4299685888 | bytes 13632000 | tf_op jit(solution)/shard_map/dot_general | solution.py:179
  452.8 14.4 %fusion = (f32[4]{0:T(128)S(1)}, f32[4]{0:T(128)S(1)}, f32[4]{0:T(128)S(1)}, f32[4]{0:T(128)S(1)}, f32[4]{0:T(128)S(1)}, /*index=5*/f32[4]{0:T(128)S(1)}, f32[4]...) fusion(pred[512,512]{0,1:T(8,128)(4,1)S(1)} %get-tuple-element., ...), kind=kLoop, calls=%fused_computation.24 | loop fusion | flops 37748704 | bytes 42270848 | tf_op jit(solution)/shard_map/reduce_sum | solution.py:148
  492.3 5.9 scatter_custom_fusion.3.refs_2_
  498.2 8.4 %convolution_convert_fusion.3.refs_0_ = bf16[1024,3072]{1,0:T(8,128)(2,1)} fusion(bf16[512,1024]{0,1:T(8,128)(2,1)} %bitcast.190, bf16[512,1024]{0,1:T(8,128)(2,1)} %bitcast.195, bf16[512,1024]{0,1:T(8,128)(2,1)} %bitcast.181, f32[1024]{0:T(1024)S(1)} %copy-done.40, f32[512]{0:T(512)S(1)} %copy-done.43, bf16[512,1024]{1,0:T(8,128)(2,1)S(1)} %gather_fusion, ...), kind=kOutput, calls=%fused_computation.15 | convolution fusion | flops 3236429824 | bytes 10492416 | tf_op jit(solution)/shard_map/dot_general | solution.py:179
  506.6 103.5 %shard_map.267 = (f32[64,3072]{1,0:T(8,128)}, f32[64,1024]{1,0:T(8,128)}, bf16[1024,1024]{1,0:T(8,128)(2,1)}, f32[24,128]{1,0:T(8,128)}) custom-call(bf16[1024,3072]{1,0:T(8,128)(2,1)} %convolution_convert_fusion.3.refs_0_, bf16[1024,1024]{1,0:T(8,128)(2,1)} %convolution_convert_fusion.4.refs_1_, bf16[1024,1024]{1,0:T(8,128)(2,1)} %scatter_custom_fusion.3.refs_2_, ...), custom_call_target="tpu_custom_call" | custom-call | tf_op jit(solution)/shard_map/pallas_call | solution.py:796
  613.3 4.7 gather_fusion.3
  620.8 9.1 %convolution_convert_fusion.2.refs_0_ = bf16[1024,4096]{1,0:T(8,128)(2,1)} fusion(bf16[512,1024]{1,0:T(8,128)(2,1)S(1)} %copy-done.21, bf16[512,4096]{1,0:T(8,128)(2,1)} %get-tuple-element.80), kind=kOutput, calls=%fused_computation.14 | convolution fusion | flops 4299161600 | bytes 13631488 | tf_op jit(solution)/shard_map/dot_general | solution.py:179
  629.9 6.7 convolution_convert_fusion.1.refs_1_
  636.6 162.7 %shard_map.266 = (f32[64,4096]{1,0:T(8,128)}, f32[64,4096]{1,0:T(8,128)}, f32[256,1024]{1,0:T(8,128)}, bf16[1024,1024]{1,0:T(8,128)(2,1)}) custom-call(bf16[1024,4096]{1,0:T(8,128)(2,1)} %convolution_convert_fusion.2.refs_0_, bf16[1024,4096]{1,0:T(8,128)(2,1)} %convolution_convert_fusion.1.refs_1_, bf16[4096,1024]{1,0:T(8,128)(2,1)} %convolution_convert_fusion.refs_2_, ...), custom_call_target="tpu_custom_call" | custom-call | tf_op jit(solution)/shard_map/pallas_call | solution.py:796
  799.4 4.6 gather_fusion.2
  (232 shorter events, 116.1 us)
Async XLA Ops:
  8.7 142.8 %copy-start.44 = (s32[512]{0:T(512)}, s32[512]{0:T(512)S(1)}, u32[]{:S(2)}) copy-start(s32[512]{0:T(512)S(1)} %compare_select_fusion.1) | copy-start | bytes 6148
  36.6 127.6 %copy-start.39 = (f32[1024]{0:T(1024)}, f32[1024]{0:T(1024)S(1)}, u32[]{:S(2)}) copy-start(f32[1024]{0:T(1024)S(1)} %convert_element_type.149) | copy-start | bytes 12292
  39.8 127.5 %copy-start.32 = (f32[512,32]{0,1:T(8,128)}, f32[512,32]{0,1:T(8,128)S(1)}, u32[]{:S(2)}) copy-start(f32[512,32]{0,1:T(8,128)S(1)} %get-tuple-element.101) | copy-start | bytes 196612
  160.8 20.4 %copy-start.10 = (bf16[512,1024]{0,1:T(8,128)(2,1)}, bf16[512,1024]{0,1:T(8,128)(2,1)S(1)}, u32[]{:S(2)}) copy-start(bf16[512,1024]{0,1:T(8,128)(2,1)S(1)} %copy.82) | copy-start | bytes 3145732
  168.3 10.2 %copy-start.22 = (bf16[512,16,2,32]{0,3,2,1:T(8,128)(2,1)}, bf16[512,16,2,32]{0,3,2,1:T(8,128)(2,1)S(1)}, u32[]{:S(2)}) copy-start(bf16[512,16,2,32]{0,3,2,1:T(8,128)(2,1)S(1)} %pad_maximum_fusion.2) | copy-start | bytes 3145732
  168.6 9.9 %copy-start.17 = (bf16[512,16,2,32]{0,3,2,1:T(8,128)(2,1)}, bf16[512,16,2,32]{0,3,2,1:T(8,128)(2,1)S(1)}, u32[]{:S(2)}) copy-start(bf16[512,16,2,32]{0,3,2,1:T(8,128)(2,1)S(1)} %fusion.46) | copy-start | bytes 3145732
  341.5 11.5 %copy-start.20 = (bf16[512,1024]{1,0:T(8,128)(2,1)S(1)}, bf16[512,1024]{1,0:T(8,128)(2,1)}, u32[]{:S(2)}) copy-start(bf16[512,1024]{1,0:T(8,128)(2,1)} %multiply_convert_fusion.7) | copy-start | bytes 3145732
  353.0 10.2 %copy-start.55 = (bf16[1024,4096]{1,0:T(8,128)(2,1)S(1)}, bf16[1024,4096]{1,0:T(8,128)(2,1)}, u32[]{:S(2)}) copy-start(bf16[1024,4096]{1,0:T(8,128)(2,1)} %get-tuple-element.34) | copy-start | bytes 25165828
  376.8 18.2 %slice-start = ((s8[8388608]{0:T(1024)(128)(4,1)}), s8[4194304]{0:T(1024)(128)(4,1)S(1)}, s32[]{:S(2)}) async-start(s8[8388608]{0:T(1024)(128)(4,1)} %bitcast.203), calls=%async_computation | async-start | bytes 8388608
  387.5 7.5 copy-start.46
  387.5 7.6 slice-start.1
  395.1 10.3 %copy-start.12 = (bf16[512,1024]{1,0:T(8,128)(2,1)S(1)}, bf16[512,1024]{1,0:T(8,128)(2,1)}, u32[]{:S(2)}) copy-start(bf16[512,1024]{1,0:T(8,128)(2,1)} %gather_fusion.1) | copy-start | bytes 3145732
  431.3 9.3 %copy-start.1 = (f32[4,512,512]{1,2,0:T(8,128)S(1)}, f32[4,512,512]{1,2,0:T(8,128)}, u32[]{:S(2)}) copy-start(f32[4,512,512]{1,2,0:T(8,128)} %copy-done) | copy-start | bytes 12582916
  431.3 9.3 %copy-start.11 = (bf16[512,1024]{0,1:T(8,128)(2,1)S(1)}, bf16[512,1024]{0,1:T(8,128)(2,1)}, u32[]{:S(2)}) copy-start(bf16[512,1024]{0,1:T(8,128)(2,1)} %copy-done.10) | copy-start | bytes 3145732
  467.2 5.1 copy-start.16
  467.5 4.8 copy-start.18
  483.7 8.6 %copy-start.9 = (f32[512,1024]{1,0:T(8,128)S(1)}, f32[512,1024]{1,0:T(8,128)}, u32[]{:S(2)}) copy-start(f32[512,1024]{1,0:T(8,128)} %multiply_add_fusion) | copy-start | bytes 6291460
  506.6 106.7 %copy-start.38 = (s32[1024]{0:T(1024)S(1)}, s32[1024]{0:T(1024)}, u32[]{:S(2)}) copy-start(s32[1024]{0:T(1024)} %pad_clamp_fusion) | copy-start | bytes 12292
  613.3 4.7 copy-start.37
  613.3 6.6 copy-start.31
  613.3 7.5 copy-start.21
  620.8 9.1 %copy-start.57 = (bf16[512,4096]{1,0:T(8,128)(2,1)S(1)}, bf16[512,4096]{1,0:T(8,128)(2,1)}, u32[]{:S(2)}) copy-start(bf16[512,4096]{1,0:T(8,128)(2,1)} %get-tuple-element.81) | copy-start | bytes 12582916
  799.3 4.6 copy-start.45
  804.0 4.2 copy-start.28
  (38 other events, 75.2 us)

commit v2 on v1

v2 whole, which is shorter than its diff:
```python
import functools
import math

import jax
import jax.numpy as jnp
from jax import lax
from jax.experimental import pallas as pl
from jax.experimental.pallas import tpu as pltpu
from jax.sharding import PartitionSpec as P

MESH = pl.DeviceIdType.MESH
DMA = pltpu.SemaphoreType.DMA
epsilon = 1e-06
masked_score = -1e30


def angle_tables(position, head_dim):
    half_dim = head_dim // 2
    inverse_freq = 1.0 / 10000.0 ** (jnp.arange(half_dim, dtype=jnp.float32) / half_dim)
    theta_angle = position.astype(jnp.float32)[:, None] * inverse_freq[None, :]
    return (jnp.cos(theta_angle), jnp.sin(theta_angle))


def layout(lengths_row, tok_rows):
    slot_ids = jnp.arange(tok_rows, dtype=jnp.int32)
    seq_ends = jnp.cumsum(lengths_row)
    segment = jnp.sum((slot_ids[:, None] >= seq_ends[None, :]).astype(jnp.int32), axis=1)
    starts = seq_ends - lengths_row
    chosen = segment[:, None] == jnp.arange(lengths_row.shape[0], dtype=jnp.int32)[None, :]
    begins = jnp.sum(jnp.where(chosen, starts[None, :], 0), axis=1)
    return (segment, slot_ids - begins)


def ring_place(chip, chips):
    return jnp.where(chip % 2 == 0, chip // 2, chips - 1 - chip // 2)


def ring_chip(place, chips):
    wrapped = lax.rem(place + 2 * chips, chips)
    return jnp.where(wrapped < chips // 2, 2 * wrapped, 2 * (chips - 1 - wrapped) + 1)


class Spot:
    def __init__(self, shards):
        self.shards = shards
        self.chips = shards // 2
        self.hops = self.chips - 1
        self.rep = lax.axis_index("rep")
        self.shard = lax.axis_index("shard")
        self.core = lax.rem(self.shard, 2)
        self.place = ring_place(self.shard // 2, self.chips)
        self.sibling = self.shard + 1 - 2 * self.core

    def block(self, place, core=None):
        return 2 * ring_chip(place, self.chips) + (self.core if core is None else core)

    def along(self, way, distance):
        return self.place - distance if way == 0 else self.place + distance

    def ahead(self, way):
        return (self.rep, self.block(self.along(way, -1)))


def greet(spot, everyone=False):
    barrier = pltpu.get_barrier_semaphore()
    shards = spot.shards

    def peer(k, carry):
        target = lax.rem(spot.shard + k, shards)
        pl.semaphore_signal(barrier, inc=1, device_id=(spot.rep, target), device_id_type=MESH)
        return carry

    lax.fori_loop(1, shards, peer, 0)
    if not everyone:
        pl.semaphore_signal(
            barrier, inc=1, device_id=(1 - spot.rep, spot.shard), device_id_type=MESH
        )
        pl.semaphore_wait(barrier, shards)
        return

    def other(k, carry):
        pl.semaphore_signal(barrier, inc=1, device_id=(1 - spot.rep, k), device_id_type=MESH)
        return carry

    lax.fori_loop(0, shards, other, 0)
    pl.semaphore_wait(barrier, 2 * shards - 1)


def remote(src, dst, sems, at, target):
    return pltpu.make_async_remote_copy(
        src_ref=src,
        dst_ref=dst,
        send_sem=sems[0].at[at],
        recv_sem=sems[1].at[at],
        device_id=target,
        device_id_type=MESH,
    )


class Swap:
    def __init__(self, spot, source, arrived, sems, own_sem):
        self.spot, self.sems = spot, sems
        self.source, self.arrived = source, arrived
        self.capacity = arrived.shape[0] // spot.shards
        self.own = pltpu.make_async_copy(
            self.part(spot.shard), arrived.at[self.rows(spot.shard)], own_sem
        )

    def rows(self, shard):
        return pl.ds(pl.multiple_of(shard * self.capacity, 8), self.capacity)

    def part(self, shard):
        if self.source.shape[0] == self.capacity:
            return self.source
        return self.source.at[self.rows(shard)]

    def copy(self, k):
        spot = self.spot
        target = lax.rem(spot.shard + k, spot.shards)
        return remote(
            self.part(target),
            self.arrived.at[self.rows(spot.shard)],
            self.sems,
            (k,),
            (spot.rep, target),
        )

    def start(self, slot, slots):
        size = -(-self.spot.shards // slots)

        def one(k, carry):
            @pl.when(k == 0)
            def _():
                self.own.start()

            @pl.when(k > 0)
            def _():
                self.copy(k).start()

            return carry

        first = jnp.minimum(slot * size, self.spot.shards)
        lax.fori_loop(first, jnp.minimum(first + size, self.spot.shards), one, 0)

    def finish(self):
        def one(k, carry):
            self.copy(k).wait()
            return carry

        lax.fori_loop(1, self.spot.shards, one, 0)
        self.own.wait()


class Gather:
    def __init__(self, spot, lent, shard_ref, full_ref, sems):
        self.spot, self.lent, self.shard_ref, self.full_ref = spot, lent, shard_ref, full_ref
        self.rows = shard_ref.shape[0]
        self.unit = shard_ref.shape[1] // 8
        self.count = (8 - lent) // 2
        self.ring_sems, self.near_sems, self.far_sems, self.far_near_sems = (
            sems[0:2],
            sems[2:4],
            sems[4:6],
            sems[6:8],
        )
        self.whole_sems, self.own_sem = sems[8:10], sems[10]
        self.far_ways = (0, 1) if lent == 4 else (0,)

    def first(self, way):
        return self.lent * self.spot.rep + self.count * way

    def cut(self, block, first, count):
        columns = pl.ds(pl.multiple_of(first * self.unit, 128), count * self.unit)
        return self.full_ref.at[pl.ds(block * self.rows, self.rows), columns]

    def ring(self, way, hop, source=None):
        spot = self.spot
        region = self.cut(spot.block(spot.along(way, hop)), self.first(way), self.count)
        return remote(
            region if source is None else source,
            region,
            self.ring_sems,
            (way, hop),
            spot.ahead(way),
        )

    def near(self, way, hop):
        spot = self.spot
        region = self.cut(spot.block(spot.along(way, hop + 1)), self.first(way), self.count)
        return remote(region, region, self.near_sems, (way, hop), (spot.rep, spot.sibling))

    def far_region(self, way, hop, owner):
        spot = self.spot
        if self.lent == 4:
            block = spot.block(spot.along(way, hop + 1))
            return self.cut(block, 4 * owner + 2 * way, 2)
        turn = (1 - 2 * owner) * (hop + 1)
        return self.cut(spot.block(spot.place - turn), 6 * owner, 2)

    def far(self, way, hop):
        spot = self.spot
        region = self.far_region(way, hop, spot.rep)
        return remote(region, region, self.far_sems, (way, hop), (1 - spot.rep, spot.shard))

    def far_near(self, way, hop):
        spot = self.spot
        region = self.far_region(way, hop, 1 - spot.rep)
        return remote(region, region, self.far_near_sems, (way, hop), (spot.rep, spot.sibling))

    def own(self):
        spot = self.spot
        mine = self.full_ref.at[pl.ds(spot.shard * self.rows, self.rows)]
        whole = remote(self.shard_ref, mine, self.whole_sems, (0,), (spot.rep, spot.sibling))
        return whole, pltpu.make_async_copy(self.shard_ref, mine, self.own_sem)

    def start(self):
        for way in (0, 1):
            columns = pl.ds(
                pl.multiple_of(self.first(way) * self.unit, 128), self.count * self.unit
            )
            self.ring(way, 0, self.shard_ref.at[:, columns]).start()
        for copy in self.own():
            copy.start()

    def step(self, hop):
        for way in (0, 1):
            self.ring(way, hop).wait_recv()

            @pl.when(hop < self.spot.hops - 1)
            def _():
                self.ring(way, hop + 1).start()

        for way in self.far_ways:
            self.far(way, hop).start()
        for way in (0, 1):
            self.near(way, hop).start()

        @pl.when(hop > 0)
        def _():
            self.relay(hop - 1)

    def relay(self, hop):
        for way in self.far_ways:
            self.far(way, hop).wait_recv()
            self.far_near(way, hop).start()

    def finish(self):
        for copy in self.own():
            copy.wait()

        def one(hop, carry):
            for way in (0, 1):
                self.ring(way, hop).wait_send()
                self.near(way, hop).wait()
            for way in self.far_ways:
                self.far(way, hop).wait_send()
                self.far_near(way, hop).wait()
            return carry

        lax.fori_loop(0, self.spot.hops, one, 0)

    @staticmethod
    def scratch(hops):
        return [DMA((2, hops))] * 8 + [DMA((1,))] * 2 + [DMA]


class GatherAll:
    def __init__(self, spot, lents, swap_count, inputs, outputs, scratch):
        count = len(lents)
        self.spot = spot
        self.gathers = [
            Gather(spot, lents[g], inputs[g], outputs[g], scratch[11 * g : 11 * g + 11])
            for g in range(count)
        ]
        scratch = scratch[11 * count :]
        self.swaps = [
            Swap(
                spot,
                inputs[count + i],
                outputs[count + i],
                scratch[3 * i : 3 * i + 2],
                scratch[3 * i + 2],
            )
            for i in range(swap_count)
        ]

    def start(self):
        greet(self.spot)
        for gather in self.gathers:
            gather.start()

    def step(self, hop):
        for swap in self.swaps:
            swap.start(hop, self.spot.hops)
        for gather in self.gathers:
            gather.step(hop)

    def steps(self, slot, slots):
        size = -(-self.spot.hops // slots)

        def one(hop, carry):
            self.step(hop)
            return carry

        first = jnp.minimum(slot * size, self.spot.hops)
        lax.fori_loop(first, jnp.minimum(first + size, self.spot.hops), one, 0)

    def finish(self):
        for gather in self.gathers:
            gather.relay(self.spot.hops - 1)
        for each in self.gathers + self.swaps:
            each.finish()

    @staticmethod
    def scratch(shards, count, swap_count):
        return Gather.scratch(shards // 2 - 1) * count + [
            DMA((shards,)),
            DMA((shards,)),
            DMA,
        ] * swap_count


def gather_kernel(shards, lents, swap_count, *refs):
    spot = Spot(shards)
    total = len(lents) + swap_count
    work = GatherAll(
        spot, lents, swap_count, refs[:total], refs[total : 2 * total], refs[2 * total :]
    )
    work.start()
    work.steps(0, 1)
    work.finish()


def gather_shapes(shards, pieces, sent, shared):
    return (
        [
            jax.ShapeDtypeStruct((shards * piece.shape[0], piece.shape[1]), piece.dtype)
            for piece in pieces
        ]
        + [jax.ShapeDtypeStruct(rows.shape, rows.dtype) for rows in sent]
        + [
            jax.ShapeDtypeStruct((shards * each.shape[0], each.shape[1]), each.dtype)
            for each in shared
        ]
    )


def gather_call(shards, pieces, lents, sent, shared, collective_id):
    swaps = [*sent, *shared]
    anywhere = pl.BlockSpec(memory_space=pl.ANY)
    results = pl.pallas_call(
        functools.partial(gather_kernel, shards, lents, len(swaps)),
        out_shape=gather_shapes(shards, pieces, sent, shared),
        in_specs=[anywhere] * (len(pieces) + len(swaps)),
        out_specs=[anywhere] * (len(pieces) + len(swaps)),
        scratch_shapes=GatherAll.scratch(shards, len(pieces), len(swaps)),
        compiler_params=pltpu.CompilerParams(
            collective_id=collective_id, has_side_effects=True
        ),
    )(*pieces, *swaps)
    first, second = len(pieces), len(pieces) + len(sent)
    return results[:first], results[first:second], results[second:]


class Reduce:
    def __init__(self, spot, partial_ref, out_ref, refs):
        self.spot, self.partial, self.out = spot, partial_ref, out_ref
        self.rows, self.columns = out_ref.shape
        self.unit = self.columns // 8
        (
            self.own_ring,
            self.sib_ring,
            self.got_ring,
            self.own_far,
            self.sib_far,
            self.got_far,
            self.got_last,
        ) = refs[:7]
        sems = refs[7:]
        self.load_ring_sem, self.load_far_sem = sems[0], sems[1]
        self.sib_ring_sems, self.sib_far_sems = sems[2:4], sems[4:6]
        self.ring_sems, self.far_sems, self.last_sems = sems[6:8], sems[8:10], sems[10:12]

    @staticmethod
    def scratch(shards, rows, columns):
        chips = shards // 2
        unit = columns // 8
        half = jnp.bfloat16
        buffers = [
            pltpu.VMEM((2, chips, rows, 3 * unit), half),
            pltpu.VMEM((2, chips, rows, 3 * unit), half),
            pltpu.VMEM((2, chips - 1, rows, 3 * unit), half),
            pltpu.VMEM((chips, rows, 2 * unit), half),
            pltpu.VMEM((chips, rows, 2 * unit), half),
            pltpu.VMEM((chips, rows, 2 * unit), half),
            pltpu.VMEM((2, rows, 3 * unit), half),
        ]
        sems = [DMA((2, chips)), DMA((chips,))]
        sems += [DMA((2, chips))] * 2 + [DMA((chips,))] * 2
        sems += [DMA((2, chips))] * 2 + [DMA((chips,))] * 2 + [DMA((2,))] * 2
        return buffers + sems

    def cut(self, block, first, count):
        columns = pl.ds(pl.multiple_of(first * self.unit, 128), count * self.unit)
        return self.partial.at[pl.ds(block * self.rows, self.rows), columns]

    def ring_cut(self, way, step, core):
        spot = self.spot
        return self.cut(
            spot.block(spot.along(way, step + 1), core), 2 * spot.rep + 3 * way, 3
        )

    def far_cut(self, step, core):
        spot = self.spot
        place = spot.place + (1 - 2 * spot.rep) * (step + 1)
        return self.cut(spot.block(place, core), 6 * (1 - spot.rep), 2)

    def load_ring(self, way, step):
        return pltpu.make_async_copy(
            self.ring_cut(way, step, self.spot.core),
            self.own_ring.at[way, step],
            self.load_ring_sem.at[way, step],
        )

    def load_far(self, step):
        return pltpu.make_async_copy(
            self.far_cut(step, self.spot.core), self.own_far.at[step], self.load_far_sem.at[step]
        )

    def give_ring(self, way, step):
        spot = self.spot
        return remote(
            self.ring_cut(way, step, 1 - spot.core),
            self.sib_ring.at[way, step],
            self.sib_ring_sems,
            (way, step),
            (spot.rep, spot.sibling),
        )

    def give_far(self, step):
        spot = self.spot
        return remote(
            self.far_cut(step, 1 - spot.core),
            self.sib_far.at[step],
            self.sib_far_sems,
            (step,),
            (spot.rep, spot.sibling),
        )

    def ring(self, way, step):
        return remote(
            self.own_ring.at[way, step],
            self.got_ring.at[way, step],
            self.ring_sems,
            (way, step),
            self.spot.ahead(way),
        )

    def far(self, step):
        spot = self.spot
        return remote(
            self.own_far.at[step],
            self.got_far.at[step],
            self.far_sems,
            (step,),
            (1 - spot.rep, spot.shard),
        )

    def last(self, way):
        spot = self.spot
        return remote(
            self.own_ring.at[way, spot.hops],
            self.got_last.at[way],
            self.last_sems,
            (way,),
            (1 - spot.rep, spot.shard),
        )

    def start(self, step):
        self.load_far(step).start()
        self.give_far(step).start()
        for way in (0, 1):
            self.load_ring(way, step).start()
            self.give_ring(way, step).start()

    def tiles(self, body):
        def one(tile, carry):
            body(pl.ds(pl.multiple_of(tile * 16, 16), 16))
            return carry

        lax.fori_loop(0, self.rows // 16, one, 0)

    def far_step(self, step):
        self.load_far(step).wait()
        self.give_far(step).wait_recv()

        def add(rows):
            total = self.own_far[step, rows].astype(jnp.float32)
            total += self.sib_far[step, rows].astype(jnp.float32)
            self.own_far[step, rows] = total.astype(jnp.bfloat16)

        self.tiles(add)
        self.far(step).start()

    def ring_step(self, way, step):
        unit = self.unit
        self.load_ring(way, step).wait()
        self.give_ring(way, step).wait_recv()

        @pl.when(self.spot.rep == way)
        def _():
            self.far(step).wait_recv()

            def add_far(rows):
                part = pl.ds(way * unit, 2 * unit)
                total = self.sib_ring[way, step, rows, part].astype(jnp.float32)
                total += self.got_far[step, rows].astype(jnp.float32)
                self.sib_ring[way, step, rows, part] = total.astype(jnp.bfloat16)

            self.tiles(add_far)

        @pl.when(step == 0)
        def _():
            def add(rows):
                total = self.own_ring[way, step, rows].astype(jnp.float32)
                total += self.sib_ring[way, step, rows].astype(jnp.float32)
                self.own_ring[way, step, rows] = total.astype(jnp.bfloat16)

            self.tiles(add)

        @pl.when(step > 0)
        def _():
            self.ring(way, step - 1).wait_recv()

            def add(rows):
                total = self.own_ring[way, step, rows].astype(jnp.float32)
                total += self.sib_ring[way, step, rows].astype(jnp.float32)
                total += self.got_ring[way, step - 1, rows].astype(jnp.float32)
                self.own_ring[way, step, rows] = total.astype(jnp.bfloat16)

            self.tiles(add)

        @pl.when(step < self.spot.hops)
        def _():
            self.ring(way, step).start()

        @pl.when(step == self.spot.hops)
        def _():
            self.last(way).start()

    def finish(self):
        spot, unit = self.spot, self.unit
        for way in (0, 1):
            self.last(way).wait()
        mine = [self.own_ring.at[way, spot.hops] for way in (0, 1)]
        theirs = [self.got_last.at[way] for way in (0, 1)]

        def write(lower, upper):
            def body(rows):
                def read(ref, first, count):
                    return ref[rows, pl.ds(first * unit, count * unit)].astype(jnp.float32)

                def put(first, count, value):
                    self.out[rows, pl.ds(first * unit, count * unit)] = value

                put(0, 2, read(lower[0], 0, 2))
                put(2, 1, read(lower[0], 2, 1) + read(upper[0], 0, 1))
                put(3, 2, read(lower[1], 0, 2) + read(upper[0], 1, 2))
                put(5, 1, read(lower[1], 2, 1) + read(upper[1], 0, 1))
                put(6, 2, read(upper[1], 1, 2))

            self.tiles(body)

        @pl.when(spot.rep == 0)
        def _():
            write(mine, theirs)

        @pl.when(spot.rep == 1)
        def _():
            write(theirs, mine)

        def one(step, carry):
            self.give_far(step).wait_send()
            self.far(step).wait_send()
            for way in (0, 1):
                self.give_ring(way, step).wait_send()

            @pl.when(step < spot.hops)
            def _():
                for way in (0, 1):
                    self.ring(way, step).wait_send()

            return carry

        lax.fori_loop(0, spot.chips, one, 0)


class Tally:
    def __init__(self, spot, mine, out, got, sems, own_sem):
        self.spot, self.mine, self.out, self.got = spot, mine, out, got
        self.sems = sems
        self.whole = 2 * spot.shards
        self.rank = spot.rep * spot.shards + spot.shard
        self.own = pltpu.make_async_copy(mine, got.at[self.rank], own_sem)

    def copy(self, k):
        target = lax.rem(self.rank + k, self.whole)
        shards = self.spot.shards
        return remote(
            self.mine,
            self.got.at[self.rank],
            self.sems,
            (k,),
            (target // shards, lax.rem(target, shards)),
        )

    def start(self):
        def one(k, carry):
            self.copy(k).start()
            return carry

        lax.fori_loop(1, self.whole, one, 0)
        self.own.start()

    def finish(self):
        def one(k, carry):
            self.copy(k).wait()
            return carry

        lax.fori_loop(1, self.whole, one, 0)
        self.own.wait()

        def add(k, total):
            return total + self.got[k]

        self.out[...] = lax.fori_loop(0, self.whole, add, jnp.zeros_like(self.out))


class ReduceAll:
    def __init__(self, spot, count, swap_count, tally_count, inputs, outputs, scratch):
        self.spot = spot
        self.reduces = [
            Reduce(spot, inputs[g], outputs[g], scratch[19 * g : 19 * g + 19])
            for g in range(count)
        ]
        scratch = scratch[19 * count :]
        self.swaps = [
            Swap(
                spot,
                inputs[count + i],
                outputs[count + i],
                scratch[3 * i : 3 * i + 2],
                scratch[3 * i + 2],
            )
            for i in range(swap_count)
        ]
        scratch = scratch[3 * swap_count :]
        self.tallies = [
            Tally(spot, inputs[-1], outputs[-1], scratch[0], scratch[1:3], scratch[3])
            for _ in range(tally_count)
        ]

    def start(self):
        greet(self.spot, everyone=len(self.tallies) > 0)

        def one(step, carry):
            for reduce in self.reduces:
                reduce.start(step)
            return carry

        lax.fori_loop(0, self.spot.chips, one, 0)
        for tally in self.tallies:
            tally.start()
        for reduce in self.reduces:
            reduce.far_step(0)

    def step(self, step):
        chips = self.spot.chips
        for swap in self.swaps:
            swap.start(step, chips)
        for reduce in self.reduces:
            for way in (0, 1):
                reduce.ring_step(way, step)

            @pl.when(step < chips - 1)
            def _():
                reduce.far_step(step + 1)

    def steps(self, slot, slots):
        size = -(-self.spot.chips // slots)

        def one(step, carry):
            self.step(step)
            return carry

        first = jnp.minimum(slot * size, self.spot.chips)
        lax.fori_loop(first, jnp.minimum(first + size, self.spot.chips), one, 0)

    def finish(self):
        for each in self.reduces + self.swaps + self.tallies:
            each.finish()


def reduce_kernel(shards, group_count, swap_count, tally_count, *refs):
    total = group_count + swap_count + tally_count
    work = ReduceAll(
        Spot(shards),
        group_count,
        swap_count,
        tally_count,
        refs[:total],
        refs[total : 2 * total],
        refs[2 * total :],
    )
    work.start()
    work.steps(0, 1)
    work.finish()


def reduce_call(shards, partials, sent, tallied, collective_id):
    scratch = []
    out_shape, out_specs = [], []
    anywhere = pl.BlockSpec(memory_space=pl.ANY)
    inside = pl.BlockSpec(memory_space=pltpu.VMEM)
    for part in partials:
        rows, columns = part.shape[0] // shards, part.shape[1]
        scratch += Reduce.scratch(shards, rows, columns)
        out_shape.append(jax.ShapeDtypeStruct((rows, columns), jnp.float32))
        out_specs.append(inside)
    for rows in sent:
        scratch += [DMA((shards,)), DMA((shards,)), DMA]
        out_shape.append(jax.ShapeDtypeStruct(rows.shape, rows.dtype))
        out_specs.append(anywhere)
    for each in tallied:
        scratch += [pltpu.VMEM((2 * shards, *each.shape), each.dtype)]
        scratch += [DMA((2 * shards,)), DMA((2 * shards,)), DMA]
        out_shape.append(jax.ShapeDtypeStruct(each.shape, each.dtype))
        out_specs.append(inside)
    in_specs = [anywhere] * (len(partials) + len(sent)) + [inside] * len(tallied)
    results = pl.pallas_call(
        functools.partial(reduce_kernel, shards, len(partials), len(sent), len(tallied)),
        out_shape=out_shape,
        in_specs=in_specs,
        out_specs=out_specs,
        scratch_shapes=scratch,
        compiler_params=pltpu.CompilerParams(
            collective_id=collective_id, has_side_effects=True, vmem_limit_bytes=56 << 20
        ),
    )(*partials, *sent, *tallied)
    first, second = len(partials), len(partials) + len(sent)
    return results[:first], results[first:second], results[second:]


def matmul(left, right, left_dim=1, right_dim=0):
    return lax.dot_general(
        left, right, (((left_dim,), (right_dim,)), ((), ())), preferred_element_type=jnp.float32
    )


def pick_rows(slot_column, slot_total):
    shape = (slot_column.shape[0], slot_total)
    return (slot_column == lax.broadcasted_iota(jnp.int32, shape, 1)).astype(jnp.bfloat16)


def place_rows(slot_row, slot_total):
    shape = (slot_total, slot_row.shape[1])
    return (slot_row == lax.broadcasted_iota(jnp.int32, shape, 0)).astype(jnp.bfloat16)


def pack_kernel(rows_ref, tokens_ref, cotangent_ref, tokens_out, cotangent_out):
    chosen = place_rows(rows_ref[0:1, :], tokens_out.shape[0])
    tokens_out[...] = matmul(chosen, tokens_ref[...]).astype(jnp.bfloat16)
    cotangent_out[...] = matmul(chosen, cotangent_ref[...]).astype(jnp.bfloat16)


def unpack_kernel(columns_ref, output_ref, grad_ref, output_out, grad_out):
    chosen = pick_rows(columns_ref[:, 0:1], output_ref.shape[0])
    output_out[...] = matmul(chosen, output_ref[...]).astype(jnp.bfloat16)
    grad_out[...] = matmul(chosen, grad_ref[...]).astype(jnp.bfloat16)


def local_call(kernel, out_shape, inputs, spaces=None, scratch=()):
    inside = pl.BlockSpec(memory_space=pltpu.VMEM)
    return pl.pallas_call(
        kernel,
        out_shape=out_shape,
        in_specs=spaces or [inside] * len(inputs),
        out_specs=[inside] * len(out_shape),
        scratch_shapes=list(scratch),
        compiler_params=pltpu.CompilerParams(vmem_limit_bytes=56 << 20),
    )(*inputs)


def segment_of(index, lengths_ref):
    first = lengths_ref[0, 0]
    second = first + lengths_ref[0, 1]
    third = second + lengths_ref[0, 2]
    return (
        (index >= first).astype(jnp.int32)
        + (index >= second).astype(jnp.int32)
        + (index >= third).astype(jnp.int32)
    )


def pair_masks(columns_ref, rows_ref, lengths_ref, same_ref, hidden_ref):
    size = columns_ref.shape[0]
    shape = (size, size)
    key_id = lax.broadcasted_iota(jnp.int32, shape, 0)
    query_id = lax.broadcasted_iota(jnp.int32, shape, 1)
    key_column = lax.broadcasted_iota(jnp.int32, (size, 1), 0)
    query_row = lax.broadcasted_iota(jnp.int32, (1, size), 1)
    together = segment_of(key_column, lengths_ref) == segment_of(query_row, lengths_ref)
    seen = together & ((columns_ref[:, 3:4] > 0) | (key_id == query_id))
    same_ref[...] = (columns_ref[:, 2:3] == rows_ref[2:3, :]).astype(jnp.float32)
    hidden_ref[...] = jnp.where(seen, 0.0, masked_score)


def turn(values, cosine, sine):
    width = values.shape[1]
    lane = lax.broadcasted_iota(jnp.int32, values.shape, 1)
    other = jnp.where(
        lane % 64 < 32, pltpu.roll(values, width - 32, 1), pltpu.roll(values, 32, 1)
    )
    return values * cosine + other * sine


def head_lanes(values, head):
    lane = lax.broadcasted_iota(jnp.int32, values.shape, 1)
    return jnp.where((lane < 64) == (head == 0), values, jnp.zeros_like(values))


def project(input_ref, weight_ref, cosine_ref, sine_ref, out_ref, scale):
    width = weight_ref.shape[0]
    cosine = jnp.concatenate([cosine_ref[...]] * 2, axis=1)
    sine = jnp.concatenate([sine_ref[...]] * 2, axis=1)

    def one(i, carry):
        def columns(part):
            return pl.ds(pl.multiple_of(part * width + i * 256, 256), 256)

        query = matmul(input_ref[...], weight_ref[:, columns(0)])
        out_ref[:, columns(0)] = (turn(query, cosine, sine) * scale).astype(jnp.bfloat16)
        key = matmul(input_ref[...], weight_ref[:, columns(1)])
        out_ref[:, columns(1)] = turn(key, cosine, sine).astype(jnp.bfloat16)
        out_ref[:, columns(2)] = matmul(input_ref[...], weight_ref[:, columns(2)]).astype(
            jnp.bfloat16
        )
        return carry

    lax.fori_loop(0, width // 256, one, 0)


def attend_pair(pair, width, heads_ref, bias_ref, same_ref, hidden_ref, out_ref, log_ref):
    def columns(part):
        return pl.ds(pl.multiple_of(part * width + pair * 128, 128), 128)

    query, key, value = (heads_ref[:, columns(part)] for part in range(3))
    total = None
    for which in (0, 1):
        head = 2 * pair + which
        gap = bias_ref[0, head] - bias_ref[1, head]
        scores = matmul(head_lanes(key, which), query, 1, 1)
        scores = scores + same_ref[...] * gap + hidden_ref[...]
        top = jnp.max(scores, axis=0, keepdims=True)
        weights = jnp.exp(scores - top)
        weight_sum = jnp.sum(weights, axis=0, keepdims=True)
        log_ref[pl.ds(head, 1), :] = top + jnp.log(weight_sum)
        soft = (weights * (1.0 / weight_sum)).astype(jnp.bfloat16)
        part = matmul(head_lanes(value, which), soft, 0, 0)
        total = part if total is None else total + part
    out_ref[:, pl.ds(pl.multiple_of(pair * 128, 128), 128)] = total.T.astype(jnp.bfloat16)


def normed(values):
    factor = lax.rsqrt(jnp.mean(values * values, axis=-1, keepdims=True) + epsilon)
    return values * factor, factor


def forward_body(refs, between=None):
    (
        arrived_ref, columns_ref, rows_ref, lengths_ref, bias_ref, gain_ref, weight_ref,
        cosine_ref, sine_ref,
        stream_ref, input_ref, heads_ref, out_ref, log_ref,
        same_ref, hidden_ref,
    ) = refs
    width = gain_ref.shape[1]
    scale = 1.0 / math.sqrt(64)
    chosen = pick_rows(columns_ref[:, 1:2], arrived_ref.shape[0])
    stream = matmul(chosen, arrived_ref[...])
    stream_ref[...] = stream.astype(jnp.bfloat16)
    input_ref[...] = (normed(stream)[0] * gain_ref[...]).astype(jnp.bfloat16)
    pair_masks(columns_ref, rows_ref, lengths_ref, same_ref, hidden_ref)
    project(input_ref, weight_ref, cosine_ref, sine_ref, heads_ref, scale)

    def one(pair, carry):
        if between is not None:
            between(pair)
        attend_pair(pair, width, heads_ref, bias_ref, same_ref, hidden_ref, out_ref, log_ref)
        return carry

    lax.fori_loop(0, width // 128, one, 0)


def forward_kernel(*refs):
    forward_body(refs)


def mlp_kernel(
    head_count, columns_ref, rows_ref, gain_ref, stream_ref, attended_ref, arrived_ref, out_w_ref,
    gate_ref, up_ref, down_ref,
    grad_gate_ref, grad_up_ref, grad_down_ref, packed_ref, dh_ref, grad_out_ref, do_ref, stats_ref,
    attn_ref, middle_ref, input_ref, input_t_ref, dy_ref, mlp_ref, back_ref,
):
    step = pl.program_id(0)
    final = pl.num_programs(0) - 1
    half = jnp.bfloat16

    @pl.when(step == 0)
    def _():
        attn_out = matmul(attended_ref[...], out_w_ref[...])
        attn_ref[...] = attn_out
        middle = stream_ref[...].astype(jnp.float32) + attn_out
        middle_ref[...] = middle
        entry = normed(middle)[0] * gain_ref[...]
        input_ref[...] = entry.astype(half)
        input_t_ref[...] = entry.T.astype(half)
        chosen = pick_rows(columns_ref[:, 1:2], arrived_ref.shape[0])
        dy_ref[...] = matmul(chosen, arrived_ref[...]).astype(half)
        mlp_ref[...] = jnp.zeros_like(mlp_ref)
        back_ref[...] = jnp.zeros_like(back_ref)

    gate = matmul(input_ref[...], gate_ref[...])
    up = matmul(input_ref[...], up_ref[...])
    grad_hidden = matmul(dy_ref[...], down_ref[...], 1, 1)
    sigmoid = jax.nn.sigmoid(gate)
    silu = gate * sigmoid
    hidden = (silu * up).astype(half)
    grad_gate = (grad_hidden * up * sigmoid * (1.0 + gate * (1.0 - sigmoid))).astype(half)
    grad_up = (grad_hidden * silu).astype(half)
    mlp_ref[...] += matmul(hidden, down_ref[...])
    back_ref[...] += matmul(grad_gate, gate_ref[...], 1, 1) + matmul(grad_up, up_ref[...], 1, 1)
    grad_gate_ref[...] = matmul(input_t_ref[...], grad_gate).astype(half)
    grad_up_ref[...] = matmul(input_t_ref[...], grad_up).astype(half)
    grad_down_ref[...] = matmul(hidden, dy_ref[...], 0, 0).astype(half)

    @pl.when(step == final)
    def _():
        valid = (columns_ref[:, 3:4] > 0).astype(jnp.float32)
        width = gain_ref.shape[1]

        def square(values, at):
            across = jnp.sum(values * values * valid, axis=0, keepdims=True)
            folded = across[:, 0:128]
            for i in range(1, width // 128):
                folded += across[:, i * 128 : (i + 1) * 128]
            stats_ref[at : at + 1, :] = folded

        stats_ref[...] = jnp.zeros_like(stats_ref)
        middle, mlp_out = middle_ref[...], mlp_ref[...]
        result = middle + mlp_out
        square(stream_ref[...].astype(jnp.float32), 8)
        square(attn_ref[...], 9)
        square(middle, 10)
        square(mlp_out, 11)
        square(result, 12)
        lane = lax.broadcasted_iota(jnp.int32, (valid.shape[0], 128), 1)
        stats_ref[13:14, :] = jnp.sum(jnp.where(lane == 0, valid, 0.0), axis=0, keepdims=True)
        placed = place_rows(rows_ref[1:2, :], packed_ref.shape[0])
        packed_ref[...] = matmul(placed, result.astype(half)).astype(half)
        entry, factor = normed(middle)
        back = back_ref[...]
        gain_grad = jnp.sum(back * entry, axis=0, keepdims=True)
        for i in range(width // 128):
            stats_ref[i : i + 1, :] = gain_grad[:, i * 128 : (i + 1) * 128]
        scaled = back * gain_ref[...]
        inner = jnp.mean(scaled * entry, axis=-1, keepdims=True)
        dh = dy_ref[...].astype(jnp.float32) + factor * (scaled - entry * inner)
        dh_ref[...] = dh
        branch = dh.astype(half)
        do_ref[...] = matmul(branch, out_w_ref[...], 1, 1).astype(half)
        grad_out_ref[...] = matmul(attended_ref[...], branch, 0, 0).astype(half)


def mlp_call(head_count, slot_total, inputs, weights):
    columns, rows, gain, stream, attended, arrived, out_w = inputs
    gate, up, down = weights
    tokens, width = stream.shape
    hidden = gate.shape[1]
    tile = 512

    def whole(array):
        return pl.BlockSpec(array.shape, lambda i: (0,) * len(array.shape))

    half, full = jnp.bfloat16, jnp.float32
    across = pl.BlockSpec((width, tile), lambda i: (0, i))
    down_spec = pl.BlockSpec((tile, width), lambda i: (i, 0))
    out_shape = [
        jax.ShapeDtypeStruct((width, hidden), half),
        jax.ShapeDtypeStruct((width, hidden), half),
        jax.ShapeDtypeStruct((hidden, width), half),
        jax.ShapeDtypeStruct((slot_total, width), half),
        jax.ShapeDtypeStruct((tokens, width), full),
        jax.ShapeDtypeStruct((width, width), half),
        jax.ShapeDtypeStruct((tokens, width), half),
        jax.ShapeDtypeStruct((16, 128), full),
    ]
    rest = [pl.BlockSpec(each.shape, lambda i: (0, 0)) for each in out_shape[3:]]
    flops = 2 * tokens * width * hidden * 9
    return pl.pallas_call(
        functools.partial(mlp_kernel, head_count),
        out_shape=out_shape,
        grid=(hidden // tile,),
        in_specs=[whole(each) for each in inputs] + [across, across, down_spec],
        out_specs=[across, across, down_spec, *rest],
        scratch_shapes=[
            pltpu.VMEM((tokens, width), full),
            pltpu.VMEM((tokens, width), full),
            pltpu.VMEM((tokens, width), half),
            pltpu.VMEM((width, tokens), half),
            pltpu.VMEM((tokens, width), half),
            pltpu.VMEM((tokens, width), full),
            pltpu.VMEM((tokens, width), full),
        ],
        compiler_params=pltpu.CompilerParams(vmem_limit_bytes=60 << 20),
        cost_estimate=pl.CostEstimate(
            flops=flops, bytes_accessed=6 * 2 * width * hidden, transcendentals=tokens * hidden
        ),
    )(*inputs, *weights)


def attend_back_pair(
    pair, width, scale, heads_ref, do_ref, bias_ref, log_ref, same_ref, hidden_ref, cosine_ref,
    sine_ref, grads_ref, bias_same_ref, bias_all_ref,
):
    half = jnp.bfloat16

    def columns(part):
        return pl.ds(pl.multiple_of(part * width + pair * 128, 128), 128)

    query, key, value = (heads_ref[:, columns(part)] for part in range(3))
    grad_out = do_ref[:, columns(0)]
    query_t = key_grad = value_grad = None
    for which in (0, 1):
        head = 2 * pair + which
        gap = bias_ref[0, head] - bias_ref[1, head]
        key_part = head_lanes(key, which)
        scores = matmul(key_part, query, 1, 1)
        scores = scores + same_ref[...] * gap + hidden_ref[...]
        soft = jnp.exp(scores - log_ref[pl.ds(head, 1), :])
        grad_soft = matmul(head_lanes(value, which), grad_out, 1, 1)
        inner = jnp.sum(soft * grad_soft, axis=0, keepdims=True)
        grad_scores = (soft * (grad_soft - inner)).astype(half)
        wide = grad_scores.astype(jnp.float32)
        bias_all_ref[pl.ds(head, 1), :] = jnp.sum(wide, axis=0, keepdims=True)
        bias_same_ref[pl.ds(head, 1), :] = jnp.sum(wide * same_ref[...], axis=0, keepdims=True)
        parts = (
            matmul(key_part, grad_scores, 0, 0),
            matmul(grad_scores, head_lanes(query, which)),
            matmul(soft.astype(half), head_lanes(grad_out, which)),
        )
        if which == 0:
            query_t, key_grad, value_grad = parts
        else:
            query_t, key_grad, value_grad = (
                query_t + parts[0],
                key_grad + parts[1],
                value_grad + parts[2],
            )
    cosine, sine = cosine_ref[...], -sine_ref[...]
    grads_ref[:, columns(0)] = (turn(query_t.T, cosine, sine) * scale).astype(half)
    grads_ref[:, columns(1)] = turn(key_grad, cosine, sine).astype(half)
    grads_ref[:, columns(2)] = value_grad.astype(half)


def backward_body(refs, between=None):
    (
        columns_ref, rows_ref, lengths_ref, bias_ref, gain_ref, weight_ref, cosine_ref, sine_ref,
        stream_ref, input_ref, heads_ref, log_ref, do_ref, dh_ref,
        grad_weight_ref, packed_ref, stats_ref,
        same_ref, hidden_ref, grads_ref, bias_same_ref, bias_all_ref, back_ref,
    ) = refs
    width = gain_ref.shape[1]
    half = jnp.bfloat16
    scale = 1.0 / math.sqrt(64)
    pair_masks(columns_ref, rows_ref, lengths_ref, same_ref, hidden_ref)

    def one(pair, carry):
        if between is not None:
            between(pair)
        attend_back_pair(
            pair, width, scale, heads_ref, do_ref, bias_ref, log_ref, same_ref, hidden_ref,
            cosine_ref, sine_ref, grads_ref, bias_same_ref, bias_all_ref,
        )
        return carry

    lax.fori_loop(0, width // 128, one, 0)
    back_ref[...] = jnp.zeros_like(back_ref)

    def combine(i, carry):
        at = pl.ds(pl.multiple_of(i * 512, 512), 512)
        part = grads_ref[:, at]
        back_ref[...] += matmul(part, weight_ref[:, at], 1, 1)
        grad_weight_ref[:, at] = matmul(input_ref[...], part, 0, 0).astype(half)
        return carry

    lax.fori_loop(0, 3 * width // 512, combine, 0)
    back = back_ref[...]
    entry, factor = normed(stream_ref[...].astype(jnp.float32))
    gain_grad = jnp.sum(back * entry, axis=0, keepdims=True)
    stats_ref[...] = jnp.zeros_like(stats_ref)
    for i in range(width // 128):
        stats_ref[i : i + 1, :] = gain_grad[:, i * 128 : (i + 1) * 128]
    heads = bias_all_ref.shape[0]
    lane = lax.broadcasted_iota(jnp.int32, (heads, 128), 1)
    row = lax.broadcasted_iota(jnp.int32, (heads, 128), 0)
    same = jnp.sum(bias_same_ref[...], axis=1, keepdims=True)
    other = jnp.sum(bias_all_ref[...], axis=1, keepdims=True) - same
    stats_ref[8:9, :] = jnp.sum(
        jnp.where(lane == row, same, 0.0) + jnp.where(lane == row + heads, other, 0.0),
        axis=0,
        keepdims=True,
    )
    scaled = back * gain_ref[...]
    inner = jnp.mean(scaled * entry, axis=-1, keepdims=True)
    grad_stream = dh_ref[...] + factor * (scaled - entry * inner)
    placed = place_rows(rows_ref[1:2, :], packed_ref.shape[0])
    packed_ref[...] = matmul(placed, grad_stream.astype(half)).astype(half)


def backward_kernel(*refs):
    backward_body(refs)


def forward_gather_kernel(shards, lents, swap_count, compute_counts, *refs):
    ins, outs = compute_counts
    total = len(lents) + swap_count
    in_refs, refs = refs[: ins + total], refs[ins + total :]
    out_refs, refs = refs[: outs + total], refs[outs + total :]
    masks, scratch = refs[:2], refs[2:]
    work = GatherAll(
        Spot(shards), lents, swap_count, in_refs[ins:], out_refs[outs:], scratch
    )
    work.start()
    pairs = in_refs[5].shape[1] // 128
    forward_body(
        (*in_refs[:ins], *out_refs[:outs], *masks), lambda pair: work.steps(pair, pairs)
    )
    work.finish()


def forward_gather_call(shards, inputs, spaces, out_shape, pieces, lents, sent, collective_id):
    anywhere = pl.BlockSpec(memory_space=pl.ANY)
    inside = pl.BlockSpec(memory_space=pltpu.VMEM)
    tokens = out_shape[0].shape[0]
    counts = (len(inputs), len(out_shape))
    comm = len(pieces) + len(sent)
    results = pl.pallas_call(
        functools.partial(forward_gather_kernel, shards, lents, len(sent), counts),
        out_shape=[*out_shape, *gather_shapes(shards, pieces, sent, [])],
        in_specs=spaces + [anywhere] * comm,
        out_specs=[inside] * len(out_shape) + [anywhere] * comm,
        scratch_shapes=[pltpu.VMEM((tokens, tokens), jnp.float32)] * 2
        + GatherAll.scratch(shards, len(pieces), len(sent)),
        compiler_params=pltpu.CompilerParams(
            collective_id=collective_id, has_side_effects=True, vmem_limit_bytes=56 << 20
        ),
    )(*inputs, *pieces, *sent)
    first = len(out_shape)
    second = first + len(pieces)
    return results[:first], results[first:second], results[second:]


def on_device(
    tokens,
    cotangent,
    send_slot,
    recv_slot,
    lengths,
    variate,
    valid_mask,
    norm_attn,
    w_query,
    w_key,
    w_value,
    w_out,
    variate_bias,
    norm_mlp,
    w_gate,
    w_up,
    w_down,
):
    shards = lax.axis_size("shard")
    tok_rows, width = tokens.shape
    slot_total = 2 * tok_rows
    heads = variate_bias.shape[1]
    half, full = jnp.bfloat16, jnp.float32
    share = width // shards
    indices = jnp.stack([send_slot, recv_slot, variate, valid_mask])
    rows = jnp.concatenate([indices, jnp.zeros_like(indices)])
    columns = rows.T
    _, position = layout(lengths[0], tok_rows)
    cosine, sine = angle_tables(position, width // heads)
    cosine = jnp.concatenate([cosine] * 4, axis=1)
    sine = jnp.concatenate([-sine, sine] * 2, axis=1)
    gains = jnp.stack([norm_attn, norm_mlp]).astype(full)
    gains = jnp.pad(gains, ((0, 6), (0, 128 - share)))
    shape = jax.ShapeDtypeStruct
    packed_shape = shape((slot_total, width), half)
    token_shape = shape((tok_rows, width), half)
    out_tokens, out_cotangent = local_call(
        pack_kernel, [packed_shape] * 2, [rows, tokens, cotangent]
    )
    (full_in,), (arrived_tokens,), (gains,) = gather_call(
        shards,
        [jnp.concatenate([w_query, w_key, w_value], axis=1)],
        (4,),
        [out_tokens],
        [gains],
        1,
    )
    gains = gains.reshape(shards, 8, 128)
    gain_attn = gains[:, 0, :share].reshape(1, width)
    gain_mlp = gains[:, 1, :share].reshape(1, width)
    inside = pl.BlockSpec(memory_space=pltpu.VMEM)
    scalar = pl.BlockSpec(memory_space=pltpu.SMEM)
    (
        (stream, input_attn, head_rows, attended, logs),
        (full_out, full_gate, full_up, full_down),
        (arrived_grads,),
    ) = forward_gather_call(
        shards,
        [
            arrived_tokens, columns, rows, lengths, variate_bias, gain_attn, full_in, cosine, sine,
        ],
        [inside] * 3 + [scalar] * 2 + [inside] * 4,
        [
            token_shape,
            token_shape,
            shape((tok_rows, 3 * width), half),
            token_shape,
            shape((heads, tok_rows), full),
        ],
        [w_out, w_gate, w_up, w_down],
        (2, 4, 4, 2),
        [out_cotangent],
        2,
    )
    part_gate, part_up, part_down, home_out, grad_middle, part_out, grad_attended, stats_mlp = (
        mlp_call(
            heads,
            slot_total,
            [columns, rows, gain_mlp, stream, attended, arrived_grads, full_out],
            [full_gate, full_up, full_down],
        )
    )
    part_in, home_grad, stats_attn = local_call(
        backward_kernel,
        [shape((width, 3 * width), half), packed_shape, shape((16, 128), full)],
        [
            columns, rows, lengths, variate_bias, gain_attn, full_in, cosine, sine,
            stream, input_attn, head_rows, logs, grad_attended, grad_middle,
        ],
        [inside] * 2 + [scalar] * 2 + [inside] * 10,
        [
            pltpu.VMEM((tok_rows, tok_rows), full),
            pltpu.VMEM((tok_rows, tok_rows), full),
            pltpu.VMEM((tok_rows, 3 * width), half),
            pltpu.VMEM((heads, tok_rows), full),
            pltpu.VMEM((heads, tok_rows), full),
            pltpu.VMEM((tok_rows, width), full),
        ],
    )
    (grad_gate, grad_up, grad_down, grad_out), (home_out,), _ = reduce_call(
        shards, [part_gate, part_up, part_down, part_out], [home_out], [], 3
    )
    (grad_in,), (home_grad,), (sums,) = reduce_call(
        shards, [part_in], [home_grad], [jnp.concatenate([stats_mlp, stats_attn])], 4
    )
    output, input_grad = local_call(
        unpack_kernel, [token_shape] * 2, [columns, home_out, home_grad]
    )
    squares = jnp.sum(sums[8:14], axis=1)
    root_means = jnp.sqrt(squares[:5] / (squares[5] * width))
    share_start = lax.axis_index("shard") * share
    grad_norm_mlp = lax.dynamic_slice_in_dim(sums[0:8].reshape(-1), share_start, share)
    grad_norm_attn = lax.dynamic_slice_in_dim(sums[16:24].reshape(-1), share_start, share)
    bias_grads = sums[24, : 2 * heads].reshape(2, heads)
    grad_query, grad_key, grad_value = (grad_in[:, i * width : (i + 1) * width] for i in range(3))
    return (
        output,
        input_grad,
        grad_norm_attn,
        grad_query,
        grad_key,
        grad_value,
        grad_out,
        bias_grads,
        grad_norm_mlp,
        grad_gate,
        grad_up,
        grad_down,
        root_means,
    )


def solution(mesh):
    in_specs = (
        P(("rep", "shard"), None),
        P(("rep", "shard"), None),
        P(("rep", "shard")),
        P(("rep", "shard")),
        P(("rep", "shard"), None),
        P(("rep", "shard")),
        P(("rep", "shard")),
        P("shard"),
        P("shard", None),
        P("shard", None),
        P("shard", None),
        P("shard", None),
        P(),
        P("shard"),
        P("shard", None),
        P("shard", None),
        P("shard", None),
    )
    out_specs = (
        P(("rep", "shard"), None),
        P(("rep", "shard"), None),
        P("shard"),
        P("shard", None),
        P("shard", None),
        P("shard", None),
        P("shard", None),
        P(),
        P("shard"),
        P("shard", None),
        P("shard", None),
        P("shard", None),
        P(),
    )
    return jax.shard_map(
        on_device, mesh=mesh, in_specs=in_specs, out_specs=out_specs, check_vma=False
    )
```

time: 819 us -> 637 us (0.78)
  matrix products: 158 us -> 0 us
  Pallas kernels: 513 us -> 610 us
  local copies, waits for them, and re-layouts: 58.9 us -> 10.7 us
  other arithmetic: 50.9 us -> 7.95 us
  blocking collectives: 25.5 us -> 0 us
    dot_general x43 -> x0, matrix products: 158 us -> none  [the longest x7 40.9 us: contract_cols(): lax.dot_general(left, right, (((1,), (1,)), ((), ())), preferred_element_...]
    pallas_call x2 -> x6, Pallas kernels: 247 us -> 337 us  [the longest x1 149 us: forward_gather_call(): pl.pallas_call(functools.partial(forward_gather_kernel, shards, lents, le...]
    unnamed x1 -> x0, blocking collectives: 25.5 us -> none
    gather x4 -> x0, local copies, waits for them, and re-layouts: 19.2 us -> none  [the longest x1 5.33 us: on_device(): grad_out_rows = jnp.take(arrived_grads, recv_slot, axis=0)]
    reduce_sum x7 -> x1, other arithmetic: 18.5 us -> 0.79 us  [on_device(): squares = jnp.sum(sums[8:14], axis=1)]
    unnamed x134 -> x38, local copies, waits for them, and re-layouts: 17.2 us -> 3.69 us
    scatter x2 -> x0, other arithmetic: 11.1 us -> none  [deal_buffer(): jnp.zeros((slot_total, rows_in.shape[1]), rows_in.dtype).at[slot_ids]]
    scatter x2 -> x0, local copies, waits for them, and re-layouts: 9.57 us -> none  [deal_buffer(): jnp.zeros((slot_total, rows_in.shape[1]), rows_in.dtype).at[slot_ids]]
where the time goes in v2:
time: 637 us; the launch traced here: 631 us
  Pallas kernels  610 us (96%)
  local copies, waits for them, and re-layouts  10.7 us (2%)
  other arithmetic  7.95 us (1%)
    pallas_call x2, Pallas kernels, reduce_call(): pl.pallas_call(functools.partial(reduce_kernel, shards, len(partials), le...  273 us
    pallas_call x1, Pallas kernels, forward_gather_call(): pl.pallas_call(functools.partial(forward_gather_kernel, shards, lents, le...  149 us
    pallas_call x1, Pallas kernels, gather_call(): pl.pallas_call(functools.partial(gather_kernel, shards, lents, len(swaps)...  82.8 us
    pallas_call x1, Pallas kernels, mlp_call(): pl.pallas_call(functools.partial(mlp_kernel, head_count), out_shape=out_s...  58.9 us
    pallas_call x3, Pallas kernels, local_call(): pl.pallas_call(kernel, out_shape=out_shape, in_specs=spaces or [inside] *...  46.5 us

profile of v2, /device:TPU:8, one launch (start us, length us, event | category | flops | bytes accessed | tf_op | source)
XLA Modules:
  0.0 630.6 jit_solution(7828769763298552271)
XLA Ops:
  0.7 0.8 reduce-window.4
  1.6 0.7 fusion.8
  2.4 1.0 fusion
  3.4 1.3 pad_maximum_fusion.1
  5.4 5.2 shard_map.264
  10.6 0.8 pad_maximum_fusion.refs_0_
  12.0 82.8 %shard_map.265 = (bf16[1024,3072]{1,0:T(8,128)(2,1)}, bf16[1024,1024]{1,0:T(8,128)(2,1)}, f32[128,128]{1,0:T(8,128)}) custom-call(bf16[64,3072]{1,0:T(8,128)(2,1)} %pad_maximum_fusion.refs_0_, bf16[1024,1024]{1,0:T(8,128)(2,1)} %get-tuple-element.49.refs_1_, f32[8,128]{1,0:T(8,128)} %fusion.7.refs_2_), custom_call_target="tpu_custom_call" | custom-call | tf_op jit(solution)/shard_map/pallas_call | solution.py:351
  94.8 0.9 fusion.10
  95.7 0.7 reshape_squeeze.10.refs_5_.refs_4_
  96.4 0.8 copy.52
  97.2 149.0 %shard_map.266 = (bf16[512,1024]{1,0:T(8,128)(2,1)}, bf16[512,1024]{1,0:T(8,128)(2,1)}, bf16[512,3072]{1,0:T(8,128)(2,1)}, bf16[512,1024]{1,0:T(8,128)(2,1)}, f3...) custom-call(bf16[1024,1024]{1,0:T(8,128)(2,1)} %get-tuple-element.51, ...), custom_call_target="tpu_custom_call" | custom-call | tf_op jit(solution)/shard_map/pallas_call | solution.py:1157
  246.2 0.7 reshape_squeeze.9.gain_ref
  246.9 58.9 %shard_map.267 = (bf16[1024,4096]{1,0:T(8,128)(2,1)}, bf16[1024,4096]{1,0:T(8,128)(2,1)}, bf16[4096,1024]{1,0:T(8,128)(2,1)}, bf16[1024,1024]{1,0:T(8,128)(2,1)}...) custom-call(s32[512,8]{1,0:T(8,128)} %bitcast.28, ...), custom_call_target="tpu_custom_call" | custom-call | flops 38654705664 | bytes 50331648 | tf_op jit(solution)/shard_map/pallas_call | solution.py:1009
  305.8 35.5 %shard_map.269 = (bf16[1024,3072]{1,0:T(8,128)(2,1)}, bf16[1024,1024]{1,0:T(8,128)(2,1)}, f32[16,128]{1,0:T(8,128)}) custom-call(s32[512,8]{1,0:T(8,128)} %bitcast.29, s32[8,512]{1,0:T(8,128)} %concatenate.15.rows_ref.refs_2_.refs_1_, s32[1,4]{1,0:T(1,128)} %refs_2_.1, f32[2,16]{1,0:T(2,128)} %refs_3_.3, f32[1,1024]{1,0:T(1,128)} %reshape_squeeze.10.refs_5_.refs_4_, ...), custom_call_target="tpu_custom_call" | custom-call | tf_op jit(solution)/shard_map/pallas_call | solution.py:784
  341.4 1.3 pad_maximum_fusion.3.refs_2_
  342.7 96.2 %shard_map.270 = (f32[64,3072]{1,0:T(8,128)}, bf16[1024,1024]{1,0:T(8,128)(2,1)}, f32[32,128]{1,0:T(8,128)}) custom-call(bf16[1024,3072]{1,0:T(8,128)(2,1)} %get-tuple-element.72.refs_0_, bf16[1024,1024]{1,0:T(8,128)(2,1)} %get-tuple-element.73.refs_1_, f32[32,128]{1,0:T(8,128)} %pad_maximum_fusion.3.refs_2_), custom_call_target="tpu_custom_call" | custom-call | tf_op jit(solution)/shard_map/pallas_call | solution.py:740
  438.9 0.8 slice_reduce_fusion
  441.4 177.0 %shard_map.268 = (f32[64,4096]{1,0:T(8,128)}, f32[64,4096]{1,0:T(8,128)}, f32[256,1024]{1,0:T(8,128)}, f32[64,1024]{1,0:T(8,128)}, bf16[1024,1024]{1,0:T(8,128)(2,1)}) custom-call(bf16[1024,4096]{1,0:T(8,128)(2,1)} %get-tuple-element.61.refs_0_, bf16[1024,4096]{1,0:T(8,128)(2,1)} %get-tuple-element.62.refs_1_, bf16[4096,1024]{1,0:T(8,128)(2,1)} %get-tuple-element.63.refs_2_, ...), custom_call_target="tpu_custom_call" | custom-call | tf_op jit(solution)/shard_map/pallas_call | solution.py:740
  618.5 5.7 shard_map.271
  624.2 0.9 fusion.9
  626.9 0.7 copy.62
  627.7 1.0 copy.63
  628.6 1.0 copy.64
  629.6 1.0 copy.65
  (48 shorter events, 4.4 us)
Async XLA Ops:
  0.6 4.1 copy-start.11
  0.7 4.1 copy-start.12
  0.7 4.1 copy-start.13
  0.7 4.1 copy-start.14
  2.4 8.2 %copy-start.6 = (bf16[64,1024]{1,0:T(8,128)(2,1)S(1)}, bf16[64,1024]{1,0:T(8,128)(2,1)}, u32[]{:S(2)}) copy-start(bf16[64,1024]{1,0:T(8,128)(2,1)} %param.27) | copy-start | bytes 393220
  2.4 8.2 %copy-start.7 = (bf16[64,1024]{1,0:T(8,128)(2,1)S(1)}, bf16[64,1024]{1,0:T(8,128)(2,1)}, u32[]{:S(2)}) copy-start(bf16[64,1024]{1,0:T(8,128)(2,1)} %param.26) | copy-start | bytes 393220
  2.4 8.2 %copy-start.8 = (bf16[64,1024]{1,0:T(8,128)(2,1)S(1)}, bf16[64,1024]{1,0:T(8,128)(2,1)}, u32[]{:S(2)}) copy-start(bf16[64,1024]{1,0:T(8,128)(2,1)} %param.25) | copy-start | bytes 393220
  3.4 8.0 %copy-start.15 = (bf16[64]{0:T(256)(128)(2,1)S(1)}, bf16[64]{0:T(256)(128)(2,1)}, u32[]{:S(2)}) copy-start(bf16[64]{0:T(256)(128)(2,1)} %param.30) | copy-start | bytes 388
  3.4 8.0 %copy-start.16 = (bf16[64]{0:T(256)(128)(2,1)S(1)}, bf16[64]{0:T(256)(128)(2,1)}, u32[]{:S(2)}) copy-start(bf16[64]{0:T(256)(128)(2,1)} %param.24) | copy-start | bytes 388
  10.6 85.8 %copy-start.4 = (s32[8,512]{1,0:T(8,128)S(1)}, s32[8,512]{1,0:T(8,128)}, u32[]{:S(2)}) copy-start(s32[8,512]{1,0:T(8,128)} %concatenate.15.rows_ref.refs_2_.refs_1_) | copy-start | bytes 49156
  305.8 35.6 %copy-start.10 = (f32[16,128]{1,0:T(8,128)S(1)}, f32[16,128]{1,0:T(8,128)}, u32[]{:S(2)}) copy-start(f32[16,128]{1,0:T(8,128)} %get-tuple-element.74) | copy-start | bytes 24580
  618.4 5.8 copy-start.3
  618.4 6.7 %copy-start.9 = (f32[32,128]{1,0:T(8,128)S(1)}, f32[32,128]{1,0:T(8,128)}, u32[]{:S(2)}) copy-start(f32[32,128]{1,0:T(8,128)} %get-tuple-element.79) | copy-start | bytes 49156
  618.5 8.5 %copy-start.5 = (f32[64,1024]{1,0:T(8,128)S(1)}, f32[64,1024]{1,0:T(8,128)}, u32[]{:S(2)}) copy-start(f32[64,1024]{1,0:T(8,128)} %get-tuple-element.116) | copy-start | bytes 786436
  624.2 3.5 copy-start.2
  624.2 4.4 copy-start.1
  627.7 1.9 copy-start

commit v3 on v2

v3 whole, which is shorter than its diff:
```python
import functools
import math

import jax
import jax.numpy as jnp
from jax import lax
from jax.experimental import pallas as pl
from jax.experimental.pallas import tpu as pltpu
from jax.sharding import PartitionSpec as P

MESH = pl.DeviceIdType.MESH
DMA = pltpu.SemaphoreType.DMA
epsilon = 1e-06
masked_score = -1e30
VMEM_LIMIT = 62 << 20


def angle_tables(position, head_dim):
    half_dim = head_dim // 2
    inverse_freq = 1.0 / 10000.0 ** (jnp.arange(half_dim, dtype=jnp.float32) / half_dim)
    theta_angle = position.astype(jnp.float32)[:, None] * inverse_freq[None, :]
    return (jnp.cos(theta_angle), jnp.sin(theta_angle))


def layout(lengths_row, tok_rows):
    slot_ids = jnp.arange(tok_rows, dtype=jnp.int32)
    seq_ends = jnp.cumsum(lengths_row)
    segment = jnp.sum((slot_ids[:, None] >= seq_ends[None, :]).astype(jnp.int32), axis=1)
    starts = seq_ends - lengths_row
    chosen = segment[:, None] == jnp.arange(lengths_row.shape[0], dtype=jnp.int32)[None, :]
    begins = jnp.sum(jnp.where(chosen, starts[None, :], 0), axis=1)
    return (segment, slot_ids - begins)


def ring_place(chip, chips):
    return jnp.where(chip % 2 == 0, chip // 2, chips - 1 - chip // 2)


def ring_chip(place, chips):
    wrapped = lax.rem(place + 2 * chips, chips)
    return jnp.where(wrapped < chips // 2, 2 * wrapped, 2 * (chips - 1 - wrapped) + 1)


class Spot:
    def __init__(self, shards):
        self.shards = shards
        self.chips = shards // 2
        self.half = self.chips // 2
        self.rep = lax.axis_index("rep")
        self.shard = lax.axis_index("shard")
        self.core = lax.rem(self.shard, 2)
        self.place = ring_place(self.shard // 2, self.chips)
        self.sibling = self.shard + 1 - 2 * self.core

    def block(self, place, core=None):
        return 2 * ring_chip(place, self.chips) + (self.core if core is None else core)

    def along(self, way, distance):
        return self.place - distance if way == 0 else self.place + distance

    def ahead(self, way):
        return (self.rep, self.block(self.along(way, -1)))


def greet(spot):
    barrier = pltpu.get_barrier_semaphore()

    def peer(k, carry):
        target = lax.rem(spot.shard + k, spot.shards)
        pl.semaphore_signal(barrier, inc=1, device_id=(spot.rep, target), device_id_type=MESH)
        return carry

    lax.fori_loop(1, spot.shards, peer, 0)
    pl.semaphore_signal(
        barrier, inc=1, device_id=(1 - spot.rep, spot.shard), device_id_type=MESH
    )
    pl.semaphore_wait(barrier, spot.shards)


def remote(src, dst, sems, at, target):
    return pltpu.make_async_remote_copy(
        src_ref=src,
        dst_ref=dst,
        send_sem=sems[0].at[at],
        recv_sem=sems[1].at[at],
        device_id=target,
        device_id_type=MESH,
    )


class Swap:
    def __init__(self, spot, source, arrived, sems, own_sem):
        self.spot, self.sems = spot, sems
        self.source, self.arrived = source, arrived
        self.capacity = arrived.shape[0] // spot.shards
        self.own = pltpu.make_async_copy(
            self.part(spot.shard), arrived.at[self.rows(spot.shard)], own_sem
        )

    def rows(self, shard):
        return pl.ds(pl.multiple_of(shard * self.capacity, 8), self.capacity)

    def part(self, shard):
        if self.source.shape[0] == self.capacity:
            return self.source
        return self.source.at[self.rows(shard)]

    def copy(self, k):
        spot = self.spot
        target = lax.rem(spot.shard + k, spot.shards)
        return remote(
            self.part(target),
            self.arrived.at[self.rows(spot.shard)],
            self.sems,
            (k,),
            (spot.rep, target),
        )

    def start(self, slot, slots):
        size = -(-self.spot.shards // slots)

        def one(k, carry):
            @pl.when(k == 0)
            def _():
                self.own.start()

            @pl.when(k > 0)
            def _():
                self.copy(k).start()

            return carry

        first = jnp.minimum(slot * size, self.spot.shards)
        lax.fori_loop(first, jnp.minimum(first + size, self.spot.shards), one, 0)

    def finish(self):
        def one(k, carry):
            self.copy(k).wait()
            return carry

        lax.fori_loop(1, self.spot.shards, one, 0)
        self.own.wait()


class Gather:
    def __init__(self, spot, lent, shard_ref, full_ref, sems):
        self.spot, self.lent, self.shard_ref, self.full_ref = spot, lent, shard_ref, full_ref
        self.rows = shard_ref.shape[0]
        self.unit = shard_ref.shape[1] // 8
        self.kept = 8 - lent
        self.ring_sems, self.near_sems, self.far_sems, self.far_near_sems = (
            sems[0:2],
            sems[2:4],
            sems[4:6],
            sems[6:8],
        )
        self.whole_sems, self.own_sem = sems[8:10], sems[10]

    def span(self, way, short):
        first, count = self.lent * self.spot.rep, self.kept
        if short:
            first, count = first + way * (count // 2), count // 2
        return pl.ds(pl.multiple_of(first * self.unit, 128), count * self.unit)

    def region(self, way, hop, short):
        block = self.spot.block(self.spot.along(way, hop))
        return self.full_ref.at[pl.ds(block * self.rows, self.rows), self.span(way, short)]

    def ring(self, way, hop, short, source=None):
        region = self.region(way, hop, short)
        return remote(
            region if source is None else source,
            region,
            self.ring_sems,
            (way, hop),
            self.spot.ahead(way),
        )

    def near(self, way, hop, short):
        region = self.region(way, hop + 1, short)
        target = (self.spot.rep, self.spot.sibling)
        return remote(region, region, self.near_sems, (way, hop), target)

    def lent_region(self, way, hop, owner):
        block = self.spot.block(self.spot.along(way, hop + 1))
        columns = pl.ds(
            pl.multiple_of(self.kept * owner * self.unit, 128), self.lent * self.unit
        )
        return self.full_ref.at[pl.ds(block * self.rows, self.rows), columns]

    def far(self, way, hop):
        region = self.lent_region(way, hop, self.spot.rep)
        target = (1 - self.spot.rep, self.spot.shard)
        return remote(region, region, self.far_sems, (way, hop), target)

    def far_near(self, way, hop):
        region = self.lent_region(way, hop, 1 - self.spot.rep)
        target = (self.spot.rep, self.spot.sibling)
        return remote(region, region, self.far_near_sems, (way, hop), target)

    def own(self):
        spot = self.spot
        mine = self.full_ref.at[pl.ds(spot.shard * self.rows, self.rows)]
        whole = remote(self.shard_ref, mine, self.whole_sems, (0,), (spot.rep, spot.sibling))
        return whole, pltpu.make_async_copy(self.shard_ref, mine, self.own_sem)

    def start(self):
        for way in (0, 1):
            self.ring(way, 0, False, self.shard_ref.at[:, self.span(way, False)]).start()
        for copy in self.own():
            copy.start()

    def step(self, hop):
        final = self.spot.half - 1

        @pl.when(hop < final)
        def _():
            for way in (0, 1):
                self.ring(way, hop, False).wait_recv()

                @pl.when(hop < final - 1)
                def _():
                    self.ring(way, hop + 1, False).start()

                @pl.when(hop == final - 1)
                def _():
                    self.ring(way, hop + 1, True).start()

            for way in (0, 1):
                self.far(way, hop).start()
                self.near(way, hop, False).start()

        @pl.when(hop == final)
        def _():
            for way in (0, 1):
                self.ring(way, hop, True).wait_recv()
            self.far(0, hop).start()
            for way in (0, 1):
                self.near(way, hop, True).start()

        @pl.when(hop > 0)
        def _():
            for way in (0, 1):
                self.relay(way, hop - 1)

    def relay(self, way, hop):
        self.far(way, hop).wait_recv()
        self.far_near(way, hop).start()

    def finish(self):
        final = self.spot.half - 1
        for copy in self.own():
            copy.wait()

        def one(hop, carry):
            for way in (0, 1):
                self.ring(way, hop, False).wait_send()
                self.near(way, hop, False).wait()
                self.far(way, hop).wait_send()
                self.far_near(way, hop).wait()
            return carry

        lax.fori_loop(0, final, one, 0)
        for way in (0, 1):
            self.ring(way, final, True).wait_send()
            self.near(way, final, True).wait()
        self.far(0, final).wait_send()
        self.far_near(0, final).wait()

    @staticmethod
    def scratch(half):
        return [DMA((2, half))] * 8 + [DMA((1,))] * 2 + [DMA]


class GatherAll:
    def __init__(self, spot, lents, swap_count, inputs, outputs, scratch):
        count = len(lents)
        self.spot = spot
        self.gathers = [
            Gather(spot, lents[g], inputs[g], outputs[g], scratch[11 * g : 11 * g + 11])
            for g in range(count)
        ]
        scratch = scratch[11 * count :]
        self.swaps = [
            Swap(
                spot,
                inputs[count + i],
                outputs[count + i],
                scratch[3 * i : 3 * i + 2],
                scratch[3 * i + 2],
            )
            for i in range(swap_count)
        ]

    def start(self):
        greet(self.spot)
        for gather in self.gathers:
            gather.start()

    def step(self, hop):
        for swap in self.swaps:
            swap.start(hop, self.spot.half)
        for gather in self.gathers:
            gather.step(hop)

    def steps(self, slot, slots):
        size = -(-self.spot.half // slots)

        def one(hop, carry):
            self.step(hop)
            return carry

        first = jnp.minimum(slot * size, self.spot.half)
        lax.fori_loop(first, jnp.minimum(first + size, self.spot.half), one, 0)

    def finish(self):
        for gather in self.gathers:
            gather.relay(0, self.spot.half - 1)
        for each in self.gathers + self.swaps:
            each.finish()

    @staticmethod
    def scratch(shards, count, swap_count):
        return Gather.scratch(shards // 4) * count + [
            DMA((shards,)),
            DMA((shards,)),
            DMA,
        ] * swap_count


def gather_kernel(shards, lents, swap_count, *refs):
    spot = Spot(shards)
    total = len(lents) + swap_count
    work = GatherAll(
        spot, lents, swap_count, refs[:total], refs[total : 2 * total], refs[2 * total :]
    )
    work.start()
    work.steps(0, 1)
    work.finish()


def gather_shapes(shards, pieces, sent, shared):
    return (
        [
            jax.ShapeDtypeStruct((shards * piece.shape[0], piece.shape[1]), piece.dtype)
            for piece in pieces
        ]
        + [jax.ShapeDtypeStruct(rows.shape, rows.dtype) for rows in sent]
        + [
            jax.ShapeDtypeStruct((shards * each.shape[0], each.shape[1]), each.dtype)
            for each in shared
        ]
    )


def gather_call(shards, pieces, lents, sent, shared, collective_id):
    swaps = [*sent, *shared]
    anywhere = pl.BlockSpec(memory_space=pl.ANY)
    results = pl.pallas_call(
        functools.partial(gather_kernel, shards, lents, len(swaps)),
        out_shape=gather_shapes(shards, pieces, sent, shared),
        in_specs=[anywhere] * (len(pieces) + len(swaps)),
        out_specs=[anywhere] * (len(pieces) + len(swaps)),
        scratch_shapes=GatherAll.scratch(shards, len(pieces), len(swaps)),
        compiler_params=pltpu.CompilerParams(
            collective_id=collective_id, has_side_effects=True
        ),
    )(*pieces, *swaps)
    first, second = len(pieces), len(pieces) + len(sent)
    return results[:first], results[first:second], results[second:]


class Reduce:
    def __init__(self, spot, lent, partial_ref, out_ref, refs):
        self.spot, self.lent, self.partial, self.out = spot, lent, partial_ref, out_ref
        self.rows, self.columns = out_ref.shape
        self.unit = self.columns // 8
        self.kept = 8 - lent
        self.width = self.kept * self.unit
        (
            self.own,
            self.sib,
            self.got,
            self.own_far,
            self.sib_far,
            self.got_far,
            self.got_last,
        ) = refs[:7]
        sems = refs[7:]
        self.load_sem, self.load_far_sem = sems[0], sems[1]
        self.sib_sems, self.sib_far_sems = sems[2:4], sems[4:6]
        self.ring_sems, self.far_sems, self.last_sems = sems[6:8], sems[8:10], sems[10:12]

    @staticmethod
    def scratch(shards, lent, rows, columns):
        chips = shards // 2
        unit = columns // 8
        kept, lend = (8 - lent) * unit, lent * unit
        half = jnp.bfloat16
        buffers = [
            pltpu.VMEM((chips, rows, kept), half),
            pltpu.VMEM((chips, rows, kept), half),
            pltpu.VMEM((2, chips // 2, rows, kept), half),
            pltpu.VMEM((chips, rows, lend), half),
            pltpu.VMEM((chips, rows, lend), half),
            pltpu.VMEM((chips, rows, lend), half),
            pltpu.VMEM((rows, kept), half),
        ]
        sems = [DMA((chips,))] * 6 + [DMA((2, chips // 2))] * 2
        sems += [DMA((chips,))] * 2 + [DMA((1,))] * 2
        return buffers + sems

    def owner(self, item, core):
        half = self.spot.half
        pair = (item + 1) // 2
        ahead = lax.rem(item, 2) == 1
        distance = half - pair
        place = jnp.where(ahead, self.spot.place + distance, self.spot.place - distance)
        return self.spot.block(place, core)

    def cut(self, item, core, first, count):
        columns = pl.ds(pl.multiple_of(first * self.unit, 128), count * self.unit)
        block = self.owner(item, core)
        return self.partial.at[pl.ds(block * self.rows, self.rows), columns]

    def kept_cut(self, item, core):
        return self.cut(item, core, self.lent * self.spot.rep, self.kept)

    def lent_cut(self, item, core):
        return self.cut(item, core, self.kept * (1 - self.spot.rep), self.lent)

    def load(self, item):
        source = self.kept_cut(item, self.spot.core)
        return pltpu.make_async_copy(source, self.own.at[item], self.load_sem.at[item])

    def load_far(self, item):
        source = self.lent_cut(item, self.spot.core)
        return pltpu.make_async_copy(source, self.own_far.at[item], self.load_far_sem.at[item])

    def give(self, item):
        source = self.kept_cut(item, 1 - self.spot.core)
        target = (self.spot.rep, self.spot.sibling)
        return remote(source, self.sib.at[item], self.sib_sems, (item,), target)

    def give_far(self, item):
        source = self.lent_cut(item, 1 - self.spot.core)
        target = (self.spot.rep, self.spot.sibling)
        return remote(source, self.sib_far.at[item], self.sib_far_sems, (item,), target)

    def ring(self, way, step, short=False):
        item = 0 if short else 2 * step - 1 + way
        columns = pl.ds(way * self.width // 2, self.width // 2) if short else slice(None)
        return remote(
            self.own.at[item, :, columns],
            self.got.at[way, step, :, columns],
            self.ring_sems,
            (way, step),
            self.spot.ahead(way),
        )

    def far(self, item):
        target = (1 - self.spot.rep, self.spot.shard)
        return remote(
            self.own_far.at[item], self.got_far.at[item], self.far_sems, (item,), target
        )

    def last(self):
        target = (1 - self.spot.rep, self.spot.shard)
        source = self.own.at[self.spot.chips - 1]
        return remote(source, self.got_last, self.last_sems, (0,), target)

    def start(self, item):
        self.load_far(item).start()
        self.give_far(item).start()
        self.load(item).start()
        self.give(item).start()

    def tiles(self, width, body):
        chunk = width if width <= 768 else 512

        def one(tile, carry):
            for first in range(0, width, chunk):
                body(pl.ds(pl.multiple_of(tile * 16, 16), 16), first, chunk)
            return carry

        lax.fori_loop(0, self.rows // 16, one, 0)

    def far_step(self, item):
        self.load_far(item).wait()
        self.give_far(item).wait_recv()

        def add(rows, first, count):
            at = pl.ds(first, count)
            total = self.own_far[item, rows, at].astype(jnp.float32)
            total += self.sib_far[item, rows, at].astype(jnp.float32)
            self.own_far[item, rows, at] = total.astype(jnp.bfloat16)

        self.tiles(self.lent * self.unit, add)
        self.far(item).start()

    def fold(self, item, extra=(), start=0, width=None):
        def add(rows, first, count):
            at = pl.ds(start + first, count)
            total = self.own[item, rows, at].astype(jnp.float32)
            total += self.sib[item, rows, at].astype(jnp.float32)
            for way, step in extra:
                total += self.got[way, step, rows, at].astype(jnp.float32)
            self.own[item, rows, at] = total.astype(jnp.bfloat16)

        self.tiles(self.width if width is None else width, add)

    def ready(self, item):
        self.load(item).wait()
        self.give(item).wait_recv()
        self.far(item).wait_recv()
        offset = self.spot.rep * (self.kept - self.lent) * self.unit

        def add(rows, first, count):
            at = pl.ds(pl.multiple_of(offset + first, 128), count)
            total = self.sib[item, rows, at].astype(jnp.float32)
            total += self.got_far[item, rows, pl.ds(first, count)].astype(jnp.float32)
            self.sib[item, rows, at] = total.astype(jnp.bfloat16)

        self.tiles(self.lent * self.unit, add)

    def step(self, step):
        half, chips = self.spot.half, self.spot.chips

        @pl.when(step == 0)
        def _():
            self.ready(0)
            self.fold(0)
            for way in (0, 1):
                self.ring(way, 0, True).start()

        @pl.when((step > 0) & (step < half))
        def _():
            for way in (0, 1):
                item = 2 * step - 1 + way
                self.ready(item)

                @pl.when(step == 1)
                def _():
                    self.ring(way, 0, True).wait_recv()
                    middle = self.width // 2
                    self.fold(item, [(way, 0)], way * middle, middle)
                    self.fold(item, [], (1 - way) * middle, middle)

                @pl.when(step > 1)
                def _():
                    self.ring(way, step - 1).wait_recv()
                    self.fold(item, [(way, step - 1)])

                self.ring(way, step).start()

        @pl.when(step == half)
        def _():
            self.ready(chips - 1)
            for way in (0, 1):
                self.ring(way, half - 1).wait_recv()
            self.fold(chips - 1, [(0, half - 1), (1, half - 1)])
            self.last().start()

        @pl.when(step < half)
        def _():
            self.far_step(2 * step + 1)

            @pl.when(step < half - 1)
            def _():
                self.far_step(2 * step + 2)

    def finish(self):
        spot, unit, lent = self.spot, self.unit, self.lent
        self.last().wait()
        mine = self.own.at[spot.chips - 1]
        theirs = self.got_last

        def write(lower, upper):
            def one(tile, carry):
                rows = pl.ds(pl.multiple_of(tile * 16, 16), 16)

                def read(ref, first, count):
                    return ref[rows, pl.ds(first * unit, count * unit)].astype(jnp.float32)

                kept, both = self.kept, self.kept - lent
                self.out[rows, pl.ds(0, lent * unit)] = read(lower, 0, lent)
                for i in range(both):
                    self.out[rows, pl.ds((lent + i) * unit, unit)] = read(
                        lower, lent + i, 1
                    ) + read(upper, i, 1)
                self.out[rows, pl.ds(kept * unit, lent * unit)] = read(upper, both, lent)
                return carry

            lax.fori_loop(0, self.rows // 16, one, 0)

        @pl.when(spot.rep == 0)
        def _():
            write(mine, theirs)

        @pl.when(spot.rep == 1)
        def _():
            write(theirs, mine)

        def one(item, carry):
            self.give_far(item).wait_send()
            self.far(item).wait_send()
            self.give(item).wait_send()
            return carry

        lax.fori_loop(0, spot.chips, one, 0)
        for way in (0, 1):
            self.ring(way, 0, True).wait_send()

        def two(step, carry):
            for way in (0, 1):
                self.ring(way, step).wait_send()
            return carry

        lax.fori_loop(1, spot.half, two, 0)


class Tally:
    def __init__(self, spot, mine, out, refs):
        self.spot, self.mine, self.out = spot, mine, out
        self.got, self.half, self.other = refs[0:3]
        self.sems, self.own_sem, self.far_sems = refs[3:5], refs[5], refs[6:8]
        self.own = pltpu.make_async_copy(mine, self.got.at[spot.shard], self.own_sem)

    def copy(self, k):
        spot = self.spot
        target = lax.rem(spot.shard + k, spot.shards)
        return remote(self.mine, self.got.at[spot.shard], self.sems, (k,), (spot.rep, target))

    def far(self):
        target = (1 - self.spot.rep, self.spot.shard)
        return remote(self.half, self.other, self.far_sems, (0,), target)

    def start(self):
        def one(k, carry):
            self.copy(k).start()
            return carry

        lax.fori_loop(1, self.spot.shards, one, 0)
        self.own.start()

    def middle(self):
        def one(k, carry):
            self.copy(k).wait()
            return carry

        lax.fori_loop(1, self.spot.shards, one, 0)
        self.own.wait()

        def add(k, total):
            return total + self.got[k]

        self.half[...] = lax.fori_loop(0, self.spot.shards, add, jnp.zeros_like(self.half))
        self.far().start()

    def finish(self):
        self.far().wait()
        self.out[...] = self.half[...] + self.other[...]

    @staticmethod
    def scratch(shards, shape):
        full = jnp.float32
        return [
            pltpu.VMEM((shards, *shape), full),
            pltpu.VMEM(shape, full),
            pltpu.VMEM(shape, full),
            DMA((shards,)),
            DMA((shards,)),
            DMA,
            DMA((1,)),
            DMA((1,)),
        ]


class ReduceAll:
    def __init__(self, spot, lents, swap_count, tally_count, inputs, outputs, scratch):
        count = len(lents)
        self.spot = spot
        self.reduces = [
            Reduce(spot, lents[g], inputs[g], outputs[g], scratch[19 * g : 19 * g + 19])
            for g in range(count)
        ]
        scratch = scratch[19 * count :]
        self.swaps = [
            Swap(
                spot,
                inputs[count + i],
                outputs[count + i],
                scratch[3 * i : 3 * i + 2],
                scratch[3 * i + 2],
            )
            for i in range(swap_count)
        ]
        scratch = scratch[3 * swap_count :]
        self.tallies = [
            Tally(spot, inputs[-1], outputs[-1], scratch[:8]) for _ in range(tally_count)
        ]

    def start(self):
        greet(self.spot)

        def one(item, carry):
            for reduce in self.reduces:
                reduce.start(item)
            return carry

        lax.fori_loop(0, self.spot.chips, one, 0)
        for tally in self.tallies:
            tally.start()
        for reduce in self.reduces:
            reduce.far_step(0)

    def step(self, step):
        for swap in self.swaps:
            swap.start(step, self.spot.half + 1)
        for reduce in self.reduces:
            reduce.step(step)

    def steps(self, slot, slots):
        total = self.spot.half + 1
        size = -(-total // slots)

        def one(step, carry):
            self.step(step)
            return carry

        first = jnp.minimum(slot * size, total)
        lax.fori_loop(first, jnp.minimum(first + size, total), one, 0)

    def finish(self):
        for tally in self.tallies:
            tally.middle()
        for each in self.reduces + self.swaps + self.tallies:
            each.finish()

    @staticmethod
    def scratch(shards, lents, partials, swap_count, tallied):
        scratch = []
        for lent, part in zip(lents, partials, strict=True):
            scratch += Reduce.scratch(shards, lent, part.shape[0] // shards, part.shape[1])
        scratch += [DMA((shards,)), DMA((shards,)), DMA] * swap_count
        for each in tallied:
            scratch += Tally.scratch(shards, each.shape)
        return scratch


def reduce_kernel(shards, lents, swap_count, tally_count, *refs):
    total = len(lents) + swap_count + tally_count
    work = ReduceAll(
        Spot(shards),
        lents,
        swap_count,
        tally_count,
        refs[:total],
        refs[total : 2 * total],
        refs[2 * total :],
    )
    work.start()
    work.steps(0, 1)
    work.finish()


def reduce_specs(shards, partials, sent, tallied):
    anywhere = pl.BlockSpec(memory_space=pl.ANY)
    inside = pl.BlockSpec(memory_space=pltpu.VMEM)
    out_shape = [
        jax.ShapeDtypeStruct((part.shape[0] // shards, part.shape[1]), jnp.float32)
        for part in partials
    ]
    out_shape += [jax.ShapeDtypeStruct(each.shape, each.dtype) for each in [*sent, *tallied]]
    out_specs = [inside] * len(partials) + [anywhere] * len(sent) + [inside] * len(tallied)
    in_specs = [anywhere] * (len(partials) + len(sent)) + [inside] * len(tallied)
    return in_specs, out_specs, out_shape


def reduce_call(shards, partials, lents, sent, tallied, collective_id):
    in_specs, out_specs, out_shape = reduce_specs(shards, partials, sent, tallied)
    results = pl.pallas_call(
        functools.partial(reduce_kernel, shards, lents, len(sent), len(tallied)),
        out_shape=out_shape,
        in_specs=in_specs,
        out_specs=out_specs,
        scratch_shapes=ReduceAll.scratch(shards, lents, partials, len(sent), tallied),
        compiler_params=pltpu.CompilerParams(
            collective_id=collective_id, has_side_effects=True, vmem_limit_bytes=56 << 20
        ),
    )(*partials, *sent, *tallied)
    first, second = len(partials), len(partials) + len(sent)
    return results[:first], results[first:second], results[second:]


def matmul(left, right, left_dim=1, right_dim=0):
    return lax.dot_general(
        left, right, (((left_dim,), (right_dim,)), ((), ())), preferred_element_type=jnp.float32
    )


def pick_rows(slot_column, slot_total):
    shape = (slot_column.shape[0], slot_total)
    return (slot_column == lax.broadcasted_iota(jnp.int32, shape, 1)).astype(jnp.bfloat16)


def place_rows(slot_row, slot_total):
    shape = (slot_total, slot_row.shape[1])
    return (slot_row == lax.broadcasted_iota(jnp.int32, shape, 0)).astype(jnp.bfloat16)


def pack_kernel(rows_ref, tokens_ref, cotangent_ref, tokens_out, cotangent_out):
    chosen = place_rows(rows_ref[0:1, :], tokens_out.shape[0])
    tokens_out[...] = matmul(chosen, tokens_ref[...]).astype(jnp.bfloat16)
    cotangent_out[...] = matmul(chosen, cotangent_ref[...]).astype(jnp.bfloat16)


def unpack_kernel(columns_ref, output_ref, grad_ref, output_out, grad_out):
    chosen = pick_rows(columns_ref[:, 0:1], output_ref.shape[0])
    output_out[...] = matmul(chosen, output_ref[...]).astype(jnp.bfloat16)
    grad_out[...] = matmul(chosen, grad_ref[...]).astype(jnp.bfloat16)


def local_call(kernel, out_shape, inputs, spaces=None, scratch=()):
    inside = pl.BlockSpec(memory_space=pltpu.VMEM)
    return pl.pallas_call(
        kernel,
        out_shape=out_shape,
        in_specs=spaces or [inside] * len(inputs),
        out_specs=[inside] * len(out_shape),
        scratch_shapes=list(scratch),
        compiler_params=pltpu.CompilerParams(vmem_limit_bytes=56 << 20),
    )(*inputs)


def segment_of(index, lengths_ref):
    first = lengths_ref[0, 0]
    second = first + lengths_ref[0, 1]
    third = second + lengths_ref[0, 2]
    return (
        (index >= first).astype(jnp.int32)
        + (index >= second).astype(jnp.int32)
        + (index >= third).astype(jnp.int32)
    )


def pair_masks(columns_ref, rows_ref, lengths_ref, same_ref, hidden_ref):
    size = columns_ref.shape[0]
    shape = (size, size)
    key_id = lax.broadcasted_iota(jnp.int32, shape, 0)
    query_id = lax.broadcasted_iota(jnp.int32, shape, 1)
    key_column = lax.broadcasted_iota(jnp.int32, (size, 1), 0)
    query_row = lax.broadcasted_iota(jnp.int32, (1, size), 1)
    together = segment_of(key_column, lengths_ref) == segment_of(query_row, lengths_ref)
    seen = together & ((columns_ref[:, 3:4] > 0) | (key_id == query_id))
    same_ref[...] = (columns_ref[:, 2:3] == rows_ref[2:3, :]).astype(jnp.float32)
    hidden_ref[...] = jnp.where(seen, 0.0, masked_score)


def turn(values, cosine, sine):
    width = values.shape[1]
    lane = lax.broadcasted_iota(jnp.int32, values.shape, 1)
    other = jnp.where(
        lane % 64 < 32, pltpu.roll(values, width - 32, 1), pltpu.roll(values, 32, 1)
    )
    return values * cosine + other * sine


def head_lanes(values, head):
    lane = lax.broadcasted_iota(jnp.int32, values.shape, 1)
    return jnp.where((lane < 64) == (head == 0), values, jnp.zeros_like(values))


def project(input_ref, weight_refs, cosine_ref, sine_ref, out_ref, scale):
    width = weight_refs[0].shape[0]
    cosine = jnp.concatenate([cosine_ref[...]] * 2, axis=1)
    sine = jnp.concatenate([sine_ref[...]] * 2, axis=1)

    def one(i, carry):
        def columns(part):
            return pl.ds(pl.multiple_of(part * width + i * 256, 256), 256)

        at = pl.ds(pl.multiple_of(i * 256, 256), 256)
        query = matmul(input_ref[...], weight_refs[0][:, at])
        out_ref[:, columns(0)] = (turn(query, cosine, sine) * scale).astype(jnp.bfloat16)
        key = matmul(input_ref[...], weight_refs[1][:, at])
        out_ref[:, columns(1)] = turn(key, cosine, sine).astype(jnp.bfloat16)
        out_ref[:, columns(2)] = matmul(input_ref[...], weight_refs[2][:, at]).astype(
            jnp.bfloat16
        )
        return carry

    lax.fori_loop(0, width // 256, one, 0)


def attend_pair(pair, width, heads_ref, bias_ref, same_ref, hidden_ref, out_ref, log_ref):
    def columns(part):
        return pl.ds(pl.multiple_of(part * width + pair * 128, 128), 128)

    query, key, value = (heads_ref[:, columns(part)] for part in range(3))
    total = None
    for which in (0, 1):
        head = 2 * pair + which
        gap = bias_ref[0, head] - bias_ref[1, head]
        scores = matmul(head_lanes(key, which), query, 1, 1)
        scores = scores + same_ref[...] * gap + hidden_ref[...]
        top = jnp.max(scores, axis=0, keepdims=True)
        weights = jnp.exp(scores - top)
        weight_sum = jnp.sum(weights, axis=0, keepdims=True)
        log_ref[pl.ds(head, 1), :] = top + jnp.log(weight_sum)
        soft = (weights * (1.0 / weight_sum)).astype(jnp.bfloat16)
        part = matmul(head_lanes(value, which), soft, 0, 0)
        total = part if total is None else total + part
    out_ref[:, pl.ds(pl.multiple_of(pair * 128, 128), 128)] = total.T.astype(jnp.bfloat16)


def normed(values):
    factor = lax.rsqrt(jnp.mean(values * values, axis=-1, keepdims=True) + epsilon)
    return values * factor, factor


def forward_body(refs, between=None):
    (
        arrived_ref, columns_ref, rows_ref, lengths_ref, bias_ref, gain_ref,
        query_w_ref, key_w_ref, value_w_ref, cosine_ref, sine_ref,
        stream_ref, input_ref, heads_ref, out_ref, log_ref,
        same_ref, hidden_ref,
    ) = refs
    width = gain_ref.shape[1]
    scale = 1.0 / math.sqrt(64)
    chosen = pick_rows(columns_ref[:, 1:2], arrived_ref.shape[0])
    stream = matmul(chosen, arrived_ref[...])
    stream_ref[...] = stream.astype(jnp.bfloat16)
    input_ref[...] = (normed(stream)[0] * gain_ref[...]).astype(jnp.bfloat16)
    pair_masks(columns_ref, rows_ref, lengths_ref, same_ref, hidden_ref)
    weight_refs = (query_w_ref, key_w_ref, value_w_ref)
    project(input_ref, weight_refs, cosine_ref, sine_ref, heads_ref, scale)

    def one(pair, carry):
        if between is not None:
            between(pair)
        attend_pair(pair, width, heads_ref, bias_ref, same_ref, hidden_ref, out_ref, log_ref)
        return carry

    lax.fori_loop(0, width // 128, one, 0)


def forward_kernel(*refs):
    forward_body(refs)


def fold_lanes(row):
    folded = row[:, 0:128]
    for i in range(1, row.shape[1] // 128):
        folded += row[:, i * 128 : (i + 1) * 128]
    return folded


def mlp_kernel(
    shards, columns_ref, rows_ref, gain_ref, stream_ref, attended_ref, arrived_ref, out_w_ref,
    gate_ref, up_ref, down_ref,
    grad_gate_ref, grad_up_ref, grad_down_ref, dh_ref, grad_out_ref, do_ref, stats_ref, home_ref,
    middle_ref, input_ref, input_t_ref, dy_ref, mlp_ref, back_ref, packed_ref, gates_ref, ups_ref,
    send_sems, recv_sems, own_sem,
):
    step = pl.program_id(0)
    final = pl.num_programs(0) - 1
    tiles = pl.num_programs(0) // 2
    half = jnp.bfloat16
    spot = Spot(shards)
    swap = Swap(spot, packed_ref, home_ref, (send_sems, recv_sems), own_sem)

    def square(values, at):
        valid = (columns_ref[:, 3:4] > 0).astype(jnp.float32)
        across = jnp.sum(values * values * valid, axis=0, keepdims=True)
        stats_ref[at : at + 1, :] = fold_lanes(across)

    @pl.when(step == 0)
    def _():
        greet(spot)
        stats_ref[...] = jnp.zeros_like(stats_ref)
        stream = stream_ref[...].astype(jnp.float32)
        square(stream, 8)
        attn_out = matmul(attended_ref[...], out_w_ref[...])
        square(attn_out, 9)
        middle = stream + attn_out
        square(middle, 10)
        middle_ref[...] = middle
        entry = normed(middle)[0] * gain_ref[...]
        input_ref[...] = entry.astype(half)
        input_t_ref[...] = entry.T.astype(half)
        chosen = pick_rows(columns_ref[:, 1:2], arrived_ref.shape[0])
        dy_ref[...] = matmul(chosen, arrived_ref[...]).astype(half)
        mlp_ref[...] = jnp.zeros_like(mlp_ref)
        back_ref[...] = jnp.zeros_like(back_ref)

    @pl.when(step < tiles)
    def _():
        gate = matmul(input_ref[...], gate_ref[...])
        up = matmul(input_ref[...], up_ref[...])
        gates_ref[step] = gate
        ups_ref[step] = up
        hidden = (gate * jax.nn.sigmoid(gate) * up).astype(half)
        mlp_ref[...] += matmul(hidden, down_ref[...])

    @pl.when(step == tiles - 1)
    def _():
        valid = (columns_ref[:, 3:4] > 0).astype(jnp.float32)
        mlp_out = mlp_ref[...]
        result = middle_ref[...] + mlp_out
        placed = place_rows(rows_ref[1:2, :], packed_ref.shape[0])
        packed_ref[...] = matmul(placed, result.astype(half)).astype(half)
        swap.start(0, 1)
        square(mlp_out, 11)
        square(result, 12)
        lane = lax.broadcasted_iota(jnp.int32, (valid.shape[0], 128), 1)
        stats_ref[13:14, :] = jnp.sum(jnp.where(lane == 0, valid, 0.0), axis=0, keepdims=True)

    @pl.when(step >= tiles)
    def _():
        gate, up = gates_ref[step - tiles], ups_ref[step - tiles]
        grad_hidden = matmul(dy_ref[...], down_ref[...], 1, 1)
        sigmoid = jax.nn.sigmoid(gate)
        silu = gate * sigmoid
        hidden = (silu * up).astype(half)
        grad_gate = (grad_hidden * up * sigmoid * (1.0 + gate * (1.0 - sigmoid))).astype(half)
        grad_up = (grad_hidden * silu).astype(half)
        back_ref[...] += matmul(grad_gate, gate_ref[...], 1, 1) + matmul(
            grad_up, up_ref[...], 1, 1
        )
        grad_gate_ref[...] = matmul(input_t_ref[...], grad_gate).astype(half)
        grad_up_ref[...] = matmul(input_t_ref[...], grad_up).astype(half)
        grad_down_ref[...] = matmul(hidden, dy_ref[...], 0, 0).astype(half)

    @pl.when(step == final)
    def _():
        width = gain_ref.shape[1]
        entry, factor = normed(middle_ref[...])
        back = back_ref[...]
        gain_grad = jnp.sum(back * entry, axis=0, keepdims=True)
        for i in range(width // 128):
            stats_ref[i : i + 1, :] = gain_grad[:, i * 128 : (i + 1) * 128]
        scaled = back * gain_ref[...]
        inner = jnp.mean(scaled * entry, axis=-1, keepdims=True)
        dh = dy_ref[...].astype(jnp.float32) + factor * (scaled - entry * inner)
        dh_ref[...] = dh
        branch = dh.astype(half)
        do_ref[...] = matmul(branch, out_w_ref[...], 1, 1).astype(half)
        grad_out_ref[...] = matmul(attended_ref[...], branch, 0, 0).astype(half)
        swap.finish()


def mlp_call(shards, slot_total, inputs, weights, collective_id):
    columns, rows, gain, stream, attended, arrived, out_w = inputs
    gate, up, down = weights
    tokens, width = stream.shape
    hidden = gate.shape[1]
    tile = 512
    tiles = hidden // tile

    def whole(array):
        return pl.BlockSpec(
            array.shape, lambda i: (0,) * len(array.shape), pipeline_mode=pl.Buffered(1)
        )

    half, full = jnp.bfloat16, jnp.float32
    across = pl.BlockSpec((width, tile), lambda i: (0, lax.rem(i, tiles)))
    down_spec = pl.BlockSpec((tile, width), lambda i: (lax.rem(i, tiles), 0))
    across_out = pl.BlockSpec((width, tile), lambda i: (0, jnp.maximum(i - tiles, 0)))
    down_out = pl.BlockSpec((tile, width), lambda i: (jnp.maximum(i - tiles, 0), 0))
    out_shape = [
        jax.ShapeDtypeStruct((width, hidden), half),
        jax.ShapeDtypeStruct((width, hidden), half),
        jax.ShapeDtypeStruct((hidden, width), half),
        jax.ShapeDtypeStruct((tokens, width), full),
        jax.ShapeDtypeStruct((width, width), half),
        jax.ShapeDtypeStruct((tokens, width), half),
        jax.ShapeDtypeStruct((16, 128), full),
        jax.ShapeDtypeStruct((slot_total, width), half),
    ]
    rest = [pl.BlockSpec(each.shape, lambda i: (0, 0)) for each in out_shape[3:7]]
    return pl.pallas_call(
        functools.partial(mlp_kernel, shards),
        out_shape=out_shape,
        grid=(2 * tiles,),
        in_specs=[whole(each) for each in inputs] + [across, across, down_spec],
        out_specs=[across_out, across_out, down_out, *rest, pl.BlockSpec(memory_space=pl.ANY)],
        scratch_shapes=[
            pltpu.VMEM((tokens, width), full),
            pltpu.VMEM((tokens, width), half),
            pltpu.VMEM((width, tokens), half),
            pltpu.VMEM((tokens, width), half),
            pltpu.VMEM((tokens, width), full),
            pltpu.VMEM((tokens, width), full),
            pltpu.VMEM((slot_total, width), half),
            pltpu.VMEM((tiles, tokens, tile), full),
            pltpu.VMEM((tiles, tokens, tile), full),
            DMA((shards,)),
            DMA((shards,)),
            DMA,
        ],
        compiler_params=pltpu.CompilerParams(
            collective_id=collective_id, has_side_effects=True, vmem_limit_bytes=VMEM_LIMIT
        ),
    )(*inputs, *weights)


def attend_back_pair(
    pair, width, scale, heads_ref, do_ref, bias_ref, log_ref, same_ref, hidden_ref, cosine_ref,
    sine_ref, grads_ref, bias_same_ref, bias_all_ref,
):
    half = jnp.bfloat16

    def columns(part):
        return pl.ds(pl.multiple_of(part * width + pair * 128, 128), 128)

    query, key, value = (heads_ref[:, columns(part)] for part in range(3))
    grad_out = do_ref[:, columns(0)]
    query_t = key_grad = value_grad = None
    for which in (0, 1):
        head = 2 * pair + which
        gap = bias_ref[0, head] - bias_ref[1, head]
        key_part = head_lanes(key, which)
        scores = matmul(key_part, query, 1, 1)
        scores = scores + same_ref[...] * gap + hidden_ref[...]
        soft = jnp.exp(scores - log_ref[pl.ds(head, 1), :])
        grad_soft = matmul(head_lanes(value, which), grad_out, 1, 1)
        inner = jnp.sum(soft * grad_soft, axis=0, keepdims=True)
        grad_scores = (soft * (grad_soft - inner)).astype(half)
        wide = grad_scores.astype(jnp.float32)
        bias_all_ref[pl.ds(head, 1), :] = jnp.sum(wide, axis=0, keepdims=True)
        bias_same_ref[pl.ds(head, 1), :] = jnp.sum(wide * same_ref[...], axis=0, keepdims=True)
        parts = (
            matmul(key_part, grad_scores, 0, 0),
            matmul(grad_scores, head_lanes(query, which)),
            matmul(soft.astype(half), head_lanes(grad_out, which)),
        )
        if which == 0:
            query_t, key_grad, value_grad = parts
        else:
            query_t, key_grad, value_grad = (
                query_t + parts[0],
                key_grad + parts[1],
                value_grad + parts[2],
            )
    cosine, sine = cosine_ref[...], -sine_ref[...]
    grads_ref[:, columns(0)] = (turn(query_t.T, cosine, sine) * scale).astype(half)
    grads_ref[:, columns(1)] = turn(key_grad, cosine, sine).astype(half)
    grads_ref[:, columns(2)] = value_grad.astype(half)


def backward_reduce_kernel(shards, lents, *refs):
    (
        columns_ref, rows_ref, lengths_ref, bias_ref, cosine_ref, sine_ref, heads_ref, log_ref,
        do_ref,
    ) = refs[:9]
    count = len(lents)
    partials, refs = refs[9 : 9 + count], refs[9 + count :]
    (grads_ref, bias_out_ref), refs = refs[:2], refs[2:]
    outputs, refs = refs[:count], refs[count:]
    same_ref, hidden_ref, bias_same_ref, bias_all_ref = refs[:4]
    work = ReduceAll(Spot(shards), lents, 0, 0, partials, outputs, refs[4:])
    work.start()
    width = do_ref.shape[1]
    scale = 1.0 / math.sqrt(64)
    pair_masks(columns_ref, rows_ref, lengths_ref, same_ref, hidden_ref)
    pairs = width // 128

    def one(pair, carry):
        work.steps(pair, pairs)
        attend_back_pair(
            pair, width, scale, heads_ref, do_ref, bias_ref, log_ref, same_ref, hidden_ref,
            cosine_ref, sine_ref, grads_ref, bias_same_ref, bias_all_ref,
        )
        return carry

    lax.fori_loop(0, pairs, one, 0)
    heads = bias_all_ref.shape[0]
    lane = lax.broadcasted_iota(jnp.int32, (heads, 128), 1)
    row = lax.broadcasted_iota(jnp.int32, (heads, 128), 0)
    same = jnp.sum(bias_same_ref[...], axis=1, keepdims=True)
    other = jnp.sum(bias_all_ref[...], axis=1, keepdims=True) - same
    bias_out_ref[...] = jnp.broadcast_to(
        jnp.sum(
            jnp.where(lane == row, same, 0.0) + jnp.where(lane == row + heads, other, 0.0),
            axis=0,
            keepdims=True,
        ),
        bias_out_ref.shape,
    )
    work.finish()


def backward_reduce_call(shards, inputs, spaces, partials, lents, heads, collective_id):
    in_specs, out_specs, out_shape = reduce_specs(shards, partials, [], [])
    inside = pl.BlockSpec(memory_space=pltpu.VMEM)
    tokens, width = inputs[-1].shape
    full = jnp.float32
    results = pl.pallas_call(
        functools.partial(backward_reduce_kernel, shards, lents),
        out_shape=[
            jax.ShapeDtypeStruct((tokens, 3 * width), jnp.bfloat16),
            jax.ShapeDtypeStruct((8, 128), full),
            *out_shape,
        ],
        in_specs=[*spaces, *in_specs],
        out_specs=[inside, inside, *out_specs],
        scratch_shapes=[
            pltpu.VMEM((tokens, tokens), full),
            pltpu.VMEM((tokens, tokens), full),
            pltpu.VMEM((heads, tokens), full),
            pltpu.VMEM((heads, tokens), full),
            *ReduceAll.scratch(shards, lents, partials, 0, []),
        ],
        compiler_params=pltpu.CompilerParams(
            collective_id=collective_id, has_side_effects=True, vmem_limit_bytes=VMEM_LIMIT
        ),
    )(*inputs, *partials)
    return results[0], results[1], results[2:]


def entry_kernel(shards, lents, *refs):
    (
        rows_ref, gain_ref, query_w_ref, key_w_ref, value_w_ref, stream_ref, input_ref, grads_ref,
        dh_ref, stats_mlp_ref, bias_ref,
    ) = refs[:11]
    outputs, home_ref, sums_ref = refs[11:14], refs[14], refs[15]
    partials, back_ref, packed_ref, stats_ref = refs[16:19], refs[19], refs[20], refs[21]
    spot = Spot(shards)
    work = ReduceAll(
        spot, lents, 1, 1, [*partials, packed_ref, stats_ref], [*outputs, home_ref, sums_ref],
        refs[22:],
    )
    half = jnp.bfloat16
    width = gain_ref.shape[1]
    greet(spot)
    columns = [pl.ds(which * width, width) for which in range(3)]
    for which in range(3):
        reduce = work.reduces[which]

        def one(i, carry, which=which):
            at = pl.ds(pl.multiple_of(i * 256, 256), 256)
            part = grads_ref[:, pl.ds(pl.multiple_of(which * width + i * 256, 256), 256)]
            partials[which][:, at] = matmul(input_ref[...], part, 0, 0).astype(half)
            return carry

        lax.fori_loop(0, width // 256, one, 0)

        def begin(item, carry, reduce=reduce):
            reduce.start(item)
            return carry

        lax.fori_loop(0, spot.chips, begin, 0)
        reduce.far_step(0)
    back_ref[...] = matmul(grads_ref[:, columns[0]], query_w_ref[...], 1, 1)
    for reduce in work.reduces:
        reduce.step(0)
    back_ref[...] += matmul(grads_ref[:, columns[1]], key_w_ref[...], 1, 1)
    back_ref[...] += matmul(grads_ref[:, columns[2]], value_w_ref[...], 1, 1)
    back = back_ref[...]
    entry, factor = normed(stream_ref[...].astype(jnp.float32))
    gain_grad = jnp.sum(back * entry, axis=0, keepdims=True)
    scaled = back * gain_ref[...]
    inner = jnp.mean(scaled * entry, axis=-1, keepdims=True)
    grad_stream = dh_ref[...] + factor * (scaled - entry * inner)
    placed = place_rows(rows_ref[1:2, :], packed_ref.shape[0])
    packed_ref[...] = matmul(placed, grad_stream.astype(half)).astype(half)
    stats_ref[0:16, :] = stats_mlp_ref[...]
    for i in range(width // 128):
        stats_ref[16 + i : 17 + i, :] = gain_grad[:, i * 128 : (i + 1) * 128]
    stats_ref[24:32, :] = bias_ref[...]
    for swap in work.swaps:
        swap.start(0, 1)
    for tally in work.tallies:
        tally.start()

    def rest(step, carry):
        for reduce in work.reduces:
            reduce.step(step)
        return carry

    lax.fori_loop(1, spot.half + 1, rest, 0)
    work.finish()


def entry_call(shards, slot_total, inputs, lents, collective_id):
    anywhere = pl.BlockSpec(memory_space=pl.ANY)
    inside = pl.BlockSpec(memory_space=pltpu.VMEM)
    weights, stream = inputs[2:5], inputs[5]
    tokens, width = stream.shape
    half, full = jnp.bfloat16, jnp.float32
    tallied = jax.ShapeDtypeStruct((32, 128), full)
    results = pl.pallas_call(
        functools.partial(entry_kernel, shards, lents),
        out_shape=[
            *[jax.ShapeDtypeStruct((width // shards, width), full)] * 3,
            jax.ShapeDtypeStruct((slot_total, width), half),
            tallied,
        ],
        in_specs=[inside] * len(inputs),
        out_specs=[inside] * 3 + [anywhere, inside],
        scratch_shapes=[
            *[pltpu.VMEM((width, width), half)] * 3,
            pltpu.VMEM((tokens, width), full),
            pltpu.VMEM((slot_total, width), half),
            pltpu.VMEM((32, 128), full),
            *ReduceAll.scratch(shards, lents, weights, 1, [tallied]),
        ],
        compiler_params=pltpu.CompilerParams(
            collective_id=collective_id, has_side_effects=True, vmem_limit_bytes=VMEM_LIMIT
        ),
    )(*inputs)
    return results[:3], results[3], results[4]


def forward_gather_kernel(shards, lents, swap_count, compute_counts, *refs):
    ins, outs = compute_counts
    total = len(lents) + swap_count
    in_refs, refs = refs[: ins + total], refs[ins + total :]
    out_refs, refs = refs[: outs + total], refs[outs + total :]
    masks, scratch = refs[:2], refs[2:]
    work = GatherAll(
        Spot(shards), lents, swap_count, in_refs[ins:], out_refs[outs:], scratch
    )
    work.start()
    pairs = in_refs[5].shape[1] // 128
    forward_body(
        (*in_refs[:ins], *out_refs[:outs], *masks), lambda pair: work.steps(pair, pairs)
    )
    work.finish()


def forward_gather_call(shards, inputs, spaces, out_shape, pieces, lents, sent, collective_id):
    anywhere = pl.BlockSpec(memory_space=pl.ANY)
    inside = pl.BlockSpec(memory_space=pltpu.VMEM)
    tokens = out_shape[0].shape[0]
    counts = (len(inputs), len(out_shape))
    comm = len(pieces) + len(sent)
    results = pl.pallas_call(
        functools.partial(forward_gather_kernel, shards, lents, len(sent), counts),
        out_shape=[*out_shape, *gather_shapes(shards, pieces, sent, [])],
        in_specs=spaces + [anywhere] * comm,
        out_specs=[inside] * len(out_shape) + [anywhere] * comm,
        scratch_shapes=[pltpu.VMEM((tokens, tokens), jnp.float32)] * 2
        + GatherAll.scratch(shards, len(pieces), len(sent)),
        compiler_params=pltpu.CompilerParams(
            collective_id=collective_id, has_side_effects=True, vmem_limit_bytes=56 << 20
        ),
    )(*inputs, *pieces, *sent)
    first = len(out_shape)
    second = first + len(pieces)
    return results[:first], results[first:second], results[second:]


def on_device(
    tokens,
    cotangent,
    send_slot,
    recv_slot,
    lengths,
    variate,
    valid_mask,
    norm_attn,
    w_query,
    w_key,
    w_value,
    w_out,
    variate_bias,
    norm_mlp,
    w_gate,
    w_up,
    w_down,
):
    shards = lax.axis_size("shard")
    tok_rows, width = tokens.shape
    slot_total = 2 * tok_rows
    heads = variate_bias.shape[1]
    half, full = jnp.bfloat16, jnp.float32
    share = width // shards
    indices = jnp.stack([send_slot, recv_slot, variate, valid_mask])
    rows = jnp.concatenate([indices, jnp.zeros_like(indices)])
    columns = rows.T
    _, position = layout(lengths[0], tok_rows)
    cosine, sine = angle_tables(position, width // heads)
    cosine = jnp.concatenate([cosine] * 4, axis=1)
    sine = jnp.concatenate([-sine, sine] * 2, axis=1)
    gains = jnp.stack([norm_attn, norm_mlp]).astype(full)
    gains = jnp.pad(gains, ((0, 6), (0, 128 - share)))
    shape = jax.ShapeDtypeStruct
    packed_shape = shape((slot_total, width), half)
    token_shape = shape((tok_rows, width), half)
    out_tokens, out_cotangent = local_call(
        pack_kernel, [packed_shape] * 2, [rows, tokens, cotangent]
    )
    full_in, (arrived_tokens,), (gains,) = gather_call(
        shards,
        [w_query, w_key, w_value],
        (4, 4, 4),
        [out_tokens],
        [gains],
        1,
    )
    gains = gains.reshape(shards, 8, 128)
    gain_attn = gains[:, 0, :share].reshape(1, width)
    gain_mlp = gains[:, 1, :share].reshape(1, width)
    inside = pl.BlockSpec(memory_space=pltpu.VMEM)
    scalar = pl.BlockSpec(memory_space=pltpu.SMEM)
    (
        (stream, input_attn, head_rows, attended, logs),
        (full_out, full_gate, full_up, full_down),
        (arrived_grads,),
    ) = forward_gather_call(
        shards,
        [
            arrived_tokens, columns, rows, lengths, variate_bias, gain_attn, *full_in,
            cosine, sine,
        ],
        [inside] * 3 + [scalar] * 2 + [inside] * 6,
        [
            token_shape,
            token_shape,
            shape((tok_rows, 3 * width), half),
            token_shape,
            shape((heads, tok_rows), full),
        ],
        [w_out, w_gate, w_up, w_down],
        (2, 4, 4, 2),
        [out_cotangent],
        2,
    )
    part_gate, part_up, part_down, grad_middle, part_out, grad_attended, stats_mlp, home_out = (
        mlp_call(
            shards,
            slot_total,
            [columns, rows, gain_mlp, stream, attended, arrived_grads, full_out],
            [full_gate, full_up, full_down],
            3,
        )
    )
    head_grads, bias_sums, (grad_gate, grad_up, grad_down, grad_out) = backward_reduce_call(
        shards,
        [columns, rows, lengths, variate_bias, cosine, sine, head_rows, logs, grad_attended],
        [inside] * 2 + [scalar] * 2 + [inside] * 5,
        [part_gate, part_up, part_down, part_out],
        (2, 2, 2, 2),
        heads,
        4,
    )
    (grad_query, grad_key, grad_value), home_grad, sums = entry_call(
        shards,
        slot_total,
        [
            rows, gain_attn, *full_in, stream, input_attn, head_grads, grad_middle, stats_mlp,
            bias_sums,
        ],
        (2, 2, 2),
        5,
    )
    output, input_grad = local_call(
        unpack_kernel, [token_shape] * 2, [columns, home_out, home_grad]
    )
    squares = jnp.sum(sums[8:14], axis=1)
    root_means = jnp.sqrt(squares[:5] / (squares[5] * width))
    share_start = lax.axis_index("shard") * share
    grad_norm_mlp = lax.dynamic_slice_in_dim(sums[0:8].reshape(-1), share_start, share)
    grad_norm_attn = lax.dynamic_slice_in_dim(sums[16:24].reshape(-1), share_start, share)
    bias_grads = sums[24, : 2 * heads].reshape(2, heads)
    return (
        output,
        input_grad,
        grad_norm_attn,
        grad_query,
        grad_key,
        grad_value,
        grad_out,
        bias_grads,
        grad_norm_mlp,
        grad_gate,
        grad_up,
        grad_down,
        root_means,
    )


def solution(mesh):
    in_specs = (
        P(("rep", "shard"), None),
        P(("rep", "shard"), None),
        P(("rep", "shard")),
        P(("rep", "shard")),
        P(("rep", "shard"), None),
        P(("rep", "shard")),
        P(("rep", "shard")),
        P("shard"),
        P("shard", None),
        P("shard", None),
        P("shard", None),
        P("shard", None),
        P(),
        P("shard"),
        P("shard", None),
        P("shard", None),
        P("shard", None),
    )
    out_specs = (
        P(("rep", "shard"), None),
        P(("rep", "shard"), None),
        P("shard"),
        P("shard", None),
        P("shard", None),
        P("shard", None),
        P("shard", None),
        P(),
        P("shard"),
        P("shard", None),
        P("shard", None),
        P("shard", None),
        P(),
    )
    return jax.shard_map(
        on_device, mesh=mesh, in_specs=in_specs, out_specs=out_specs, check_vma=False
    )
```

time: 637 us -> 563 us (0.88)
  Pallas kernels: 610 us -> 537 us
    pallas_call x3 -> x2, Pallas kernels: 46.5 us -> 11 us  [local_call(): pl.pallas_call(kernel, out_shape=out_shape, in_specs=spaces or [inside] *...]
    pallas_call x3, Pallas kernels: 332 us -> 315 us  [the longest x1 127 us: backward_reduce_call(): pl.pallas_call(functools.partial(backward_reduce_kernel, shards, lents),...]
    pallas_call x1, Pallas kernels: 82.8 us -> 68.8 us  [gather_call(): pl.pallas_call(functools.partial(gather_kernel, shards, lents, len(swaps)...]
    pallas_call x1, Pallas kernels: 149 us -> 141 us  [forward_gather_call(): pl.pallas_call(functools.partial(forward_gather_kernel, shards, lents, le...]
where the time goes in v3:
time: 563 us; the launch traced here: 556 us
  Pallas kernels  537 us (95%)
  local copies, waits for them, and re-layouts  11.9 us (2%)
  other arithmetic  5.87 us (1%)
    pallas_call x1, Pallas kernels, forward_gather_call(): pl.pallas_call(functools.partial(forward_gather_kernel, shards, lents, le...  141 us
    pallas_call x1, Pallas kernels, backward_reduce_call(): pl.pallas_call(functools.partial(backward_reduce_kernel, shards, lents),...  127 us
    pallas_call x1, Pallas kernels, entry_call(): pl.pallas_call(functools.partial(entry_kernel, shards, lents), out_shape=...  103 us
    pallas_call x1, Pallas kernels, mlp_call(): pl.pallas_call(functools.partial(mlp_kernel, shards), out_shape=out_shape...  85.2 us
    pallas_call x1, Pallas kernels, gather_call(): pl.pallas_call(functools.partial(gather_kernel, shards, lents, len(swaps)...  68.8 us

profile of v3, /device:TPU:8, one launch (start us, length us, event | category | flops | bytes accessed | tf_op | source)
XLA Modules:
  0.0 556.1 jit_solution(3947231073643943453)
XLA Ops:
  0.7 0.8 reduce-window.4
  1.6 0.7 fusion.8
  2.4 1.0 fusion
  3.4 1.3 pad_maximum_fusion
  5.3 5.2 shard_map.264
  11.2 68.8 %shard_map.265 = (bf16[1024,1024]{1,0:T(8,128)(2,1)}, bf16[1024,1024]{1,0:T(8,128)(2,1)}, bf16[1024,1024]{1,0:T(8,128)(2,1)}, bf16[1024,1024]{1,0:T(8,128)(2,1)}, f32[128,128]{1,0:T(8,128)}) custom-call(bf16[64,1024]{1,0:T(8,128)(2,1)} %refs_0_.1, bf16[64,1024]{1,0:T(8,128)(2,1)} %refs_1_.1, bf16[64,1024]{1,0:T(8,128)(2,1)} %refs_2_.2, ...), custom_call_target="tpu_custom_call" | custom-call | tf_op jit(solution)/shard_map/pallas_call | solution.py:359
  80.0 0.9 fusion.9
  80.9 0.7 reshape_squeeze.10.refs_5_.refs_1_
  81.6 0.8 copy.54
  82.4 141.5 %shard_map.266 = (bf16[512,1024]{1,0:T(8,128)(2,1)}, bf16[512,1024]{1,0:T(8,128)(2,1)}, bf16[512,3072]{1,0:T(8,128)(2,1)}, bf16[512,1024]{1,0:T(8,128)(2,1)}, f3...) custom-call(bf16[1024,1024]{1,0:T(8,128)(2,1)} %get-tuple-element.53, ...), custom_call_target="tpu_custom_call" | custom-call | tf_op jit(solution)/shard_map/pallas_call | solution.py:1339
  223.9 0.7 reshape_squeeze.9.gain_ref
  224.6 85.2 %shard_map.267 = (bf16[1024,4096]{1,0:T(8,128)(2,1)}, bf16[1024,4096]{1,0:T(8,128)(2,1)}, bf16[4096,1024]{1,0:T(8,128)(2,1)}, f32[512,1024]{1,0:T(8,128)}, bf16[...) custom-call(s32[512,8]{1,0:T(8,128)} %bitcast.28, ...), custom_call_target="tpu_custom_call" | custom-call | tf_op jit(solution)/shard_map/pallas_call | solution.py:1082
  309.7 127.1 %shard_map.268 = (bf16[512,3072]{1,0:T(8,128)(2,1)}, f32[8,128]{1,0:T(8,128)}, f32[64,4096]{1,0:T(8,128)}, f32[64,4096]{1,0:T(8,128)}, f32[256,1024]{1,0:T(8,128)}, /*index=5*/f32[64,1024]{1,0:T(8,128)}) custom-call(s32[512,8]{1,0:T(8,128)} %bitcast.29, s32[8,512]{1,0:T(8,128)} %concatenate.9.rows_ref.refs_2_.refs_1_.refs_0_, s32[1,4]{1,0:T(1,128)} %refs_2_.3, ...), custom_call_target="tpu_custom_call" | custom-call | tf_op jit(solution)/shard_map/pallas_call | solution.py:1199
  436.8 103.1 %shard_map.269 = (f32[64,1024]{1,0:T(8,128)}, f32[64,1024]{1,0:T(8,128)}, f32[64,1024]{1,0:T(8,128)}, bf16[1024,1024]{1,0:T(8,128)(2,1)}, f32[32,128]{1,0:T(8,128)}) custom-call(s32[8,512]{1,0:T(8,128)} %concatenate.9.rows_ref.refs_2_.refs_1_.refs_0_, f32[1,1024]{1,0:T(1,128)} %reshape_squeeze.10.refs_5_.refs_1_, ...), custom_call_target="tpu_custom_call" | custom-call | tf_op jit(solution)/shard_map/pallas_call | solution.py:1293
  540.0 0.8 slice_reduce_fusion
  542.5 5.7 %shard_map.270 = (bf16[512,1024]{1,0:T(8,128)(2,1)}, bf16[512,1024]{1,0:T(8,128)(2,1)}) custom-call(s32[512,8]{1,0:T(8,128)} %bitcast.30, bf16[1024,1024]{1,0:T(8,128)(2,1)} %get-tuple-element.65.output_ref, bf16[1024,1024]{1,0:T(8,128)(2,1)} %get-tuple-element.78.grad_ref), custom_call_target="tpu_custom_call" | custom-call | tf_op jit(solution)/shard_map/pallas_call | solution.py:826
  549.5 0.6 reshape_squeeze.11
  550.1 0.7 copy.67
  550.8 0.7 copy.68
  551.5 0.7 copy.69
  552.2 0.7 copy.70
  553.0 1.0 copy.71
  553.9 1.0 copy.72
  554.9 1.0 copy.73
  (43 shorter events, 3.8 us)
Async XLA Ops:
  0.6 4.0 copy-start.9
  0.7 4.0 copy-start.10
  0.7 4.0 copy-start.11
  0.7 4.0 copy-start.12
  2.4 8.2 %copy-start.13 = (bf16[64]{0:T(256)(128)(2,1)S(1)}, bf16[64]{0:T(256)(128)(2,1)}, u32[]{:S(2)}) copy-start(bf16[64]{0:T(256)(128)(2,1)} %param.30) | copy-start | bytes 388
  2.4 8.2 %copy-start.14 = (bf16[64]{0:T(256)(128)(2,1)S(1)}, bf16[64]{0:T(256)(128)(2,1)}, u32[]{:S(2)}) copy-start(bf16[64]{0:T(256)(128)(2,1)} %param.24) | copy-start | bytes 388
  5.3 76.3 %copy-start.3 = (s32[8,512]{1,0:T(8,128)S(1)}, s32[8,512]{1,0:T(8,128)}, u32[]{:S(2)}) copy-start(s32[8,512]{1,0:T(8,128)} %concatenate.9.rows_ref.refs_2_.refs_1_.refs_0_) | copy-start | bytes 49156
  542.5 5.8 %copy-start.8 = (f32[32,128]{1,0:T(8,128)S(1)}, f32[32,128]{1,0:T(8,128)}, u32[]{:S(2)}) copy-start(f32[32,128]{1,0:T(8,128)} %get-tuple-element.81) | copy-start | bytes 49156
  542.5 7.6 %copy-start.7 = (f32[64,1024]{1,0:T(8,128)S(1)}, f32[64,1024]{1,0:T(8,128)}, u32[]{:S(2)}) copy-start(f32[64,1024]{1,0:T(8,128)} %get-tuple-element.114) | copy-start | bytes 786436
  542.5 8.3 %copy-start.6 = (f32[64,1024]{1,0:T(8,128)S(1)}, f32[64,1024]{1,0:T(8,128)}, u32[]{:S(2)}) copy-start(f32[64,1024]{1,0:T(8,128)} %get-tuple-element.115) | copy-start | bytes 786436
  542.5 9.0 %copy-start.5 = (f32[64,1024]{1,0:T(8,128)S(1)}, f32[64,1024]{1,0:T(8,128)}, u32[]{:S(2)}) copy-start(f32[64,1024]{1,0:T(8,128)} %get-tuple-element.116) | copy-start | bytes 786436
  542.5 9.7 %copy-start.4 = (f32[64,1024]{1,0:T(8,128)S(1)}, f32[64,1024]{1,0:T(8,128)}, u32[]{:S(2)}) copy-start(f32[64,1024]{1,0:T(8,128)} %get-tuple-element.117) | copy-start | bytes 786436
  548.3 4.7 copy-start.2
  550.1 3.8 copy-start.1
  552.9 1.9 copy-start

commit v4 on v3

--- a/solution.py
+++ b/solution.py
@@ -107,7 +107,7 @@
 
     def copy(self, k):
         spot = self.spot
-        target = lax.rem(spot.shard + k, spot.shards)
+        target = lax.rem(spot.shard + 7 * k, spot.shards)
         return remote(
             self.part(target),
             self.arrived.at[self.rows(spot.shard)],
@@ -273,9 +273,9 @@
 
 
 class GatherAll:
-    def __init__(self, spot, lents, swap_count, inputs, outputs, scratch):
+    def __init__(self, spot, lents, swap_count, inputs, outputs, scratch, late=False):
         count = len(lents)
-        self.spot = spot
+        self.spot, self.late = spot, late
         self.gathers = [
             Gather(spot, lents[g], inputs[g], outputs[g], scratch[11 * g : 11 * g + 11])
             for g in range(count)
@@ -298,8 +298,9 @@
             gather.start()
 
     def step(self, hop):
-        for swap in self.swaps:
-            swap.start(hop, self.spot.half)
+        if not self.late:
+            for swap in self.swaps:
+                swap.start(hop, self.spot.half)
         for gather in self.gathers:
             gather.step(hop)
 
@@ -313,11 +314,19 @@
         first = jnp.minimum(slot * size, self.spot.half)
         lax.fori_loop(first, jnp.minimum(first + size, self.spot.half), one, 0)
 
-    def finish(self):
+    def finish_gathers(self):
         for gather in self.gathers:
             gather.relay(0, self.spot.half - 1)
-        for each in self.gathers + self.swaps:
-            each.finish()
+        if self.late:
+            for swap in self.swaps:
+                swap.start(0, 1)
+        for gather in self.gathers:
+            gather.finish()
+
+    def finish(self):
+        self.finish_gathers()
+        for swap in self.swaps:
+            swap.finish()
 
     @staticmethod
     def scratch(shards, count, swap_count):
@@ -676,123 +685,6 @@
         ]
 
 
-class ReduceAll:
-    def __init__(self, spot, lents, swap_count, tally_count, inputs, outputs, scratch):
-        count = len(lents)
-        self.spot = spot
-        self.reduces = [
-            Reduce(spot, lents[g], inputs[g], outputs[g], scratch[19 * g : 19 * g + 19])
-            for g in range(count)
-        ]
-        scratch = scratch[19 * count :]
-        self.swaps = [
-            Swap(
-                spot,
-                inputs[count + i],
-                outputs[count + i],
-                scratch[3 * i : 3 * i + 2],
-                scratch[3 * i + 2],
-            )
-            for i in range(swap_count)
-        ]
-        scratch = scratch[3 * swap_count :]
-        self.tallies = [
-            Tally(spot, inputs[-1], outputs[-1], scratch[:8]) for _ in range(tally_count)
-        ]
-
-    def start(self):
-        greet(self.spot)
-
-        def one(item, carry):
-            for reduce in self.reduces:
-                reduce.start(item)
-            return carry
-
-        lax.fori_loop(0, self.spot.chips, one, 0)
-        for tally in self.tallies:
-            tally.start()
-        for reduce in self.reduces:
-            reduce.far_step(0)
-
-    def step(self, step):
-        for swap in self.swaps:
-            swap.start(step, self.spot.half + 1)
-        for reduce in self.reduces:
-            reduce.step(step)
-
-    def steps(self, slot, slots):
-        total = self.spot.half + 1
-        size = -(-total // slots)
-
-        def one(step, carry):
-            self.step(step)
-            return carry
-
-        first = jnp.minimum(slot * size, total)
-        lax.fori_loop(first, jnp.minimum(first + size, total), one, 0)
-
-    def finish(self):
-        for tally in self.tallies:
-            tally.middle()
-        for each in self.reduces + self.swaps + self.tallies:
-            each.finish()
-
-    @staticmethod
-    def scratch(shards, lents, partials, swap_count, tallied):
-        scratch = []
-        for lent, part in zip(lents, partials, strict=True):
-            scratch += Reduce.scratch(shards, lent, part.shape[0] // shards, part.shape[1])
-        scratch += [DMA((shards,)), DMA((shards,)), DMA] * swap_count
-        for each in tallied:
-            scratch += Tally.scratch(shards, each.shape)
-        return scratch
-
-
-def reduce_kernel(shards, lents, swap_count, tally_count, *refs):
-    total = len(lents) + swap_count + tally_count
-    work = ReduceAll(
-        Spot(shards),
-        lents,
-        swap_count,
-        tally_count,
-        refs[:total],
-        refs[total : 2 * total],
-        refs[2 * total :],
-    )
-    work.start()
-    work.steps(0, 1)
-    work.finish()
-
-
-def reduce_specs(shards, partials, sent, tallied):
-    anywhere = pl.BlockSpec(memory_space=pl.ANY)
-    inside = pl.BlockSpec(memory_space=pltpu.VMEM)
-    out_shape = [
-        jax.ShapeDtypeStruct((part.shape[0] // shards, part.shape[1]), jnp.float32)
-        for part in partials
-    ]
-    out_shape += [jax.ShapeDtypeStruct(each.shape, each.dtype) for each in [*sent, *tallied]]
-    out_specs = [inside] * len(partials) + [anywhere] * len(sent) + [inside] * len(tallied)
-    in_specs = [anywhere] * (len(partials) + len(sent)) + [inside] * len(tallied)
-    return in_specs, out_specs, out_shape
-
-
-def reduce_call(shards, partials, lents, sent, tallied, collective_id):
-    in_specs, out_specs, out_shape = reduce_specs(shards, partials, sent, tallied)
-    results = pl.pallas_call(
-        functools.partial(reduce_kernel, shards, lents, len(sent), len(tallied)),
-        out_shape=out_shape,
-        in_specs=in_specs,
-        out_specs=out_specs,
-        scratch_shapes=ReduceAll.scratch(shards, lents, partials, len(sent), tallied),
-        compiler_params=pltpu.CompilerParams(
-            collective_id=collective_id, has_side_effects=True, vmem_limit_bytes=56 << 20
-        ),
-    )(*partials, *sent, *tallied)
-    first, second = len(partials), len(partials) + len(sent)
-    return results[:first], results[first:second], results[second:]
-
-
 def matmul(left, right, left_dim=1, right_dim=0):
     return lax.dot_general(
         left, right, (((left_dim,), (right_dim,)), ((), ())), preferred_element_type=jnp.float32
@@ -813,12 +705,6 @@
     chosen = place_rows(rows_ref[0:1, :], tokens_out.shape[0])
     tokens_out[...] = matmul(chosen, tokens_ref[...]).astype(jnp.bfloat16)
     cotangent_out[...] = matmul(chosen, cotangent_ref[...]).astype(jnp.bfloat16)
-
-
-def unpack_kernel(columns_ref, output_ref, grad_ref, output_out, grad_out):
-    chosen = pick_rows(columns_ref[:, 0:1], output_ref.shape[0])
-    output_out[...] = matmul(chosen, output_ref[...]).astype(jnp.bfloat16)
-    grad_out[...] = matmul(chosen, grad_ref[...]).astype(jnp.bfloat16)
 
 
 def local_call(kernel, out_shape, inputs, spaces=None, scratch=()):
@@ -829,7 +715,7 @@
         in_specs=spaces or [inside] * len(inputs),
         out_specs=[inside] * len(out_shape),
         scratch_shapes=list(scratch),
-        compiler_params=pltpu.CompilerParams(vmem_limit_bytes=56 << 20),
+        compiler_params=pltpu.CompilerParams(vmem_limit_bytes=VMEM_LIMIT),
     )(*inputs)
 
 
@@ -945,10 +831,6 @@
     lax.fori_loop(0, width // 128, one, 0)
 
 
-def forward_kernel(*refs):
-    forward_body(refs)
-
-
 def fold_lanes(row):
     folded = row[:, 0:128]
     for i in range(1, row.shape[1] // 128):
@@ -956,153 +838,10 @@
     return folded
 
 
-def mlp_kernel(
-    shards, columns_ref, rows_ref, gain_ref, stream_ref, attended_ref, arrived_ref, out_w_ref,
-    gate_ref, up_ref, down_ref,
-    grad_gate_ref, grad_up_ref, grad_down_ref, dh_ref, grad_out_ref, do_ref, stats_ref, home_ref,
-    middle_ref, input_ref, input_t_ref, dy_ref, mlp_ref, back_ref, packed_ref, gates_ref, ups_ref,
-    send_sems, recv_sems, own_sem,
-):
-    step = pl.program_id(0)
-    final = pl.num_programs(0) - 1
-    tiles = pl.num_programs(0) // 2
-    half = jnp.bfloat16
-    spot = Spot(shards)
-    swap = Swap(spot, packed_ref, home_ref, (send_sems, recv_sems), own_sem)
-
-    def square(values, at):
-        valid = (columns_ref[:, 3:4] > 0).astype(jnp.float32)
-        across = jnp.sum(values * values * valid, axis=0, keepdims=True)
-        stats_ref[at : at + 1, :] = fold_lanes(across)
-
-    @pl.when(step == 0)
-    def _():
-        greet(spot)
-        stats_ref[...] = jnp.zeros_like(stats_ref)
-        stream = stream_ref[...].astype(jnp.float32)
-        square(stream, 8)
-        attn_out = matmul(attended_ref[...], out_w_ref[...])
-        square(attn_out, 9)
-        middle = stream + attn_out
-        square(middle, 10)
-        middle_ref[...] = middle
-        entry = normed(middle)[0] * gain_ref[...]
-        input_ref[...] = entry.astype(half)
-        input_t_ref[...] = entry.T.astype(half)
-        chosen = pick_rows(columns_ref[:, 1:2], arrived_ref.shape[0])
-        dy_ref[...] = matmul(chosen, arrived_ref[...]).astype(half)
-        mlp_ref[...] = jnp.zeros_like(mlp_ref)
-        back_ref[...] = jnp.zeros_like(back_ref)
-
-    @pl.when(step < tiles)
-    def _():
-        gate = matmul(input_ref[...], gate_ref[...])
-        up = matmul(input_ref[...], up_ref[...])
-        gates_ref[step] = gate
-        ups_ref[step] = up
-        hidden = (gate * jax.nn.sigmoid(gate) * up).astype(half)
-        mlp_ref[...] += matmul(hidden, down_ref[...])
-
-    @pl.when(step == tiles - 1)
-    def _():
-        valid = (columns_ref[:, 3:4] > 0).astype(jnp.float32)
-        mlp_out = mlp_ref[...]
-        result = middle_ref[...] + mlp_out
-        placed = place_rows(rows_ref[1:2, :], packed_ref.shape[0])
-        packed_ref[...] = matmul(placed, result.astype(half)).astype(half)
-        swap.start(0, 1)
-        square(mlp_out, 11)
-        square(result, 12)
-        lane = lax.broadcasted_iota(jnp.int32, (valid.shape[0], 128), 1)
-        stats_ref[13:14, :] = jnp.sum(jnp.where(lane == 0, valid, 0.0), axis=0, keepdims=True)
-
-    @pl.when(step >= tiles)
-    def _():
-        gate, up = gates_ref[step - tiles], ups_ref[step - tiles]
-        grad_hidden = matmul(dy_ref[...], down_ref[...], 1, 1)
-        sigmoid = jax.nn.sigmoid(gate)
-        silu = gate * sigmoid
-        hidden = (silu * up).astype(half)
-        grad_gate = (grad_hidden * up * sigmoid * (1.0 + gate * (1.0 - sigmoid))).astype(half)
-        grad_up = (grad_hidden * silu).astype(half)
-        back_ref[...] += matmul(grad_gate, gate_ref[...], 1, 1) + matmul(
-            grad_up, up_ref[...], 1, 1
-        )
-        grad_gate_ref[...] = matmul(input_t_ref[...], grad_gate).astype(half)
-        grad_up_ref[...] = matmul(input_t_ref[...], grad_up).astype(half)
-        grad_down_ref[...] = matmul(hidden, dy_ref[...], 0, 0).astype(half)
-
-    @pl.when(step == final)
-    def _():
-        width = gain_ref.shape[1]
-        entry, factor = normed(middle_ref[...])
-        back = back_ref[...]
-        gain_grad = jnp.sum(back * entry, axis=0, keepdims=True)
-        for i in range(width // 128):
-            stats_ref[i : i + 1, :] = gain_grad[:, i * 128 : (i + 1) * 128]
-        scaled = back * gain_ref[...]
-        inner = jnp.mean(scaled * entry, axis=-1, keepdims=True)
-        dh = dy_ref[...].astype(jnp.float32) + factor * (scaled - entry * inner)
-        dh_ref[...] = dh
-        branch = dh.astype(half)
-        do_ref[...] = matmul(branch, out_w_ref[...], 1, 1).astype(half)
-        grad_out_ref[...] = matmul(attended_ref[...], branch, 0, 0).astype(half)
-        swap.finish()
-
-
-def mlp_call(shards, slot_total, inputs, weights, collective_id):
-    columns, rows, gain, stream, attended, arrived, out_w = inputs
-    gate, up, down = weights
-    tokens, width = stream.shape
-    hidden = gate.shape[1]
-    tile = 512
-    tiles = hidden // tile
-
-    def whole(array):
-        return pl.BlockSpec(
-            array.shape, lambda i: (0,) * len(array.shape), pipeline_mode=pl.Buffered(1)
-        )
-
-    half, full = jnp.bfloat16, jnp.float32
-    across = pl.BlockSpec((width, tile), lambda i: (0, lax.rem(i, tiles)))
-    down_spec = pl.BlockSpec((tile, width), lambda i: (lax.rem(i, tiles), 0))
-    across_out = pl.BlockSpec((width, tile), lambda i: (0, jnp.maximum(i - tiles, 0)))
-    down_out = pl.BlockSpec((tile, width), lambda i: (jnp.maximum(i - tiles, 0), 0))
-    out_shape = [
-        jax.ShapeDtypeStruct((width, hidden), half),
-        jax.ShapeDtypeStruct((width, hidden), half),
-        jax.ShapeDtypeStruct((hidden, width), half),
-        jax.ShapeDtypeStruct((tokens, width), full),
-        jax.ShapeDtypeStruct((width, width), half),
-        jax.ShapeDtypeStruct((tokens, width), half),
-        jax.ShapeDtypeStruct((16, 128), full),
-        jax.ShapeDtypeStruct((slot_total, width), half),
-    ]
-    rest = [pl.BlockSpec(each.shape, lambda i: (0, 0)) for each in out_shape[3:7]]
-    return pl.pallas_call(
-        functools.partial(mlp_kernel, shards),
-        out_shape=out_shape,
-        grid=(2 * tiles,),
-        in_specs=[whole(each) for each in inputs] + [across, across, down_spec],
-        out_specs=[across_out, across_out, down_out, *rest, pl.BlockSpec(memory_space=pl.ANY)],
-        scratch_shapes=[
-            pltpu.VMEM((tokens, width), full),
-            pltpu.VMEM((tokens, width), half),
-            pltpu.VMEM((width, tokens), half),
-            pltpu.VMEM((tokens, width), half),
-            pltpu.VMEM((tokens, width), full),
-            pltpu.VMEM((tokens, width), full),
-            pltpu.VMEM((slot_total, width), half),
-            pltpu.VMEM((tiles, tokens, tile), full),
-            pltpu.VMEM((tiles, tokens, tile), full),
-            DMA((shards,)),
-            DMA((shards,)),
-            DMA,
-        ],
-        compiler_params=pltpu.CompilerParams(
-            collective_id=collective_id, has_side_effects=True, vmem_limit_bytes=VMEM_LIMIT
-        ),
-    )(*inputs, *weights)
+def square_into(stats_ref, at, values, columns_ref):
+    valid = (columns_ref[:, 3:4] > 0).astype(jnp.float32)
+    across = jnp.sum(values * values * valid, axis=0, keepdims=True)
+    stats_ref[at : at + 1, :] = fold_lanes(across)
 
 
 def attend_back_pair(
@@ -1149,207 +888,618 @@
     grads_ref[:, columns(2)] = value_grad.astype(half)
 
 
-def backward_reduce_kernel(shards, lents, *refs):
+def feed_forward(refs, weights, gates_out, ups_out, hidden_out, scratch):
+    columns_ref, rows_ref, gain_ref, stream_ref, attended_ref, out_w_ref = refs[:6]
+    packed_ref, middle_ref, input_ref, stats_ref = refs[6:]
     (
-        columns_ref, rows_ref, lengths_ref, bias_ref, cosine_ref, sine_ref, heads_ref, log_ref,
-        do_ref,
-    ) = refs[:9]
-    count = len(lents)
-    partials, refs = refs[9 : 9 + count], refs[9 + count :]
-    (grads_ref, bias_out_ref), refs = refs[:2], refs[2:]
-    outputs, refs = refs[:count], refs[count:]
-    same_ref, hidden_ref, bias_same_ref, bias_all_ref = refs[:4]
-    work = ReduceAll(Spot(shards), lents, 0, 0, partials, outputs, refs[4:])
+        gate_buf, up_buf, down_buf, gates_buf, ups_buf, hidden_buf, mlp_ref,
+        load_sems, store_sems,
+    ) = scratch
+    tile = gate_buf.shape[2]
+    tiles = gates_out.shape[1] // tile
+    half = jnp.bfloat16
+
+    def at(i):
+        return pl.ds(pl.multiple_of(i * tile, tile), tile)
+
+    def loads(i):
+        slot = lax.rem(i, 2)
+        return [
+            pltpu.make_async_copy(weights[0].at[:, at(i)], gate_buf.at[slot], load_sems.at[slot, 0]),
+            pltpu.make_async_copy(weights[1].at[:, at(i)], up_buf.at[slot], load_sems.at[slot, 1]),
+            pltpu.make_async_copy(weights[2].at[at(i)], down_buf.at[slot], load_sems.at[slot, 2]),
+        ]
+
+    def stores(i):
+        slot = lax.rem(i, 2)
+        return [
+            pltpu.make_async_copy(gates_buf.at[slot], gates_out.at[:, at(i)], store_sems.at[slot, 0]),
+            pltpu.make_async_copy(ups_buf.at[slot], ups_out.at[:, at(i)], store_sems.at[slot, 1]),
+            pltpu.make_async_copy(
+                hidden_buf.at[slot], hidden_out.at[:, at(i)], store_sems.at[slot, 2]
+            ),
+        ]
+
+    for copy in loads(0):
+        copy.start()
+    stats_ref[...] = jnp.zeros_like(stats_ref)
+    stream = stream_ref[...].astype(jnp.float32)
+    square_into(stats_ref, 0, stream, columns_ref)
+    attn_out = matmul(attended_ref[...], out_w_ref[...])
+    square_into(stats_ref, 1, attn_out, columns_ref)
+    middle = stream + attn_out
+    square_into(stats_ref, 2, middle, columns_ref)
+    middle_ref[...] = middle
+    input_ref[...] = (normed(middle)[0] * gain_ref[...]).astype(half)
+    mlp_ref[...] = jnp.zeros_like(mlp_ref)
+
+    def one(i, carry):
+        slot = lax.rem(i, 2)
+        for copy in loads(i):
+            copy.wait()
+
+        @pl.when(i + 1 < tiles)
+        def _():
+            for copy in loads(i + 1):
+                copy.start()
+
+        @pl.when(i >= 2)
+        def _():
+            for copy in stores(i - 2):
+                copy.wait()
+
+        gate = matmul(input_ref[...], gate_buf[slot])
+        up = matmul(input_ref[...], up_buf[slot])
+        gates_buf[slot] = gate
+        ups_buf[slot] = up
+        hidden = (gate * jax.nn.sigmoid(gate) * up).astype(half)
+        hidden_buf[slot] = hidden
+        for copy in stores(i):
+            copy.start()
+        mlp_ref[...] += matmul(hidden, down_buf[slot])
+        return carry
+
+    lax.fori_loop(0, tiles, one, 0)
+    valid = (columns_ref[:, 3:4] > 0).astype(jnp.float32)
+    mlp_out = mlp_ref[...]
+    result = middle_ref[...] + mlp_out
+    placed = place_rows(rows_ref[1:2, :], packed_ref.shape[0])
+    packed_ref[...] = matmul(placed, result.astype(half)).astype(half)
+    square_into(stats_ref, 3, mlp_out, columns_ref)
+    square_into(stats_ref, 4, result, columns_ref)
+    lane = lax.broadcasted_iota(jnp.int32, (valid.shape[0], 128), 1)
+    stats_ref[5:6, :] = jnp.sum(jnp.where(lane == 0, valid, 0.0), axis=0, keepdims=True)
+    for i in (tiles - 2, tiles - 1):
+        for copy in stores(i):
+            copy.wait()
+
+
+def forward_gather_kernel(shards, lents, swap_count, late, compute_counts, *refs):
+    ins, outs = compute_counts
+    total = len(lents) + swap_count
+    in_refs, refs = refs[: ins + total], refs[ins + total :]
+    out_refs, refs = refs[: outs + total], refs[outs + total :]
+    masks, out_w_buf, out_w_sem, feed_scratch, scratch = (
+        refs[:2], refs[2], refs[3], refs[4:13], refs[13:],
+    )
+    work = GatherAll(
+        Spot(shards), lents, swap_count, in_refs[ins:], out_refs[outs:], scratch, late
+    )
     work.start()
-    width = do_ref.shape[1]
+    *attend_ins, gain_mlp_ref = in_refs[:ins]
+    pairs = attend_ins[5].shape[1] // 128
+    attend_outs, feed_outs = out_refs[:5], out_refs[5:outs]
+    forward_body((*attend_ins, *attend_outs, *masks), lambda pair: work.steps(pair, pairs))
+    work.finish_gathers()
+    full_refs = out_refs[outs:]
+    copy = pltpu.make_async_copy(full_refs[0], out_w_buf, out_w_sem)
+    copy.start()
+    copy.wait()
+    gates_out, ups_out, hidden_out, *feed_outs = feed_outs
+    feed_forward(
+        (
+            attend_ins[1], attend_ins[2], gain_mlp_ref, attend_outs[0], attend_outs[3], out_w_buf,
+            *feed_outs,
+        ),
+        full_refs[1:4], gates_out, ups_out, hidden_out, feed_scratch,
+    )
+    for swap in work.swaps:
+        swap.finish()
+
+
+def forward_gather_call(
+    shards, inputs, spaces, out_shape, out_specs, pieces, lents, sent, late, collective_id
+):
+    anywhere = pl.BlockSpec(memory_space=pl.ANY)
+    tokens, width = out_shape[0].shape
+    tile = 512
+    half, full = jnp.bfloat16, jnp.float32
+    counts = (len(inputs), len(out_shape))
+    comm = len(pieces) + len(sent)
+    results = pl.pallas_call(
+        functools.partial(forward_gather_kernel, shards, lents, len(sent), late, counts),
+        out_shape=[*out_shape, *gather_shapes(shards, pieces, sent, [])],
+        in_specs=spaces + [anywhere] * comm,
+        out_specs=out_specs + [anywhere] * comm,
+        scratch_shapes=[
+            pltpu.VMEM((tokens, tokens), full),
+            pltpu.VMEM((tokens, tokens), full),
+            pltpu.VMEM((width, width), half),
+            DMA,
+            pltpu.VMEM((2, width, tile), half),
+            pltpu.VMEM((2, width, tile), half),
+            pltpu.VMEM((2, tile, width), half),
+            pltpu.VMEM((2, tokens, tile), full),
+            pltpu.VMEM((2, tokens, tile), full),
+            pltpu.VMEM((2, tokens, tile), half),
+            pltpu.VMEM((tokens, width), full),
+            DMA((2, 3)),
+            DMA((2, 3)),
+            *GatherAll.scratch(shards, len(pieces), len(sent)),
+        ],
+        compiler_params=pltpu.CompilerParams(
+            collective_id=collective_id, has_side_effects=True, vmem_limit_bytes=VMEM_LIMIT
+        ),
+    )(*inputs, *pieces, *sent)
+    first = len(out_shape)
+    second = first + len(pieces)
+    return results[:first], results[first:second], results[second:]
+
+
+def input_grad_kernel(shards, lent, *refs):
+    (
+        columns_ref, rows_ref, lengths_ref, bias_ref, gain_mlp_ref, gain_attn_ref, middle_ref,
+        out_w_ref, arrived_ref, heads_ref, log_ref, cosine_ref, sine_ref, stream_ref,
+        query_w_ref, key_w_ref, value_w_ref, packed_out_ref, gates_ref, ups_ref, rows_mlp_ref,
+        gate_w_ref, up_w_ref, down_w_ref,
+        dy_ref, grads_ref, packed_ref, stats_ref, grad_down_ref,
+        grad_gate_ref, grad_up_ref, home_ref, partial_ref,
+        gates_buf, ups_buf, gate_buf, up_buf, down_buf, grad_gate_buf, grad_up_buf,
+        back_ref, dh_ref, do_ref, same_ref, hidden_ref, bias_same_ref, bias_all_ref,
+        load_sems, store_sems, weight_sems, send_sems, recv_sems, own_sem,
+    ) = refs[:53]
+    spot = Spot(shards)
+    swap = Swap(spot, packed_out_ref, home_ref, (send_sems, recv_sems), own_sem)
+    reduce = Reduce(spot, lent, partial_ref, grad_down_ref, refs[53:])
+    tile = gate_buf.shape[2]
+    tiles = gates_ref.shape[1] // tile
+    width = gain_attn_ref.shape[1]
+    half = jnp.bfloat16
+
+    def at(i):
+        return pl.ds(pl.multiple_of(i * tile, tile), tile)
+
+    def loads(i):
+        slot = lax.rem(i, 2)
+        pairs = [
+            (gates_ref.at[:, at(i)], gates_buf),
+            (ups_ref.at[:, at(i)], ups_buf),
+            (gate_w_ref.at[:, at(i)], gate_buf),
+            (up_w_ref.at[:, at(i)], up_buf),
+            (down_w_ref.at[at(i)], down_buf),
+        ]
+        return [
+            pltpu.make_async_copy(source, buffer.at[slot], load_sems.at[slot, j])
+            for j, (source, buffer) in enumerate(pairs)
+        ]
+
+    def stores(i):
+        slot = lax.rem(i, 2)
+        pairs = [(grad_gate_buf, grad_gate_ref), (grad_up_buf, grad_up_ref)]
+        return [
+            pltpu.make_async_copy(buffer.at[slot], target.at[:, at(i)], store_sems.at[slot, j])
+            for j, (buffer, target) in enumerate(pairs)
+        ]
+
+    def row_loads(i):
+        slot = lax.rem(i, 2)
+        return [
+            pltpu.make_async_copy(
+                rows_mlp_ref.at[:, at(i)], grad_gate_buf.at[slot], load_sems.at[slot, 0]
+            )
+        ]
+
+    def row_stores(i):
+        slot = lax.rem(i, 2)
+        return [
+            pltpu.make_async_copy(
+                down_buf.at[slot], partial_ref.at[at(i)], store_sems.at[slot, 0]
+            )
+        ]
+
+    pairs = width // 128
+    slots = tiles + pairs
+    steps = spot.half + 1
+
+    def reduce_steps(slot):
+        def one(step, carry):
+            reduce.step(step)
+            return carry
+
+        lax.fori_loop(slot * steps // slots, (slot + 1) * steps // slots, one, 0)
+
+    greet(spot)
+    swap.start(0, tiles // 2)
+    for copy in row_loads(0):
+        copy.start()
+    chosen = pick_rows(columns_ref[:, 1:2], arrived_ref.shape[0])
+    dy_ref[...] = matmul(chosen, arrived_ref[...]).astype(half)
+
+    def rows_step(i, carry):
+        slot = lax.rem(i, 2)
+        for copy in row_loads(i):
+            copy.wait()
+
+        @pl.when(i + 1 < tiles)
+        def _():
+            for copy in row_loads(i + 1):
+                copy.start()
+
+        @pl.when(i >= 2)
+        def _():
+            for copy in row_stores(i - 2):
+                copy.wait()
+
+        down_buf[slot] = matmul(grad_gate_buf[slot], dy_ref[...], 0, 0).astype(half)
+        for copy in row_stores(i):
+            copy.start()
+        return carry
+
+    lax.fori_loop(0, tiles, rows_step, 0)
+    for i in (tiles - 2, tiles - 1):
+        for copy in row_stores(i):
+            copy.wait()
+    for copy in loads(0):
+        copy.start()
+
+    def begin(item, carry):
+        reduce.start(item)
+        return carry
+
+    lax.fori_loop(0, spot.chips, begin, 0)
+    back_ref[...] = jnp.zeros_like(back_ref)
+    pair_masks(columns_ref, rows_ref, lengths_ref, same_ref, hidden_ref)
+    reduce.far_step(0)
+
+    def one(i, carry):
+        slot = lax.rem(i, 2)
+
+        @pl.when(i < tiles // 2 - 1)
+        def _():
+            swap.start(i + 1, tiles // 2)
+
+        reduce_steps(i)
+        for copy in loads(i):
+            copy.wait()
+
+        @pl.when(i + 1 < tiles)
+        def _():
+            for copy in loads(i + 1):
+                copy.start()
+
+        @pl.when(i >= 2)
+        def _():
+            for copy in stores(i - 2):
+                copy.wait()
+
+        gate, up = gates_buf[slot], ups_buf[slot]
+        grad_hidden = matmul(dy_ref[...], down_buf[slot], 1, 1)
+        sigmoid = jax.nn.sigmoid(gate)
+        grad_gate = (grad_hidden * up * sigmoid * (1.0 + gate * (1.0 - sigmoid))).astype(half)
+        grad_up = (grad_hidden * gate * sigmoid).astype(half)
+        grad_gate_buf[slot] = grad_gate
+        grad_up_buf[slot] = grad_up
+        for copy in stores(i):
+            copy.start()
+        back_ref[...] += matmul(grad_gate, gate_buf[slot], 1, 1) + matmul(
+            grad_up, up_buf[slot], 1, 1
+        )
+        return carry
+
+    lax.fori_loop(0, tiles, one, 0)
+    stats_ref[...] = jnp.zeros_like(stats_ref)
+
+    def through_norm(values, grad, gain_ref, first):
+        entry, factor = normed(values)
+        gain_grad = jnp.sum(grad * entry, axis=0, keepdims=True)
+        for i in range(width // 128):
+            stats_ref[first + i : first + i + 1, :] = gain_grad[:, i * 128 : (i + 1) * 128]
+        scaled = grad * gain_ref[...]
+        inner = jnp.mean(scaled * entry, axis=-1, keepdims=True)
+        return factor * (scaled - entry * inner)
+
+    dh = dy_ref[...].astype(jnp.float32) + through_norm(
+        middle_ref[...], back_ref[...], gain_mlp_ref, 0
+    )
+    dh_ref[...] = dh
+    branch = dh.astype(half)
+    grads_ref[:, pl.ds(3 * width, width)] = branch
+    do_ref[...] = matmul(branch, out_w_ref[...], 1, 1).astype(half)
     scale = 1.0 / math.sqrt(64)
-    pair_masks(columns_ref, rows_ref, lengths_ref, same_ref, hidden_ref)
-    pairs = width // 128
-
-    def one(pair, carry):
-        work.steps(pair, pairs)
+    for i in (tiles - 2, tiles - 1):
+        for copy in stores(i):
+            copy.wait()
+    halves = [pl.ds(0, tile), pl.ds(tile, tile)]
+
+    def weight_loads(source, buffer, which):
+        return [
+            pltpu.make_async_copy(source.at[:, columns], buffer.at[j], weight_sems.at[which, j])
+            for j, columns in enumerate(halves)
+        ]
+
+    for copy in weight_loads(query_w_ref, gate_buf, 0) + weight_loads(key_w_ref, up_buf, 1):
+        copy.start()
+
+    def two(pair, carry):
+        reduce_steps(tiles + pair)
         attend_back_pair(
             pair, width, scale, heads_ref, do_ref, bias_ref, log_ref, same_ref, hidden_ref,
             cosine_ref, sine_ref, grads_ref, bias_same_ref, bias_all_ref,
         )
         return carry
 
-    lax.fori_loop(0, pairs, one, 0)
+    lax.fori_loop(0, width // 128, two, 0)
     heads = bias_all_ref.shape[0]
     lane = lax.broadcasted_iota(jnp.int32, (heads, 128), 1)
     row = lax.broadcasted_iota(jnp.int32, (heads, 128), 0)
     same = jnp.sum(bias_same_ref[...], axis=1, keepdims=True)
     other = jnp.sum(bias_all_ref[...], axis=1, keepdims=True) - same
-    bias_out_ref[...] = jnp.broadcast_to(
-        jnp.sum(
-            jnp.where(lane == row, same, 0.0) + jnp.where(lane == row + heads, other, 0.0),
-            axis=0,
-            keepdims=True,
-        ),
-        bias_out_ref.shape,
-    )
-    work.finish()
-
-
-def backward_reduce_call(shards, inputs, spaces, partials, lents, heads, collective_id):
-    in_specs, out_specs, out_shape = reduce_specs(shards, partials, [], [])
+    stats_ref[16:17, :] = jnp.sum(
+        jnp.where(lane == row, same, 0.0) + jnp.where(lane == row + heads, other, 0.0),
+        axis=0,
+        keepdims=True,
+    )
+    def through(buffer, first):
+        return sum(
+            matmul(grads_ref[:, pl.ds(first + j * tile, tile)], buffer[j], 1, 1) for j in (0, 1)
+        )
+
+    for copy in weight_loads(query_w_ref, gate_buf, 0):
+        copy.wait()
+    back_ref[...] = through(gate_buf, 0)
+    for copy in weight_loads(value_w_ref, gate_buf, 0):
+        copy.start()
+    for copy in weight_loads(key_w_ref, up_buf, 1):
+        copy.wait()
+    back_ref[...] += through(up_buf, width)
+    for copy in weight_loads(value_w_ref, gate_buf, 0):
+        copy.wait()
+    back_ref[...] += through(gate_buf, 2 * width)
+    grad_stream = dh_ref[...] + through_norm(
+        stream_ref[...].astype(jnp.float32), back_ref[...], gain_attn_ref, 8
+    )
+    placed = place_rows(rows_ref[1:2, :], packed_ref.shape[0])
+    packed_ref[...] = matmul(placed, grad_stream.astype(half)).astype(half)
+    swap.finish()
+    reduce.finish()
+
+
+def input_grad_call(shards, inputs, spaces, far_inputs, lent, collective_id):
+    anywhere = pl.BlockSpec(memory_space=pl.ANY)
     inside = pl.BlockSpec(memory_space=pltpu.VMEM)
-    tokens, width = inputs[-1].shape
-    full = jnp.float32
-    results = pl.pallas_call(
-        functools.partial(backward_reduce_kernel, shards, lents),
+    packed, gates = far_inputs[3], far_inputs[4]
+    tokens, hidden = gates.shape
+    width = packed.shape[1]
+    heads = inputs[10].shape[0]
+    tile = 512
+    assert 2 * tile == width
+    half, full = jnp.bfloat16, jnp.float32
+    vmem, shape = pltpu.VMEM, jax.ShapeDtypeStruct
+    return pl.pallas_call(
+        functools.partial(input_grad_kernel, shards, lent),
         out_shape=[
-            jax.ShapeDtypeStruct((tokens, 3 * width), jnp.bfloat16),
-            jax.ShapeDtypeStruct((8, 128), full),
-            *out_shape,
+            shape((tokens, width), half),
+            shape((tokens, 4 * width), half),
+            shape(packed.shape, half),
+            shape((24, 128), full),
+            shape((hidden // shards, width), full),
+            shape((tokens, hidden), half),
+            shape((tokens, hidden), half),
+            shape(packed.shape, half),
+            shape((hidden, width), half),
         ],
-        in_specs=[*spaces, *in_specs],
-        out_specs=[inside, inside, *out_specs],
+        in_specs=[*spaces, *[anywhere] * len(far_inputs)],
+        out_specs=[inside] * 5 + [anywhere] * 4,
         scratch_shapes=[
-            pltpu.VMEM((tokens, tokens), full),
-            pltpu.VMEM((tokens, tokens), full),
-            pltpu.VMEM((heads, tokens), full),
-            pltpu.VMEM((heads, tokens), full),
-            *ReduceAll.scratch(shards, lents, partials, 0, []),
+            vmem((2, tokens, tile), full),
+            vmem((2, tokens, tile), full),
+            vmem((2, width, tile), half),
+            vmem((2, width, tile), half),
+            vmem((2, tile, width), half),
+            vmem((2, tokens, tile), half),
+            vmem((2, tokens, tile), half),
+            vmem((tokens, width), full),
+            vmem((tokens, width), full),
+            vmem((tokens, width), half),
+            vmem((tokens, tokens), full),
+            vmem((tokens, tokens), full),
+            vmem((heads, tokens), full),
+            vmem((heads, tokens), full),
+            DMA((2, 5)),
+            DMA((2, 2)),
+            DMA((2, 2)),
+            DMA((shards,)),
+            DMA((shards,)),
+            DMA,
+            *Reduce.scratch(shards, lent, hidden // shards, width),
         ],
         compiler_params=pltpu.CompilerParams(
             collective_id=collective_id, has_side_effects=True, vmem_limit_bytes=VMEM_LIMIT
         ),
-    )(*inputs, *partials)
-    return results[0], results[1], results[2:]
-
-
-def entry_kernel(shards, lents, *refs):
+    )(*inputs, *far_inputs)
+
+
+def weight_grad_kernel(shards, lents, *refs):
     (
-        rows_ref, gain_ref, query_w_ref, key_w_ref, value_w_ref, stream_ref, input_ref, grads_ref,
-        dh_ref, stats_mlp_ref, bias_ref,
-    ) = refs[:11]
-    outputs, home_ref, sums_ref = refs[11:14], refs[14], refs[15]
-    partials, back_ref, packed_ref, stats_ref = refs[16:19], refs[19], refs[20], refs[21]
+        columns_ref, input_attn_ref, attended_ref, input_mlp_ref, stats_forward_ref,
+        stats_back_ref, home_out_ref, packed_ref, gate_ref, up_ref, entry_ref,
+        grad_gate_ref, grad_up_ref, grad_in_ref, output_ref, input_grad_ref, sums_ref,
+    ) = refs[:17]
+    partials = refs[17:20]
+    (
+        attn_t_ref, attended_t_ref, mlp_t_ref, home_ref, stats_ref, tile_buf, part_buf,
+        load_sems, store_sems, send_sems, recv_sems, own_sem,
+    ) = refs[20:32]
+    tally_refs, refs = refs[32:40], refs[40:]
+    half, full = jnp.bfloat16, jnp.float32
     spot = Spot(shards)
-    work = ReduceAll(
-        spot, lents, 1, 1, [*partials, packed_ref, stats_ref], [*outputs, home_ref, sums_ref],
-        refs[22:],
-    )
-    half = jnp.bfloat16
-    width = gain_ref.shape[1]
-    greet(spot)
-    columns = [pl.ds(which * width, width) for which in range(3)]
-    for which in range(3):
-        reduce = work.reduces[which]
-
-        def one(i, carry, which=which):
-            at = pl.ds(pl.multiple_of(i * 256, 256), 256)
-            part = grads_ref[:, pl.ds(pl.multiple_of(which * width + i * 256, 256), 256)]
-            partials[which][:, at] = matmul(input_ref[...], part, 0, 0).astype(half)
-            return carry
-
-        lax.fori_loop(0, width // 256, one, 0)
-
-        def begin(item, carry, reduce=reduce):
+    swap = Swap(spot, packed_ref, home_ref, (send_sems, recv_sems), own_sem)
+    tally = Tally(spot, stats_ref, sums_ref, tally_refs)
+    outputs = (grad_gate_ref, grad_up_ref, grad_in_ref)
+    reduces = [
+        Reduce(spot, lents[g], partials[g], outputs[g], refs[19 * g : 19 * g + 19])
+        for g in range(3)
+    ]
+    steps = spot.half + 1
+    parts = 5
+    tile = tile_buf.shape[2]
+    tiles = gate_ref.shape[1] // tile
+
+    def at(i):
+        return pl.ds(pl.multiple_of(i * tile, tile), tile)
+
+    def product(source, lefts, partial, reduce):
+        def load(i):
+            slot = lax.rem(i, 2)
+            return pltpu.make_async_copy(
+                source.at[:, at(i)], tile_buf.at[slot], load_sems.at[slot]
+            )
+
+        def store(i):
+            slot = lax.rem(i, 2)
+            return pltpu.make_async_copy(
+                part_buf.at[slot], partial.at[:, at(i)], store_sems.at[slot]
+            )
+
+        load(0).start()
+        first = 0
+        for left, count in lefts:
+
+            def one(i, carry, left=left):
+                slot = lax.rem(i, 2)
+                load(i).wait()
+
+                @pl.when(i + 1 < tiles)
+                def _():
+                    load(i + 1).start()
+
+                @pl.when(i >= 2)
+                def _():
+                    store(i - 2).wait()
+
+                part_buf[slot] = matmul(left[...], tile_buf[slot]).astype(half)
+                store(i).start()
+                return carry
+
+            lax.fori_loop(first, first + count, one, 0)
+            first += count
+        for i in (tiles - 2, tiles - 1):
+            store(i).wait()
+
+        def begin(item, carry):
             reduce.start(item)
             return carry
 
         lax.fori_loop(0, spot.chips, begin, 0)
         reduce.far_step(0)
-    back_ref[...] = matmul(grads_ref[:, columns[0]], query_w_ref[...], 1, 1)
-    for reduce in work.reduces:
-        reduce.step(0)
-    back_ref[...] += matmul(grads_ref[:, columns[1]], key_w_ref[...], 1, 1)
-    back_ref[...] += matmul(grads_ref[:, columns[2]], value_w_ref[...], 1, 1)
-    back = back_ref[...]
-    entry, factor = normed(stream_ref[...].astype(jnp.float32))
-    gain_grad = jnp.sum(back * entry, axis=0, keepdims=True)
-    scaled = back * gain_ref[...]
-    inner = jnp.mean(scaled * entry, axis=-1, keepdims=True)
-    grad_stream = dh_ref[...] + factor * (scaled - entry * inner)
-    placed = place_rows(rows_ref[1:2, :], packed_ref.shape[0])
-    packed_ref[...] = matmul(placed, grad_stream.astype(half)).astype(half)
-    stats_ref[0:16, :] = stats_mlp_ref[...]
-    for i in range(width // 128):
-        stats_ref[16 + i : 17 + i, :] = gain_grad[:, i * 128 : (i + 1) * 128]
-    stats_ref[24:32, :] = bias_ref[...]
-    for swap in work.swaps:
-        swap.start(0, 1)
-    for tally in work.tallies:
-        tally.start()
-
-    def rest(step, carry):
-        for reduce in work.reduces:
-            reduce.step(step)
+
+    greet(spot)
+    swap.start(0, parts)
+    stats_ref[0:8, :] = stats_forward_ref[...]
+    stats_ref[8:32, :] = stats_back_ref[...]
+    tally.start()
+    mlp_t_ref[...] = input_mlp_ref[...].astype(full).T.astype(half)
+    product(gate_ref, [(mlp_t_ref, tiles)], partials[0], reduces[0])
+    swap.start(1, parts)
+    product(up_ref, [(mlp_t_ref, tiles)], partials[1], reduces[1])
+    swap.start(2, parts)
+    chosen = pick_rows(columns_ref[:, 0:1], home_ref.shape[0])
+
+    def ticks(tick, carry):
+        @pl.when(tick < steps)
+        def _():
+            reduces[0].step(tick)
+
+        @pl.when(tick < 2)
+        def _():
+            swap.start(3 + tick, parts)
+
+        @pl.when(tick == 0)
+        def _():
+            attn_t_ref[...] = input_attn_ref[...].astype(full).T.astype(half)
+            attended_t_ref[...] = attended_ref[...].astype(full).T.astype(half)
+            product(
+                entry_ref,
+                [(attn_t_ref, tiles - tiles // 4), (attended_t_ref, tiles // 4)],
+                partials[2],
+                reduces[2],
+            )
+
+        @pl.when((tick > 0) & (tick < steps + 1))
+        def _():
+            reduces[1].step(tick - 1)
+
+        @pl.when(tick == 1)
+        def _():
+            output_ref[...] = matmul(chosen, home_out_ref[...]).astype(half)
+            tally.middle()
+
+        @pl.when(tick > 1)
+        def _():
+            reduces[2].step(tick - 2)
+
         return carry
 
-    lax.fori_loop(1, spot.half + 1, rest, 0)
-    work.finish()
-
-
-def entry_call(shards, slot_total, inputs, lents, collective_id):
+    lax.fori_loop(0, steps + 2, ticks, 0)
+    swap.finish()
+    input_grad_ref[...] = matmul(chosen, home_ref[...]).astype(half)
+    tally.finish()
+    for reduce in reduces:
+        reduce.finish()
+
+
+def weight_grad_call(shards, inputs, far_inputs, lents, collective_id):
+    tile = 512
+    packed, hidden = far_inputs[0], far_inputs[1].shape[1]
+    tokens, width = inputs[1].shape
+    assert hidden == 4 * width
+    half, full = jnp.bfloat16, jnp.float32
+    shape = jax.ShapeDtypeStruct
     anywhere = pl.BlockSpec(memory_space=pl.ANY)
     inside = pl.BlockSpec(memory_space=pltpu.VMEM)
-    weights, stream = inputs[2:5], inputs[5]
-    tokens, width = stream.shape
-    half, full = jnp.bfloat16, jnp.float32
-    tallied = jax.ShapeDtypeStruct((32, 128), full)
+    scratch = []
+    for lent in lents:
+        scratch += Reduce.scratch(shards, lent, width // shards, hidden)
     results = pl.pallas_call(
-        functools.partial(entry_kernel, shards, lents),
+        functools.partial(weight_grad_kernel, shards, lents),
         out_shape=[
-            *[jax.ShapeDtypeStruct((width // shards, width), full)] * 3,
-            jax.ShapeDtypeStruct((slot_total, width), half),
-            tallied,
+            *[shape((width // shards, hidden), full)] * 3,
+            shape((tokens, width), half),
+            shape((tokens, width), half),
+            shape((32, 128), full),
+            *[shape((width, hidden), half)] * 3,
         ],
-        in_specs=[inside] * len(inputs),
-        out_specs=[inside] * 3 + [anywhere, inside],
+        in_specs=[inside] * len(inputs) + [anywhere] * len(far_inputs),
+        out_specs=[inside] * 6 + [anywhere] * 3,
         scratch_shapes=[
-            *[pltpu.VMEM((width, width), half)] * 3,
-            pltpu.VMEM((tokens, width), full),
-            pltpu.VMEM((slot_total, width), half),
+            *[pltpu.VMEM((width, tokens), half)] * 3,
+            pltpu.VMEM(packed.shape, half),
             pltpu.VMEM((32, 128), full),
-            *ReduceAll.scratch(shards, lents, weights, 1, [tallied]),
+            pltpu.VMEM((2, tokens, tile), half),
+            pltpu.VMEM((2, width, tile), half),
+            DMA((2,)),
+            DMA((2,)),
+            DMA((shards,)),
+            DMA((shards,)),
+            DMA,
+            *Tally.scratch(shards, (32, 128)),
+            *scratch,
         ],
         compiler_params=pltpu.CompilerParams(
             collective_id=collective_id, has_side_effects=True, vmem_limit_bytes=VMEM_LIMIT
         ),
-    )(*inputs)
-    return results[:3], results[3], results[4]
-
-
-def forward_gather_kernel(shards, lents, swap_count, compute_counts, *refs):
-    ins, outs = compute_counts
-    total = len(lents) + swap_count
-    in_refs, refs = refs[: ins + total], refs[ins + total :]
-    out_refs, refs = refs[: outs + total], refs[outs + total :]
-    masks, scratch = refs[:2], refs[2:]
-    work = GatherAll(
-        Spot(shards), lents, swap_count, in_refs[ins:], out_refs[outs:], scratch
-    )
-    work.start()
-    pairs = in_refs[5].shape[1] // 128
-    forward_body(
-        (*in_refs[:ins], *out_refs[:outs], *masks), lambda pair: work.steps(pair, pairs)
-    )
-    work.finish()
-
-
-def forward_gather_call(shards, inputs, spaces, out_shape, pieces, lents, sent, collective_id):
-    anywhere = pl.BlockSpec(memory_space=pl.ANY)
-    inside = pl.BlockSpec(memory_space=pltpu.VMEM)
-    tokens = out_shape[0].shape[0]
-    counts = (len(inputs), len(out_shape))
-    comm = len(pieces) + len(sent)
-    results = pl.pallas_call(
-        functools.partial(forward_gather_kernel, shards, lents, len(sent), counts),
-        out_shape=[*out_shape, *gather_shapes(shards, pieces, sent, [])],
-        in_specs=spaces + [anywhere] * comm,
-        out_specs=[inside] * len(out_shape) + [anywhere] * comm,
-        scratch_shapes=[pltpu.VMEM((tokens, tokens), jnp.float32)] * 2
-        + GatherAll.scratch(shards, len(pieces), len(sent)),
-        compiler_params=pltpu.CompilerParams(
-            collective_id=collective_id, has_side_effects=True, vmem_limit_bytes=56 << 20
-        ),
-    )(*inputs, *pieces, *sent)
-    first = len(out_shape)
-    second = first + len(pieces)
-    return results[:first], results[first:second], results[second:]
+    )(*inputs, *far_inputs)
+    return results[:6]
 
 
 def on_device(
@@ -1405,64 +1555,70 @@
     gain_mlp = gains[:, 1, :share].reshape(1, width)
     inside = pl.BlockSpec(memory_space=pltpu.VMEM)
     scalar = pl.BlockSpec(memory_space=pltpu.SMEM)
+    anywhere = pl.BlockSpec(memory_space=pl.ANY)
+    hidden = w_gate.shape[1]
     (
-        (stream, input_attn, head_rows, attended, logs),
+        (
+            stream, input_attn, head_rows, attended, logs,
+            gates, ups, hidden_rows, packed, middle, input_mlp, stats_forward,
+        ),
         (full_out, full_gate, full_up, full_down),
         (arrived_grads,),
     ) = forward_gather_call(
         shards,
         [
             arrived_tokens, columns, rows, lengths, variate_bias, gain_attn, *full_in,
-            cosine, sine,
+            cosine, sine, gain_mlp,
         ],
-        [inside] * 3 + [scalar] * 2 + [inside] * 6,
+        [inside] * 3 + [scalar] * 2 + [inside] * 7,
         [
             token_shape,
             token_shape,
             shape((tok_rows, 3 * width), half),
             token_shape,
             shape((heads, tok_rows), full),
+            shape((tok_rows, hidden), full),
+            shape((tok_rows, hidden), full),
+            shape((tok_rows, hidden), half),
+            packed_shape,
+            shape((tok_rows, width), full),
+            token_shape,
+            shape((8, 128), full),
         ],
+        [inside] * 5 + [anywhere] * 3 + [inside] * 4,
         [w_out, w_gate, w_up, w_down],
-        (2, 4, 4, 2),
+        (4, 4, 4, 2),
         [out_cotangent],
+        False,
         2,
     )
-    part_gate, part_up, part_down, grad_middle, part_out, grad_attended, stats_mlp, home_out = (
-        mlp_call(
-            shards,
-            slot_total,
-            [columns, rows, gain_mlp, stream, attended, arrived_grads, full_out],
-            [full_gate, full_up, full_down],
-            3,
-        )
-    )
-    head_grads, bias_sums, (grad_gate, grad_up, grad_down, grad_out) = backward_reduce_call(
+    (
+        _, entry_grads, packed_grad, stats_back, grad_down, grad_gates, grad_ups, home_out, _,
+    ) = input_grad_call(
         shards,
-        [columns, rows, lengths, variate_bias, cosine, sine, head_rows, logs, grad_attended],
-        [inside] * 2 + [scalar] * 2 + [inside] * 5,
-        [part_gate, part_up, part_down, part_out],
-        (2, 2, 2, 2),
-        heads,
+        [
+            columns, rows, lengths, variate_bias, gain_mlp, gain_attn, middle, full_out,
+            arrived_grads, head_rows, logs, cosine, sine, stream,
+        ],
+        [inside] * 2 + [scalar] * 2 + [inside] * 10,
+        [*full_in, packed, gates, ups, hidden_rows, full_gate, full_up, full_down],
+        2,
+        3,
+    )
+    grad_gate, grad_up, grad_in, output, input_grad, sums = weight_grad_call(
+        shards,
+        [columns, input_attn, attended, input_mlp, stats_forward, stats_back, home_out],
+        [packed_grad, grad_gates, grad_ups, entry_grads],
+        (2, 2, 2),
         4,
     )
-    (grad_query, grad_key, grad_value), home_grad, sums = entry_call(
-        shards,
-        slot_total,
-        [
-            rows, gain_attn, *full_in, stream, input_attn, head_grads, grad_middle, stats_mlp,
-            bias_sums,
-        ],
-        (2, 2, 2),
-        5,
-    )
-    output, input_grad = local_call(
-        unpack_kernel, [token_shape] * 2, [columns, home_out, home_grad]
-    )
-    squares = jnp.sum(sums[8:14], axis=1)
+    grad_query, grad_key, grad_value, grad_out = (
+        grad_in[:, i * width : (i + 1) * width] for i in range(4)
+    )
+    squares = jnp.sum(sums[0:6], axis=1)
     root_means = jnp.sqrt(squares[:5] / (squares[5] * width))
     share_start = lax.axis_index("shard") * share
-    grad_norm_mlp = lax.dynamic_slice_in_dim(sums[0:8].reshape(-1), share_start, share)
+    grad_norm_mlp = lax.dynamic_slice_in_dim(sums[8:16].reshape(-1), share_start, share)
     grad_norm_attn = lax.dynamic_slice_in_dim(sums[16:24].reshape(-1), share_start, share)
     bias_grads = sums[24, : 2 * heads].reshape(2, heads)
     return (

time: 563 us -> 527 us (0.936)
  Pallas kernels: 537 us -> 500 us
    pallas_call x3 -> x2, Pallas kernels: 315 us -> 266 us  [the longest x1 163 us: weight_grad_call(): pl.pallas_call(functools.partial(weight_grad_kernel, shards, lents), out_...]
    pallas_call x1, Pallas kernels: 141 us -> 159 us  [forward_gather_call(): pl.pallas_call(functools.partial(forward_gather_kernel, shards, lents, le...]
    pallas_call x2 -> x1, Pallas kernels: 11 us -> 5.27 us  [local_call(): pl.pallas_call(kernel, out_shape=out_shape, in_specs=spaces or [inside] *...]
where the time goes in v4:
time: 527 us; the launch traced here: 523 us
  Pallas kernels  500 us (95%)
  local copies, waits for them, and re-layouts  16.3 us (3%)
    pallas_call x1, Pallas kernels, weight_grad_call(): pl.pallas_call(functools.partial(weight_grad_kernel, shards, lents), out_...  163 us
    pallas_call x1, Pallas kernels, forward_gather_call(): pl.pallas_call(functools.partial(forward_gather_kernel, shards, lents, le...  159 us
    pallas_call x1, Pallas kernels, input_grad_call(): pl.pallas_call(functools.partial(input_grad_kernel, shards, lent), out_sh...  103 us
    pallas_call x1, Pallas kernels, gather_call(): pl.pallas_call(functools.partial(gather_kernel, shards, lents, len(swaps)...  69.7 us

profile of v4, /device:TPU:8, one launch (start us, length us, event | category | flops | bytes accessed | tf_op | source)
XLA Modules:
  0.0 523.3 jit_solution(16289070845252662335)
XLA Ops:
  0.7 0.8 concatenate.9.rows_ref.refs_2_.refs_1_
  1.4 0.8 copy.50
  2.3 5.3 %shard_map.264 = (bf16[1024,1024]{1,0:T(8,128)(2,1)}, bf16[1024,1024]{1,0:T(8,128)(2,1)}) custom-call(s32[8,512]{1,0:T(8,128)} %copy-done.4, bf16[512,1024]{1,0:T(8,128)(2,1)} %tokens_ref.1, bf16[512,1024]{1,0:T(8,128)(2,1)} %cotangent_ref.1), custom_call_target="tpu_custom_call" | custom-call | tf_op jit(solution)/shard_map/pallas_call | solution.py:712
  7.5 1.3 fusion.7.refs_4_
  8.8 69.7 %shard_map.265 = (bf16[1024,1024]{1,0:T(8,128)(2,1)}, bf16[1024,1024]{1,0:T(8,128)(2,1)}, bf16[1024,1024]{1,0:T(8,128)(2,1)}, bf16[1024,1024]{1,0:T(8,128)(2,1)}, f32[128,128]{1,0:T(8,128)}) custom-call(bf16[64,1024]{1,0:T(8,128)(2,1)} %refs_0_.1, bf16[64,1024]{1,0:T(8,128)(2,1)} %refs_1_.1, bf16[64,1024]{1,0:T(8,128)(2,1)} %refs_2_.2, ...), custom_call_target="tpu_custom_call" | custom-call | tf_op jit(solution)/shard_map/pallas_call | solution.py:368
  78.5 0.9 fusion.10
  79.4 0.7 reshape_squeeze.9.refs_5_
  80.5 1.0 fusion
  81.5 1.3 pad_maximum_fusion
  82.8 0.7 reshape_squeeze.10.refs_11_.refs_4_
  83.4 159.0 %shard_map.266 = (bf16[512,1024]{1,0:T(8,128)(2,1)}, bf16[512,1024]{1,0:T(8,128)(2,1)}, bf16[512,3072]{1,0:T(8,128)(2,1)}, bf16[512,1024]{1,0:T(8,128)(2,1)}, f3...) custom-call(bf16[1024,1024]{1,0:T(8,128)(2,1)} %get-tuple-element.51, ...), custom_call_target="tpu_custom_call" | custom-call | tf_op jit(solution)/shard_map/pallas_call | solution.py:1019
  242.5 103.4 %shard_map.267 = (bf16[512,1024]{1,0:T(8,128)(2,1)}, bf16[512,4096]{1,0:T(8,128)(2,1)}, bf16[1024,1024]{1,0:T(8,128)(2,1)}, f32[24,128]{1,0:T(8,128)}, f32[256,1...) custom-call(s32[512,8]{1,0:T(8,128)} %bitcast.28, ...), custom_call_target="tpu_custom_call" | custom-call | tf_op jit(solution)/shard_map/pallas_call | solution.py:1288
  345.9 162.9 %shard_map.268 = (f32[64,4096]{1,0:T(8,128)}, f32[64,4096]{1,0:T(8,128)}, f32[64,4096]{1,0:T(8,128)}, bf16[512,1024]{1,0:T(8,128)(2,1)}, bf16[512,1024]{1,0:T(8,...) custom-call(s32[512,8]{1,0:T(8,128)} %bitcast.29, ...), custom_call_target="tpu_custom_call" | custom-call | tf_op jit(solution)/shard_map/pallas_call | solution.py:1473
  508.9 0.8 slice_bitcast_fusion
  510.3 2.3 fusion.9
  512.5 0.7 slice_reduce_fusion.1
  513.2 0.6 reshape_squeeze.11
  514.5 0.8 slice_reduce_fusion
  515.3 0.6 slice.47
  517.0 2.4 copy.61
  519.4 1.0 copy.62
  520.4 1.0 copy.63
  521.3 1.0 copy.64
  522.3 1.0 copy.65
  (22 shorter events, 2.1 us)
Async XLA Ops:
  0.6 79.5 %copy-start.5 = (s32[1,4]{1,0:T(1,128)S(1)}, s32[1,4]{1,0:T(1,128)}, u32[]{:S(2)}) copy-start(s32[1,4]{1,0:T(1,128)} %refs_2_.3) | copy-start | bytes 52
  1.4 0.9 copy-start.4
  508.8 10.5 %copy-start.3 = (bf16[512,1024]{1,0:T(8,128)(2,1)S(1)}, bf16[512,1024]{1,0:T(8,128)(2,1)}, u32[]{:S(2)}) copy-start(bf16[512,1024]{1,0:T(8,128)(2,1)} %get-tuple-element.114) | copy-start | bytes 3145732
  508.9 11.5 %copy-start.2 = (f32[64,4096]{1,0:T(8,128)S(1)}, f32[64,4096]{1,0:T(8,128)}, u32[]{:S(2)}) copy-start(f32[64,4096]{1,0:T(8,128)} %get-tuple-element.122) | copy-start | bytes 3145732
  510.3 11.0 %copy-start.1 = (f32[64,4096]{1,0:T(8,128)S(1)}, f32[64,4096]{1,0:T(8,128)}, u32[]{:S(2)}) copy-start(f32[64,4096]{1,0:T(8,128)} %get-tuple-element.123) | copy-start | bytes 3145732
  517.0 5.3 %copy-start = (f32[256,1024]{1,0:T(8,128)S(1)}, f32[256,1024]{1,0:T(8,128)}, u32[]{:S(2)}) copy-start(f32[256,1024]{1,0:T(8,128)} %get-tuple-element.124) | copy-start | bytes 3145732
